TPU v7x, 128 devices: a whole 4x4x4 slice. The times are simulated.
128 devices in a mesh: px: 8 (over z, core), py: 16 (over y, x).
Axes of the slice: x: 4, y: 4, z: 4, core: 2. Of those that a mesh axis runs over, the one named last changes fastest.
Arguments:
- features: bfloat16 [98304, 768], P(('px', 'py')), may hold values from -6 to 6
- weight_one: bfloat16 [768, 768], replicated, may hold values from -0.21875 to 0.21875
- weight_two: bfloat16 [768, 768], replicated, may hold values from -0.21875 to 0.21875
- tile_values: bfloat16 [4096, 128, 128], P(('px', 'py')), may hold values from -0.375 to 0.375
- tile_rows: int32 [128, 32], P(('px', 'py')), may hold values from 0 to 5
- tile_cols: int32 [128, 32], P(('px', 'py')), may hold values from 0 to 13
- tile_count: int32 [128], P(('px', 'py')), may hold values from 4 to 32, as said below
- send_rows: int32 [128, 128, 8], P(('px', 'py')), may hold values from 0 to 767
- send_count: int32 [128, 128], P(('px', 'py')), may hold values from 1 to 8, as said below
- stale_hidden: bfloat16 [131072, 768], P(('px', 'py')), may hold values from -3 to 3
- stale_grad: bfloat16 [131072, 768], P(('px', 'py')), may hold values from -6 to 6
- out_grad: bfloat16 [98304, 768], P(('px', 'py')), may hold values from -6 to 6
Outputs:
- next_hidden: bfloat16 [131072, 768], P(('px', 'py'))
- next_grad: bfloat16 [131072, 768], P(('px', 'py'))
- grad_one: float32 [768, 768], replicated
- grad_two: float32 [768, 768], replicated
Inputs may be any that keep to these rules, and one draw needn't show every extreme that they name: The tiles of a part with index below its tile_count are live, the others are ignored; some part has 32 live tiles in every draw. `tile_cols`: column tiles below 6 hold the part's own rows; the rest hold the received boundary rows, 8 slots from each part in order of the part. `send_rows`: slots at or beyond the matching send_count are unused. `send_count`: every part sends 8 rows to at least one peer in every draw.
All inputs are finite; a program needn't handle non-finite values.
Results may differ from a plain program's by a relative error of at most 0.0061.
Values may be sent and summed in bfloat16 or wider, within the bound.
No kernel may reach another device: no remote copies, remote signals or barrier semaphores. Data moves between devices by JAX's collectives and lax.ppermute only.
A program may use at most 128 MiB of HBM per device.

v0:
```python
import math

import jax
import jax.numpy as jnp
from jax import lax
from jax.sharding import PartitionSpec as P


def in_blocks(value, dim, peers):
    shape = value.shape
    pieces = value.reshape(*shape[:dim], peers, shape[dim] // peers, *shape[dim + 1 :])
    return jnp.moveaxis(pieces, dim, 0)


def edges_of(length, count):
    hop = length // count
    if hop >= 8:
        hop -= hop % 8
    return [hop * k for k in range(1, count)]


def joined_along(pieces, dim):
    pieces = jnp.moveaxis(pieces, 0, dim)
    shape = pieces.shape
    return pieces.reshape(*shape[:dim], shape[dim] * shape[dim + 1], *shape[dim + 2 :])


def exchange_in_pieces(value, axis, pieces, split_dim, concat_dim):
    blocks = in_blocks(value, split_dim, lax.axis_size(axis))
    widest = max(range(1, max(2, blocks.ndim - 1)), key=lambda d: blocks.shape[d])
    gathered = []
    for slab in jnp.split(blocks, edges_of(blocks.shape[widest], pieces), axis=widest):
        if slab.size:
            gathered.append(lax.all_to_all(slab, axis, split_axis=0, concat_axis=0, tiled=True))
    return joined_along(jnp.concatenate(gathered, axis=widest), concat_dim)


def exact_gelu(value):
    return jax.nn.gelu(value, approximate=False)


def forward_blocks(source, tile_values, tile_rows, tile_cols, live, row_tiles):
    tile, width = (source.shape[1], source.shape[2])
    group = math.gcd(16, tile_values.shape[0])
    rounds = (live + group - 1) // group
    targets = jnp.arange(row_tiles, dtype=jnp.int32)

    def forward_step(index, total):
        start = index * group
        values = lax.dynamic_slice_in_dim(tile_values, start, group, 0)
        rows = lax.dynamic_slice_in_dim(tile_rows, start, group, 0)
        cols = lax.dynamic_slice_in_dim(tile_cols, start, group, 0)
        active = start + jnp.arange(group, dtype=jnp.int32) < live
        values = jnp.where(active[:, None, None], values, jnp.zeros_like(values))
        blocks = source[cols]
        partial_value = jnp.einsum(
            "gij,gjd->gid", values, blocks, preferred_element_type=jnp.float32
        )
        place = (rows[:, None] == targets[None, :]).astype(jnp.float32)
        return total + jnp.einsum(
            "gr,gid->rid", place, partial_value, precision=lax.Precision.HIGHEST
        )

    empty = jnp.zeros((row_tiles, tile, width), jnp.float32)
    return lax.fori_loop(0, rounds, forward_step, empty)


def backward_blocks(grads, tile_values, tile_rows, tile_cols, live, col_tiles):
    tile, width = (grads.shape[1], grads.shape[2])
    group = math.gcd(16, tile_values.shape[0])
    rounds = (live + group - 1) // group
    targets = jnp.arange(col_tiles, dtype=jnp.int32)

    def backward_step(index, total):
        start = index * group
        values = lax.dynamic_slice_in_dim(tile_values, start, group, 0)
        rows = lax.dynamic_slice_in_dim(tile_rows, start, group, 0)
        cols = lax.dynamic_slice_in_dim(tile_cols, start, group, 0)
        active = start + jnp.arange(group, dtype=jnp.int32) < live
        values = jnp.where(active[:, None, None], values, jnp.zeros_like(values))
        blocks = grads[rows]
        partial_value = jnp.einsum(
            "gji,gjd->gid", values, blocks, preferred_element_type=jnp.float32
        )
        place = (cols[:, None] == targets[None, :]).astype(jnp.float32)
        return total + jnp.einsum(
            "gc,gid->cid", place, partial_value, precision=lax.Precision.HIGHEST
        )

    empty = jnp.zeros((col_tiles, tile, width), jnp.float32)
    return lax.fori_loop(0, rounds, backward_step, empty)


def local(
    features,
    weight_one,
    weight_two,
    tile_values,
    tile_rows,
    tile_cols,
    tile_count,
    send_rows,
    send_count,
    stale_hidden,
    stale_grad,
    out_grad,
):
    parts = lax.axis_size(("px", "py"))
    rows_own, width = features.shape
    slots = send_rows.shape[2]
    tile = tile_values.shape[1]
    row_tiles = rows_own // tile
    col_tiles = (rows_own + parts * slots) // tile
    live = tile_count[0]
    tile_row_list = tile_rows[0]
    tile_col_list = tile_cols[0]
    chosen = send_rows[0]
    counts = send_count[0]
    slot_ids = jnp.arange(slots, dtype=jnp.int32)
    sent_mask = slot_ids[None, :] < counts[:, None]
    picked = features[chosen]
    outgoing = jnp.where(sent_mask[:, :, None], picked, jnp.zeros_like(picked))
    count_column = counts[:, None]
    arrived, heard = (
        lax.all_to_all(outgoing, ("px", "py"), split_axis=0, concat_axis=0, tiled=True),
        lax.all_to_all(count_column, ("px", "py"), split_axis=0, concat_axis=0, tiled=True),
    )
    heard_mask = slot_ids[None, :] < heard
    source_one = jnp.concatenate([features, arrived.reshape(-1, width)], axis=0).reshape(
        col_tiles, tile, width
    )
    agg_one = forward_blocks(source_one, tile_values, tile_row_list, tile_col_list, live, row_tiles)
    agg_one = agg_one.reshape(rows_own, width).astype(jnp.bfloat16)
    pre_one = jnp.dot(agg_one, weight_one, preferred_element_type=jnp.float32)
    hidden = exact_gelu(pre_one).astype(jnp.bfloat16)
    hidden_picked = hidden[chosen]
    hidden_out = jnp.where(sent_mask[:, :, None], hidden_picked, jnp.zeros_like(hidden_picked))
    next_hidden = exchange_in_pieces(hidden_out, ("px", "py"), 2, 0, 0)
    next_hidden = next_hidden.reshape(parts * slots, width)
    kept = jnp.where(heard_mask.reshape(-1, 1), stale_hidden, jnp.zeros_like(stale_hidden))
    source_two = jnp.concatenate([hidden, kept], axis=0).reshape(col_tiles, tile, width)
    agg_two = forward_blocks(source_two, tile_values, tile_row_list, tile_col_list, live, row_tiles)
    agg_two = agg_two.reshape(rows_own, width).astype(jnp.bfloat16)
    scale = 1.0 / math.sqrt(rows_own * parts)
    part_two = jnp.dot(agg_two.T, out_grad, preferred_element_type=jnp.float32)
    down = jnp.dot(out_grad, weight_two.T, preferred_element_type=jnp.float32).astype(jnp.bfloat16)
    back = backward_blocks(
        down.reshape(row_tiles, tile, width),
        tile_values,
        tile_row_list,
        tile_col_list,
        live,
        col_tiles,
    )
    back = back.reshape(-1, width)
    own_grad = back[:rows_own]
    remote = back[rows_own:].reshape(parts, slots, width)
    grad_out = jnp.where(heard_mask[:, :, None], remote, jnp.zeros_like(remote)).astype(
        jnp.bfloat16
    )
    next_grad = lax.all_to_all(grad_out, ("px", "py"), split_axis=0, concat_axis=0, tiled=True)
    next_grad = next_grad.reshape(parts * slots, width)
    old_back = stale_grad.astype(jnp.float32)
    old_back = jnp.where(sent_mask.reshape(-1, 1), old_back, jnp.zeros_like(old_back))
    hidden_grad = own_grad + jax.ops.segment_sum(
        old_back, chosen.reshape(-1), num_segments=rows_own
    )
    pull = jax.vjp(exact_gelu, pre_one)[1]
    pre_grad = pull(hidden_grad)[0].astype(jnp.bfloat16)
    part_one = jnp.dot(agg_one.T, pre_grad, preferred_element_type=jnp.float32)
    total_one, total_two = lax.psum((part_one, part_two), ("px", "py"))
    return (next_hidden, next_grad, total_one * scale, total_two * scale)


def solution(mesh):
    in_specs = (
        P(("px", "py"), None),
        P(),
        P(),
        P(("px", "py"), None, None),
        P(("px", "py"), None),
        P(("px", "py"), None),
        P(("px", "py")),
        P(("px", "py"), None, None),
        P(("px", "py"), None),
        P(("px", "py"), None),
        P(("px", "py"), None),
        P(("px", "py"), None),
    )
    out_specs = (P(("px", "py"), None), P(("px", "py"), None), P(), P())
    return jax.shard_map(local, mesh=mesh, in_specs=in_specs, out_specs=out_specs, check_vma=False)
```

profile of v0, /device:TPU:1, one launch (start us, length us, event | category | flops | bytes accessed | tf_op | source)
XLA Modules:
  0.0 380.1 jit_solution(3097699820664569553)
XLA Ops:
  7.2 1.5 copy.41
  8.7 11.5 %all-to-all-start.3 = ((s32[128,1,1]{2,1,0:T(1,128)}), s32[128,1,1]{2,1,0:T(1,128)S(1)}, u32[]{:S(2)}, u32[]{:S(2)}) async-start(s32[128,1,1]{2,1,0:T(1,128)} %copy.41), calls=%async_computation.3 | async-start | bytes 131072 | tf_op jit(solution)/shard_map/all_to_all | solution.py:126
  22.5 5.9 %gather_fusion.3 = bf16[1024,768]{1,0:T(8,128)(2,1)S(1)} fusion(bf16[768,768]{1,0:T(8,128)(2,1)} %param.18, s32[1024]{0:T(1024)S(1)} %broadcast_clamp_fusion), kind=kCustom, calls=%fused_computation.3 | custom fusion | bytes 3149824 | tf_op jit(solution)/shard_map/gather | solution.py:121
  28.4 1.4 bitcast_select_fusion.1
  30.6 1.1 convolution_convert_fusion
  31.8 10.2 %all-to-all-start = ((bf16[128,8,768]{2,1,0:T(8,128)(2,1)}), bf16[128,8,768]{2,1,0:T(8,128)(2,1)}, u32[]{:S(2)}, u32[]{:S(2)}) async-start(bf16[128,8,768]{2,1,0:T(8,128)(2,1)} %bitcast_select_fusion.1), calls=%async_computation | async-start | bytes 3145728 | tf_op jit(solution)/shard_map/all_to_all | solution.py:125
  42.0 3.4 broadcast_in_dim.95
  45.4 19.0 %while.34 = (s32[]{:T(128)}, f32[14,128,768]{2,0,1:T(8,128)}, s32[]{:T(128)}, s32[32]{0:T(128)S(1)}, s32[]{:T(128)}, /*index=5*/bf16[32,128,128]{2,1,0:T(8,128)(...) while((s32[]{:T(128)}, f32[14,128,768]{2,0,1:T(8,128)}, ...), condition=%wide.region_3.4_spmd.clone, body=%wide.region_2.3_spmd.clone.sunk | while | flops 668534080 | bytes 35656344 | solution.py:91
  45.5 2.5 gather_fusion.1
  48.8 2.0 copy.70
  51.5 3.1 fusion.105
  54.7 9.3 %fusion.106 = f32[14,128,768]{2,0,1:T(8,128)} fusion(f32[14,128,768]{2,0,1:T(8,128)} %get-tuple-element.480, f32[16,128,768]{2,1,0:T(8,128)S(1)} %fusion.105, s32[16]{0:T(128)S(1)} %dynamic_slice.62), kind=kOutput, calls=%fused_computation.27.clone.1 | convolution fusion | flops 265617632 | bytes 17301568 | tf_op jit(solution)/shard_map/while/body/gc,gid->cid/dot_general | solution.py:86
  64.7 2.1 slice.11
  66.8 7.3 %copy.43 = bf16[14,128,768]{2,1,0:T(8,128)(2,1)} copy(f32[14,128,768]{2,0,1:T(8,128)} %get-tuple-element.149) | data formatting | bytes 8257536 | tf_op jit(solution)/shard_map/while | solution.py:91
  74.0 2.1 copy.44
  76.2 11.3 %scatter_custom_fusion = f32[768,768]{1,0:T(8,128)} fusion(f32[768,768]{1,0:T(8,128)} %bitcast.61, s32[1024]{0:T(1024)S(1)} %reshape.220, bf16[1024,768]{1,0:T(8,128)(2,1)} %param.28, f32[]{:T(128)} %constant.76.clone.1, pred[1024]{0:T(1024)(128)(4,1)S(1)} %lt.135), kind=kCustom, calls=%fused_computation.57 | custom fusion | flops 2359296 | bytes 3933696 | tf_op jit(solution)/shard_map/scatter-add | solution.py:165
  87.5 2.3 reduce
  90.1 2.9 broadcast_select_fusion
  93.0 1.5 select_convert_fusion
  94.5 23.9 %all-to-all-start.4 = ((bf16[128,8,768]{2,1,0:T(8,128)(2,1)}), bf16[128,8,768]{2,1,0:T(8,128)(2,1)}, u32[]{:S(2)}, u32[]{:S(2)}) async-start(bf16[128,8,768]{2,1,0:T(8,128)(2,1)} %select_convert_fusion), calls=%async_computation.4 | async-start | bytes 3145728 | tf_op jit(solution)/shard_map/all_to_all | solution.py:161
  118.5 3.2 pad_maximum_fusion
  121.7 1.8 broadcast.227.clone
  123.5 15.4 %while.33 = (s32[]{:T(128)}, f32[6,128,768]{2,0,1:T(8,128)}, s32[]{:T(128)}, s32[32]{0:T(128)S(1)}, s32[]{:T(128)}, /*index=5*/bf16[32,128,128]{2,1,0:T(8,128)(2...) while((s32[]{:T(128)}, f32[6,128,768]{2,0,1:T(8,128)}, ...), condition=%wide.region_1.2_spmd.clone, body=%wide.region_0.1_spmd.clone.sunk | while | flops 516752576 | bytes 27268232 | solution.py:65
  123.8 4.2 %gather_fusion = bf16[16,128,768]{2,1,0:T(8,128)(2,1)} fusion(bf16[14,128,768]{2,1,0:T(8,128)(2,1)} %get-tuple-element.462, s32[1024]{0:T(1024)S(1)} %pad_clamp_fusion.6), kind=kCustom, calls=%fused_computation.clone.clone.1 | custom fusion | bytes 6291520 | tf_op jit(solution)/shard_map/while/body/gather | solution.py:55
  128.6 2.9 fusion.99
  131.6 7.3 %fusion.100 = f32[6,128,768]{2,0,1:T(8,128)} fusion(f32[6,128,768]{2,0,1:T(8,128)} %get-tuple-element.444, f32[16,128,768]{2,1,0:T(8,128)S(1)} %fusion.99, s32[16]{0:T(128)S(1)} %dynamic_slice.59), kind=kOutput, calls=%fused_computation.11.clone.1 | convolution fusion | flops 113836128 | bytes 11010112 | tf_op jit(solution)/shard_map/while/body/gr,gid->rid/dot_general | solution.py:60
  138.9 2.5 copy.63
  141.5 7.1 %multiply_convert_fusion = (bf16[768,768]{1,0:T(8,128)(2,1)S(1)}, f32[768,768]{1,0:T(8,128)}, f32[768,768]{1,0:T(8,128)}) fusion(bf16[768,768]{1,0:T(8,128)(2,1)S(1)} %bitcast.63, bf16[768,768]{1,0:T(8,128)(2,1)S(1)} %copy-done), kind=kOutput, calls=%fused_computation.67 | convolution fusion | flops 944308224 | bytes 8257536 | tf_op jit(solution)/shard_map/dot_general | solution.py:134
  148.6 1.7 pad_maximum_fusion.1
  150.3 1.8 broadcast.227
  152.2 15.5 %while.35 = (s32[]{:T(128)}, f32[6,128,768]{2,0,1:T(8,128)}, s32[]{:T(128)}, s32[32]{0:T(128)S(1)}, s32[]{:T(128)}, /*index=5*/bf16[32,128,128]{2,1,0:T(8,128)(2...) while((s32[]{:T(128)}, f32[6,128,768]{2,0,1:T(8,128)}, ...), condition=%wide.region_7.8_spmd.clone, body=%wide.region_6.7_spmd.clone.sunk | while | flops 516752576 | bytes 27268232 | solution.py:65
  152.3 4.2 %gather_fusion.2 = bf16[16,128,768]{2,1,0:T(8,128)(2,1)} fusion(bf16[14,128,768]{2,1,0:T(8,128)(2,1)} %get-tuple-element.534, s32[1024]{0:T(1024)S(1)} %pad_clamp_fusion.8), kind=kCustom, calls=%fused_computation.2.clone.clone.1 | custom fusion | bytes 6291520 | tf_op jit(solution)/shard_map/while/body/gather | solution.py:55
  157.1 2.9 fusion.111
  160.1 7.3 %fusion.112 = f32[6,128,768]{2,0,1:T(8,128)} fusion(f32[6,128,768]{2,0,1:T(8,128)} %get-tuple-element.516, f32[16,128,768]{2,1,0:T(8,128)S(1)} %fusion.111, s32[16]{0:T(128)S(1)} %dynamic_slice.65), kind=kOutput, calls=%fused_computation.42.clone.1 | convolution fusion | flops 113836128 | bytes 11010112 | tf_op jit(solution)/shard_map/while/body/gr,gid->rid/dot_general | solution.py:60
  167.7 2.7 copy.62
  170.4 2.6 fusion.66
  173.0 1.0 copy-done.9
  174.0 2.9 fusion.60
  177.6 5.2 %gather_fusion.4 = bf16[1024,768]{1,0:T(8,128)(2,1)} fusion(bf16[768,768]{1,0:T(8,128)(2,1)S(1)} %get-tuple-element.274, s32[1024]{0:T(1024)S(1)} %copy-done.8), kind=kCustom, calls=%fused_computation.4 | custom fusion | bytes 3149824 | tf_op jit(solution)/shard_map/gather | solution.py:136
  182.8 1.6 bitcast_select_fusion
  184.4 1.4 fusion.65
  185.8 53.0 %all_to_all.29 = bf16[128,1,4,768]{3,2,1,0:T(4,128)(2,1)S(1)} all-to-all(bf16[128,1,4,768]{3,2,1,0:T(4,128)(2,1)S(1)} %get-tuple-element.276), channel_id=1, replica_groups=mesh['px'=8,'py'=16] {'px','py'}, dimensions={0} | all-to-all | bytes 1572864 | tf_op jit(solution)/shard_map/all_to_all | solution.py:34
  238.8 4.7 %all-to-all-start.2 = ((bf16[128,1,4,768]{3,2,1,0:T(4,128)(2,1)}), bf16[128,1,4,768]{3,2,1,0:T(4,128)(2,1)S(1)}, u32[]{:S(2)}, u32[]{:S(2)}) async-start(bf16[128,1,4,768]{3,2,1,0:T(4,128)(2,1)} %get-tuple-element.277), calls=%async_computation.2 | async-start | bytes 1572864 | tf_op jit(solution)/shard_map/all_to_all | solution.py:34
  243.5 16.4 %all-to-all-done.2 = bf16[128,1,4,768]{3,2,1,0:T(4,128)(2,1)S(1)} async-done(((bf16[128,1,4,768]{3,2,1,0:T(4,128)(2,1)}), bf16[128,1,4,768]{3,2,1,0:T(4,128)(2,1)S(1)}, u32[]{:S(2)}, u32[]{:S(2)}) %all-to-all-start.2) | async-done | bytes 786464 | tf_op jit(solution)/shard_map/all_to_all | solution.py:34
  260.0 1.9 maximum_bitcast_fusion
  261.9 103.6 %all-reduce.3.cloned.1.call-done = (f32[768,768]{1,0:T(8,128)}, f32[768,768]{1,0:T(8,128)}) async-done(((f32[768,768]{1,0:T(8,128)}, f32[768,768]{1,0:T(8,128)}), (f32[768,768]{1,0:T(8,128)}, f32[768,768]{1,0:T(8,128)})) %all-reduce.3.cloned.1.call-update) | async-done | bytes 4718608 | tf_op jit(solution)/shard_map/psum | solution.py:171
  365.4 5.0 %broadcast_multiply_fusion = (f32[768,768]{1,0:T(8,128)}, f32[768,768]{1,0:T(8,128)}) fusion(f32[768,768]{1,0:T(8,128)} %get-tuple-element.273, f32[768,768]{1,0:T(8,128)} %get-tuple-element.272), kind=kLoop, calls=%fused_computation.88 | loop fusion | flops 1179648 | bytes 9437184 | tf_op jit(solution)/shard_map/mul | solution.py:172
  370.4 2.7 copy.96
  (63 shorter events, 7.0 us)
Async XLA Ops:
  7.2 134.3 %copy-start = (bf16[768,768]{1,0:T(8,128)(2,1)S(1)}, bf16[768,768]{1,0:T(8,128)(2,1)}, u32[]{:S(2)}) copy-start(bf16[768,768]{1,0:T(8,128)(2,1)} %param.19) | copy-start | bytes 3538948
  8.7 23.1 %all-to-all-start.3 = ((s32[128,1,1]{2,1,0:T(1,128)}), s32[128,1,1]{2,1,0:T(1,128)S(1)}, u32[]{:S(2)}, u32[]{:S(2)}) async-start(s32[128,1,1]{2,1,0:T(1,128)} %copy.41), calls=%async_computation.3 | async-start | bytes 131072 | tf_op jit(solution)/shard_map/all_to_all | solution.py:126
  22.5 5.9 %copy-start.7 = (s32[1024]{0:T(1024)}, s32[1024]{0:T(1024)S(1)}, u32[]{:S(2)}) copy-start(s32[1024]{0:T(1024)S(1)} %broadcast_clamp_fusion) | copy-start | bytes 12292
  28.4 1.5 copy-start.12
  28.4 2.2 copy-start.13
  31.8 62.7 %all-to-all-start = ((bf16[128,8,768]{2,1,0:T(8,128)(2,1)}), bf16[128,8,768]{2,1,0:T(8,128)(2,1)}, u32[]{:S(2)}, u32[]{:S(2)}) async-start(bf16[128,8,768]{2,1,0:T(8,128)(2,1)} %bitcast_select_fusion.1), calls=%async_computation | async-start | bytes 3145728 | tf_op jit(solution)/shard_map/all_to_all | solution.py:125
  41.9 3.5 copy-start.2
  42.0 3.5 copy-start.15
  42.0 3.5 copy-start.16
  45.4 19.1 %copy-start.11 = (s32[1,128,8]{1,2,0:T(8,128)S(1)}, s32[1,128,8]{1,2,0:T(8,128)}, u32[]{:S(2)}) copy-start(s32[1,128,8]{1,2,0:T(8,128)} %param.25) | copy-start | bytes 12292
  90.1 2.9 slice-start
  94.5 24.0 %copy-start.1 = (bf16[768,768]{1,0:T(8,128)(2,1)S(1)}, bf16[768,768]{1,0:T(8,128)(2,1)}, u32[]{:S(2)}) copy-start(bf16[768,768]{1,0:T(8,128)(2,1)} %param.18) | copy-start | bytes 3538948
  94.5 91.3 %all-to-all-start.4 = ((bf16[128,8,768]{2,1,0:T(8,128)(2,1)}), bf16[128,8,768]{2,1,0:T(8,128)(2,1)}, u32[]{:S(2)}, u32[]{:S(2)}) async-start(bf16[128,8,768]{2,1,0:T(8,128)(2,1)} %select_convert_fusion), calls=%async_computation.4 | async-start | bytes 3145728 | tf_op jit(solution)/shard_map/all_to_all | solution.py:161
  118.4 247.0 %all-reduce.3.cloned.1.call-start = ((), (), s32[]{:S(2)}) async-start(), calls=%async_computation.5 | async-start | bytes 9437184 | tf_op jit(solution)/shard_map/psum | solution.py:171
  141.5 7.1 %copy-start.5 = (bf16[6,128,768]{2,1,0:T(8,128)(2,1)}, bf16[6,128,768]{2,1,0:T(8,128)(2,1)S(1)}, u32[]{:S(2)}) copy-start(bf16[6,128,768]{2,1,0:T(8,128)(2,1)S(1)} %copy.63) | copy-start | bytes 3538948
  141.5 7.1 %copy-start.4 = (bf16[1024,768]{1,0:T(8,128)(2,1)S(1)}, bf16[1024,768]{1,0:T(8,128)(2,1)}, u32[]{:S(2)}) copy-start(bf16[1024,768]{1,0:T(8,128)(2,1)} %broadcast_select_fusion) | copy-start | bytes 4718596
  167.6 2.7 copy-start.14
  167.7 5.3 %copy-start.10 = (f32[768,768]{1,0:T(8,128)S(1)}, f32[768,768]{1,0:T(8,128)}, u32[]{:S(2)}) copy-start(f32[768,768]{1,0:T(8,128)} %get-tuple-element.278) | copy-start | bytes 7077892
  170.4 2.6 copy-start.3
  170.4 2.6 copy-start.6
  170.4 3.6 copy-start.9
  176.9 0.7 copy-start.8
  238.8 21.2 %all-to-all-start.2 = ((bf16[128,1,4,768]{3,2,1,0:T(4,128)(2,1)}), bf16[128,1,4,768]{3,2,1,0:T(4,128)(2,1)S(1)}, u32[]{:S(2)}, u32[]{:S(2)}) async-start(bf16[128,1,4,768]{3,2,1,0:T(4,128)(2,1)} %get-tuple-element.277), calls=%async_computation.2 | async-start | bytes 1572864 | tf_op jit(solution)/shard_map/all_to_all | solution.py:34
Sparse Core Ops, SparseCore 0:
  177.0 188.3 all-reduce.2
where the time goes:
time: 387 us; the launch traced here: 380 us
  waiting for transfers between devices  120 us (31%)
  local copies, waits for them, and re-layouts  57.6 us (15%)
  blocking collectives  53 us (14%)
  starting transfers between devices  50.4 us (13%)
  matrix products  46.5 us (12%)
  other arithmetic  36.5 us (9%)
  between operations  15.2 us (4%)
    psum x1, waiting for transfers between devices, local(): total_one, total_two = lax.psum((part_one, part_two), ('px', 'py'))  104 us
    all_to_all x1, blocking collectives, exchange_in_pieces(): lax.all_to_all(slab, axis, split_axis=0, concat_axis=0, tiled=True)  53 us
    all_to_all x1, starting transfers between devices, local(): lax.all_to_all(grad_out, ('px', 'py'), split_axis=0, concat_axis=0, tiled...  23.9 us
    all_to_all x1, waiting for transfers between devices, exchange_in_pieces(): lax.all_to_all(slab, axis, split_axis=0, concat_axis=0, tiled=True)  16.4 us
    dot_general x2, matrix products, forward_step(): jnp.einsum('gr,gid->rid', place, partial_value, precision=lax.Precision.H...  14.7 us
    all_to_all x1, starting transfers between devices, local(): lax.all_to_all(count_column, ('px', 'py'), split_axis=0, concat_axis=0, t...  11.5 us
    scatter-add x1, other arithmetic, local(): jax.ops.segment_sum(old_back, chosen.reshape(-1), num_segments=rows_own)  11.3 us
    all_to_all x1, starting transfers between devices, local(): lax.all_to_all(outgoing, ('px', 'py'), split_axis=0, concat_axis=0, tiled...  10.2 us
  transfers between devices with their start and end apart: 5, of which 2 were waited for; matrix products, arithmetic and copies ran while one was open for 34% of the time, Pallas kernels for 0%

commit v1 on v0

v1 whole, which is shorter than its diff:
```python
import functools
import math

import jax
import jax.numpy as jnp
from jax import lax
from jax.experimental import pallas as pl
from jax.experimental.pallas import tpu as pltpu
from jax.sharding import PartitionSpec as P

BOTH = ("px", "py")
LANES = 128
VMEM = pl.BlockSpec(memory_space=pltpu.VMEM)
SMEM = pl.BlockSpec(memory_space=pltpu.SMEM)
INV_SQRT2 = 1.0 / math.sqrt(2.0)
INV_SQRT_2PI = 1.0 / math.sqrt(2.0 * math.pi)


def mm(a, b, dims=((1,), (0,))):
    return lax.dot_general(a, b, (dims, ((), ())), preferred_element_type=jnp.float32)


def fill_picks(idx_ref, pick_ref):
    rows = pick_ref.shape[1]
    lane = lax.broadcasted_iota(jnp.int32, (LANES, rows), 1)
    for j in range(idx_ref.shape[0]):
        across = jnp.broadcast_to(idx_ref[j : j + 1, :], (LANES, LANES))
        down = across.T
        wide = jnp.concatenate([down] * (rows // LANES), axis=1)
        hit = jnp.where(wide == lane, 1.0, 0.0)
        pick_ref[j * LANES : (j + 1) * LANES, :] = hit.astype(pick_ref.dtype)


def pack_kernel(idx_ref, features_ref, out_ref, pick_ref):
    width = features_ref.shape[1]
    fill_picks(idx_ref, pick_ref)
    out_ref[:, :width] = mm(pick_ref[...], features_ref[...]).astype(out_ref.dtype)
    for j in range(idx_ref.shape[0]):
        across = jnp.broadcast_to(idx_ref[j : j + 1, :], (LANES, LANES))
        used = jnp.where(across.T >= 0, 1.0, 0.0)
        out_ref[j * LANES : (j + 1) * LANES, width:] = used.astype(out_ref.dtype)


def local_kernel(
    rows_ref,
    cols_ref,
    count_ref,
    idx_ref,
    tiles_ref,
    features_ref,
    out_grad_ref,
    weight_ref,
    stale_grad_ref,
    adj_ref,
    agg_ref,
    hidden_grad_ref,
    grad_out_ref,
    adj32,
    scatter,
):
    tile = tiles_ref.shape[1]
    own = features_ref.shape[0]
    adj32[...] = jnp.zeros_like(adj32)

    @pl.loop(0, count_ref[0])
    def _(t):
        r = pl.multiple_of(rows_ref[t] * tile, tile)
        c = pl.multiple_of(cols_ref[t] * tile, tile)
        adj32[pl.ds(r, tile), pl.ds(c, tile)] += tiles_ref[t].astype(jnp.float32)

    adj_ref[...] = adj32[...].astype(adj_ref.dtype)
    down = mm(out_grad_ref[...], weight_ref[...], ((1,), (1,))).astype(jnp.bfloat16)
    grad_out_ref[...] = mm(adj_ref[:, own:], down, ((0,), (0,))).astype(grad_out_ref.dtype)
    place = lax.broadcasted_iota(jnp.int32, (own, LANES), 0)
    for j in range(idx_ref.shape[0]):
        across = jnp.broadcast_to(idx_ref[j : j + 1, :], (own, LANES))
        hit = jnp.where(across == place, 1.0, 0.0)
        scatter[:, j * LANES : (j + 1) * LANES] = hit.astype(scatter.dtype)
    hidden_grad_ref[...] = mm(adj_ref[:, :own], down, ((0,), (0,))) + mm(
        scatter[...], stale_grad_ref[...]
    )
    agg_ref[...] = mm(adj_ref[:, :own], features_ref[...])


def main_kernel(
    core_ref,
    idx_ref,
    arrived_ref,
    adj_ref,
    agg_ref,
    weight_ref,
    hidden_grad_ref,
    stale_hidden_ref,
    out_grad_ref,
    hidden_out_ref,
    keep_ref,
    send_ref,
    pick_ref,
    kept_ref,
):
    own, width = agg_ref.shape
    agg_one = (agg_ref[...] + mm(adj_ref[:, own:], arrived_ref[:, :width])).astype(jnp.bfloat16)
    pre = mm(agg_one, weight_ref[...])
    cdf = 0.5 * (1.0 + lax.erf(pre * INV_SQRT2))
    hidden = (pre * cdf).astype(jnp.bfloat16)
    slope = cdf + pre * (jnp.exp(-0.5 * pre * pre) * INV_SQRT_2PI)
    pre_grad = (hidden_grad_ref[...] * slope).astype(jnp.bfloat16)
    fill_picks(idx_ref, pick_ref)
    hidden_out_ref[...] = mm(pick_ref[...], hidden).astype(hidden_out_ref.dtype)
    part_one = mm(agg_one, pre_grad, ((0,), (0,)))
    for k in range(width // LANES):
        at = slice(k * LANES, (k + 1) * LANES)
        heard = arrived_ref[:, width:].astype(jnp.float32) > 0.5
        stale = stale_hidden_ref[:, at].astype(jnp.float32)
        kept_ref[:, at] = jnp.where(heard, stale, 0.0).astype(kept_ref.dtype)
    agg_two = (mm(adj_ref[:, :own], hidden) + mm(adj_ref[:, own:], kept_ref[...])).astype(jnp.bfloat16)
    part_two = mm(agg_two, out_grad_ref[...], ((0,), (0,)))
    first = core_ref[0] == 0
    for k in range(width // LANES):
        at = slice(k * LANES, (k + 1) * LANES)
        one, two = part_one[:, at], part_two[:, at]
        keep_ref[k] = jnp.where(first, one, two)
        send_ref[k] = jnp.where(first, two, one).astype(send_ref.dtype)


def call(kernel, out_shape, scalars, scratch):
    def run(*args):
        return pl.pallas_call(
            kernel,
            out_shape=out_shape,
            in_specs=[SMEM] * scalars + [VMEM] * (len(args) - scalars),
            out_specs=jax.tree.map(lambda _: VMEM, out_shape),
            scratch_shapes=scratch,
            compiler_params=pltpu.CompilerParams(vmem_limit_bytes=48 * 1024 * 1024),
        )(*args)

    return run


def trade(value, axis, groups=None):
    return lax.all_to_all(
        value, axis, split_axis=0, concat_axis=0, tiled=True, axis_index_groups=groups
    )


def spread(value, count):
    return jnp.broadcast_to(value[None], (count, *value.shape))


def local(
    features,
    weight_one,
    weight_two,
    tile_values,
    tile_rows,
    tile_cols,
    tile_count,
    send_rows,
    send_count,
    stale_hidden,
    stale_grad,
    out_grad,
):
    bf16, f32 = jnp.bfloat16, jnp.float32
    parts = lax.axis_size(BOTH)
    n_px, n_py = lax.axis_size("px"), lax.axis_size("py")
    n_z = n_px // 2
    own, width = features.shape
    slots = send_rows.shape[2]
    boundary = parts * slots
    cols = own + boundary
    shape = jax.ShapeDtypeStruct
    slot_ids = jnp.arange(slots, dtype=jnp.int32)
    sent = slot_ids[None, :] < send_count[0][:, None]
    idx = jnp.where(sent, send_rows[0], -1).reshape(boundary // LANES, LANES)

    outgoing = call(
        pack_kernel,
        shape((boundary, width + LANES), bf16),
        0,
        [pltpu.VMEM((boundary, own), bf16)],
    )(idx, features)
    arrived = trade(outgoing.reshape(parts, slots, -1), BOTH).reshape(boundary, -1)

    adj, agg, hidden_grad, grad_out = call(
        local_kernel,
        (
            shape((own, cols), bf16),
            shape((own, width), f32),
            shape((own, width), f32),
            shape((boundary, width), bf16),
        ),
        3,
        [pltpu.VMEM((own, cols), f32), pltpu.VMEM((own, boundary), bf16)],
    )(tile_rows[0], tile_cols[0], tile_count, idx, tile_values, features, out_grad, weight_two, stale_grad)
    grads = trade(grad_out.reshape(parts, slots, width), BOTH)
    next_grad = jnp.where(sent[:, :, None], grads, jnp.zeros_like(grads)).reshape(boundary, width)

    core = (lax.axis_index("px") % 2).astype(jnp.int32).reshape(1)
    blocks = width // LANES
    hidden_out, keep, send = call(
        main_kernel,
        (
            shape((boundary, width), bf16),
            shape((blocks, width, LANES), f32),
            shape((blocks, width, LANES), bf16),
        ),
        1,
        [pltpu.VMEM((boundary, own), bf16), pltpu.VMEM((boundary, width), bf16)],
    )(core, idx, arrived, adj, agg, weight_one, hidden_grad, stale_hidden, out_grad)

    swap = [(i, i ^ 1) for i in range(n_px)]
    z_groups = [[i for i in range(n_px) if i % 2 == c] for c in range(2)]
    lines = blocks * width
    other = lax.ppermute(send, "px", swap)
    mine = (keep + other.astype(f32)).astype(bf16).reshape(n_py, lines // n_py, LANES)
    mine = trade(mine, "py").astype(f32).sum(0).astype(bf16)
    mine = trade(mine.reshape(n_z, lines // (n_py * n_z), LANES), "px", z_groups)
    mine = mine.astype(f32).sum(0).astype(bf16)
    mine = trade(spread(mine, n_z), "px", z_groups).reshape(lines // n_py, LANES)
    mine = trade(spread(mine, n_py), "py").reshape(blocks, width, LANES)
    other = lax.ppermute(mine, "px", swap)

    next_hidden = trade(hidden_out.reshape(parts, slots, width), BOTH).reshape(boundary, width)
    scale = 1.0 / math.sqrt(own * parts)
    one = jnp.where(core[0] == 0, mine, other).astype(f32) * scale
    two = jnp.where(core[0] == 0, other, mine).astype(f32) * scale
    one = jnp.moveaxis(one, 0, 1).reshape(width, width)
    two = jnp.moveaxis(two, 0, 1).reshape(width, width)
    return next_hidden, next_grad, one, two


def solution(mesh):
    in_specs = (
        P(BOTH, None),
        P(),
        P(),
        P(BOTH, None, None),
        P(BOTH, None),
        P(BOTH, None),
        P(BOTH),
        P(BOTH, None, None),
        P(BOTH, None),
        P(BOTH, None),
        P(BOTH, None),
        P(BOTH, None),
    )
    out_specs = (P(BOTH, None), P(BOTH, None), P(), P())
    return jax.shard_map(local, mesh=mesh, in_specs=in_specs, out_specs=out_specs, check_vma=False)
```

time: 387 us -> 202 us (0.52); the launches traced: 380 us -> 201 us
  waiting for transfers between devices: 120 us -> 61.3 us
  matrix products: 46.5 us -> 0 us
  local copies, waits for them, and re-layouts: 57.6 us -> 19.2 us
  Pallas kernels: 0 us -> 28.2 us
  other arithmetic: 36.5 us -> 8.41 us
  starting transfers between devices: 50.4 us -> 27.6 us
  between operations: 15.2 us -> 1.43 us
    psum x1 -> x0, waiting for transfers between devices: 104 us -> none  [local(): total_one, total_two = lax.psum((part_one, part_two), ('px', 'py'))]
    dot_general x10 -> x0, matrix products: 46.5 us -> none  [the longest x2 14.7 us: forward_step(): jnp.einsum('gr,gid->rid', place, partial_value, precision=lax.Precision.H...]
    all_to_all x4 -> x3, waiting for transfers between devices: 16.5 us -> 58.8 us  [trade(): lax.all_to_all(value, axis, split_axis=0, concat_axis=0, tiled=True, axis...]
    pallas_call x0 -> x3, Pallas kernels: none -> 28.2 us  [run(): pl.pallas_call(kernel, out_shape=out_shape, in_specs=[SMEM] * scalars + [...]
    all_to_all x4 -> x3, starting transfers between devices: 50.3 us -> 25.2 us  [trade(): lax.all_to_all(value, axis, split_axis=0, concat_axis=0, tiled=True, axis...]
    gather x5 -> x0, local copies, waits for them, and re-layouts: 22 us -> none  [the longest x2 8.4 us: forward_step(): blocks = source[cols]]
    while x3 -> x0, local copies, waits for them, and re-layouts: 12.5 us -> none  [the longest x1 7.28 us: backward_blocks(): return lax.fori_loop(0, rounds, backward_step, empty)]
    scatter-add x1 -> x0, other arithmetic: 11.3 us -> none  [local(): jax.ops.segment_sum(old_back, chosen.reshape(-1), num_segments=rows_own)]
  transfers between devices with their start and end apart: 5 -> 5, of which waited for: 2 -> 4; matrix products, arithmetic and copies ran while one was open for 34% -> 1% of each run, Pallas kernels for 0% -> 5%
where the time goes in v1:
time: 202 us; the launch traced here: 201 us
  waiting for transfers between devices  61.3 us (30%)
  blocking collectives  54.8 us (27%)
  Pallas kernels  28.2 us (14%)
  starting transfers between devices  27.6 us (14%)
  local copies, waits for them, and re-layouts  19.2 us (10%)
  other arithmetic  8.41 us (4%)
    all_to_all x3, waiting for transfers between devices, trade(): lax.all_to_all(value, axis, split_axis=0, concat_axis=0, tiled=True, axis...  58.8 us
    all_to_all x4, blocking collectives, trade(): lax.all_to_all(value, axis, split_axis=0, concat_axis=0, tiled=True, axis...  54.8 us
    pallas_call x3, Pallas kernels, run(): pl.pallas_call(kernel, out_shape=out_shape, in_specs=[SMEM] * scalars + [...  28.2 us
    all_to_all x3, starting transfers between devices, trade(): lax.all_to_all(value, axis, split_axis=0, concat_axis=0, tiled=True, axis...  25.2 us
    unnamed x27, local copies, waits for them, and re-layouts  13.6 us
  transfers between devices with their start and end apart: 5, of which 4 were waited for; matrix products, arithmetic and copies ran while one was open for 1% of the time, Pallas kernels for 5%

profile of v1, /device:TPU:1, one launch (start us, length us, event | category | flops | bytes accessed | tf_op | source)
XLA Modules:
  0.0 201.0 jit_solution(12800770959964127428)
XLA Ops:
  0.6 0.5 broadcast.28
  1.1 1.3 reduce.5
  2.5 0.1 lt.44
  2.5 0.1 lt.45
  2.6 0.1 lt.46
  2.7 0.8 copy.22
  3.5 0.1 squeeze.9
  3.6 0.1 lt.42
  3.7 0.0 copy-start.1
  3.7 1.3 copy-done.1
  5.0 2.7 %shard_map.147 = bf16[1024,896]{1,0:T(8,128)(2,1)} custom-call(s32[8,128]{1,0:T(8,128)S(1)} %compare_select_fusion.idx_ref, bf16[768,768]{1,0:T(8,128)(2,1)S(1)} %copy-done.1), custom_call_target="tpu_custom_call" | custom-call | tf_op jit(solution)/shard_map/pallas_call | solution.py:128
  7.7 11.9 %all-to-all-start = ((bf16[128,8,896]{2,1,0:T(8,128)(2,1)}), bf16[128,8,896]{2,1,0:T(8,128)(2,1)}, u32[]{:S(2)}, u32[]{:S(2)}) async-start(bf16[128,8,896]{2,1,0:T(8,128)(2,1)} %bitcast.1), calls=%async_computation | async-start | bytes 3670016 | tf_op jit(solution)/shard_map/all_to_all | solution.py:141
  20.3 0.0 copy-done
  20.3 0.0 copy-done.2
  20.3 0.0 copy-done.6
  20.3 0.0 copy-done.7
  20.3 0.0 copy-start.4
  20.3 1.3 copy-done.4
  21.6 1.2 copy-done.5
  22.8 10.3 %shard_map.148 = (bf16[768,1792]{1,0:T(8,128)(2,1)}, f32[768,768]{1,0:T(8,128)}, f32[768,768]{1,0:T(8,128)}, bf16[1024,768]{1,0:T(8,128)(2,1)}) custom-call(s32[32]{0:T(128)S(1)} %bitcast.21, s32[32]{0:T(128)S(1)} %bitcast.22, s32[1]{0:T(128)S(6)} %copy.28.count_ref, s32[8,128]{1,0:T(8,128)S(1)} %compare_select_fusion.idx_ref, ...), custom_call_target="tpu_custom_call" | custom-call | tf_op jit(solution)/shard_map/pallas_call | solution.py:128
  33.1 13.1 %all-to-all-done = bf16[128,8,896]{2,1,0:T(8,128)(2,1)} async-done(((bf16[128,8,896]{2,1,0:T(8,128)(2,1)}), bf16[128,8,896]{2,1,0:T(8,128)(2,1)}, u32[]{:S(2)}, u32[]{:S(2)}) %all-to-all-start) | async-done | bytes 1835040 | tf_op jit(solution)/shard_map/all_to_all | solution.py:141
  46.2 0.0 copy-done.3
  46.2 15.3 %shard_map.149 = (bf16[1024,768]{1,0:T(8,128)(2,1)}, f32[6,768,128]{2,1,0:T(8,128)}, bf16[6,768,128]{2,1,0:T(8,128)(2,1)S(1)}) custom-call(s32[1]{0:T(128)} %bitcast.core_ref, s32[8,128]{1,0:T(8,128)S(1)} %compare_select_fusion.idx_ref, bf16[1024,896]{1,0:T(8,128)(2,1)} %bitcast.2.arrived_ref, bf16[768,1792]{1,0:T(8,128)(2,1)} %get-tuple-element.11.adj_ref, ...), custom_call_target="tpu_custom_call" | custom-call | tf_op jit(solution)/shard_map/pallas_call | solution.py:128
  61.5 1.2 collective-permute-start
  62.7 2.5 %collective-permute-done = bf16[6,768,128]{2,1,0:T(8,128)(2,1)S(1)} collective-permute-done((bf16[6,768,128]{2,1,0:T(8,128)(2,1)S(1)}, bf16[6,768,128]{2,1,0:T(8,128)(2,1)S(1)}, u32[]{:S(2)}, u32[]{:S(2)}) %collective-permute-start) | collective-permute-done | bytes 1179680 | tf_op jit(solution)/shard_map/ppermute | solution.py:215
  65.2 1.9 add_convert_fusion
  67.1 21.3 %all_to_all.35 = bf16[16,288,128]{2,1,0:T(8,128)(2,1)S(1)} all-to-all(bf16[16,288,128]{2,1,0:T(8,128)(2,1)S(1)} %bitcast.28), channel_id=1, replica_groups=mesh['px'=8,'py'=16] {'py'}, dimensions={0} | all-to-all | bytes 2359296 | tf_op jit(solution)/shard_map/all_to_all | solution.py:141
  88.5 0.2 reduce_sum.24
  88.7 6.9 %all_to_all.36 = bf16[4,72,128]{2,1,0:T(8,128)(2,1)S(1)} all-to-all(bf16[4,72,128]{2,1,0:T(8,128)(2,1)S(1)} %bitcast.29), channel_id=1, replica_groups={{0,32,64,96},{16,48,80,112},{1,33,65,97},{17,49,81,113},{2,34,66,98},{1..., dimensions={0} | all-to-all | bytes 147456 | tf_op jit(solution)/shard_map/all_to_all | solution.py:141
  95.5 6.1 %all-to-all-start.2 = ((bf16[128,8,768]{2,1,0:T(8,128)(2,1)}), bf16[128,8,768]{2,1,0:T(8,128)(2,1)S(1)}, u32[]{:S(2)}, u32[]{:S(2)}) async-start(bf16[128,8,768]{2,1,0:T(8,128)(2,1)} %bitcast.8), calls=%async_computation.2 | async-start | bytes 3145728 | tf_op jit(solution)/shard_map/all_to_all | solution.py:141
  101.6 24.2 %all-to-all-done.2 = bf16[128,8,768]{2,1,0:T(8,128)(2,1)S(1)} async-done(((bf16[128,8,768]{2,1,0:T(8,128)(2,1)}), bf16[128,8,768]{2,1,0:T(8,128)(2,1)S(1)}, u32[]{:S(2)}, u32[]{:S(2)}) %all-to-all-start.2) | async-done | bytes 1572896 | tf_op jit(solution)/shard_map/all_to_all | solution.py:141
  125.9 6.9 %all_to_all.37 = bf16[4,72,128]{2,1,0:T(8,128)(2,1)S(1)} all-to-all(bf16[4,72,128]{2,1,0:T(8,128)(2,1)S(1)} %broadcast_in_dim.33), channel_id=1, replica_groups={{0,32,64,96},{16,48,80,112},{1,33,65,97},{17,49,81,113},{2,34,66,98},{1..., dimensions={0} | all-to-all | bytes 147456 | tf_op jit(solution)/shard_map/all_to_all | solution.py:141
  132.7 0.2 broadcast_in_dim.35
  132.9 19.7 %all_to_all.38 = bf16[16,288,128]{2,1,0:T(8,128)(2,1)} all-to-all(bf16[16,288,128]{2,1,0:T(8,128)(2,1)S(1)} %broadcast_in_dim.35), channel_id=1, replica_groups=mesh['px'=8,'py'=16] {'py'}, dimensions={0} | all-to-all | bytes 2359296 | tf_op jit(solution)/shard_map/all_to_all | solution.py:141
  152.6 7.3 %all-to-all-start.1 = ((bf16[128,8,768]{2,1,0:T(8,128)(2,1)}), bf16[128,8,768]{2,1,0:T(8,128)(2,1)S(1)}, u32[]{:S(2)}, u32[]{:S(2)}) async-start(bf16[128,8,768]{2,1,0:T(8,128)(2,1)} %bitcast.5), calls=%async_computation.1 | async-start | bytes 3145728 | tf_op jit(solution)/shard_map/all_to_all | solution.py:141
  159.8 1.1 collective-permute-start.1
  161.0 0.0 copy-done.10
  161.0 0.1 iota_compare_fusion
  161.1 1.4 select_bitcast_fusion
  162.4 21.5 %all-to-all-done.1 = bf16[128,8,768]{2,1,0:T(8,128)(2,1)S(1)} async-done(((bf16[128,8,768]{2,1,0:T(8,128)(2,1)}), bf16[128,8,768]{2,1,0:T(8,128)(2,1)S(1)}, u32[]{:S(2)}, u32[]{:S(2)}) %all-to-all-start.1) | async-done | bytes 1572896 | tf_op jit(solution)/shard_map/all_to_all | solution.py:141
  183.9 1.1 copy-done.8
  185.1 0.0 collective-permute-done.1
  185.1 3.5 %multiply_bitcast_fusion = (f32[768,6,128]{2,0,1:T(8,128)S(1)}, f32[768,6,128]{2,0,1:T(8,128)}) fusion(bf16[6,768,128]{2,1,0:T(8,128)(2,1)} %collective-permute-done.1, bf16[6,768,128]{2,1,0:T(8,128)(2,1)} %bitcast.27, pred[]{:T(512)S(6)} %eq.6), kind=kLoop, calls=%fused_computation | loop fusion | flops 3538944 | bytes 7077889 | tf_op jit(solution)/shard_map/transpose | solution.py:229
  188.6 3.1 %copy.23 = f32[768,6,128]{0,2,1:T(8,128)} copy(f32[768,6,128]{2,0,1:T(8,128)} %get-tuple-element.27) | data formatting | bytes 4718592 | tf_op jit(solution)/shard_map/transpose | solution.py:228
  191.7 3.0 %copy.25 = f32[768,768]{1,0:T(8,128)} copy(f32[768,768]{0,1:T(8,128)} %bitcast.23) | data formatting | bytes 4718592
  194.7 2.0 copy.24
  196.7 3.2 %copy.26 = f32[768,768]{1,0:T(8,128)} copy(f32[768,768]{0,1:T(8,128)} %bitcast.24) | data formatting | bytes 4718592
  199.8 1.1 copy.29
  (14 shorter events, 0.1 us)
Async XLA Ops:
  3.7 1.3 copy-start.1
  7.7 12.6 %copy-start = (bf16[768,768]{1,0:T(8,128)(2,1)S(1)}, bf16[768,768]{1,0:T(8,128)(2,1)}, u32[]{:S(2)}) copy-start(bf16[768,768]{1,0:T(8,128)(2,1)} %out_grad_ref.3) | copy-start | bytes 3538948
  7.7 12.6 %copy-start.2 = (bf16[768,768]{1,0:T(8,128)(2,1)S(1)}, bf16[768,768]{1,0:T(8,128)(2,1)}, u32[]{:S(2)}) copy-start(bf16[768,768]{1,0:T(8,128)(2,1)} %features_ref.3) | copy-start | bytes 3538948
  7.7 12.6 %copy-start.6 = (s32[1,32]{1,0:T(1,128)S(1)}, s32[1,32]{1,0:T(1,128)}, u32[]{:S(2)}) copy-start(s32[1,32]{1,0:T(1,128)} %param.16) | copy-start | bytes 388
  7.7 12.6 %copy-start.7 = (s32[1,32]{1,0:T(1,128)S(1)}, s32[1,32]{1,0:T(1,128)}, u32[]{:S(2)}) copy-start(s32[1,32]{1,0:T(1,128)} %param.17) | copy-start | bytes 388
  7.7 38.5 %all-to-all-start = ((bf16[128,8,896]{2,1,0:T(8,128)(2,1)}), bf16[128,8,896]{2,1,0:T(8,128)(2,1)}, u32[]{:S(2)}, u32[]{:S(2)}) async-start(bf16[128,8,896]{2,1,0:T(8,128)(2,1)} %bitcast.1), calls=%async_computation | async-start | bytes 3670016 | tf_op jit(solution)/shard_map/all_to_all | solution.py:141
  20.3 1.3 copy-start.4
  21.6 1.2 copy-start.5
  22.8 23.4 %copy-start.3 = (bf16[768,768]{1,0:T(8,128)(2,1)S(1)}, bf16[768,768]{1,0:T(8,128)(2,1)}, u32[]{:S(2)}) copy-start(bf16[768,768]{1,0:T(8,128)(2,1)} %weight_ref.3) | copy-start | bytes 3538948
  61.5 3.7 %collective-permute-start = (bf16[6,768,128]{2,1,0:T(8,128)(2,1)S(1)}, bf16[6,768,128]{2,1,0:T(8,128)(2,1)S(1)}, u32[]{:S(2)}, u32[]{:S(2)}) collective-permute-start(bf16[6,768,128]{2,1,0:T(8,128)(2,1)S(1)} %get-tuple-element.17), channel_id=1, source_target_pairs={{0,16},{16,0},{32,48},{48,32},{64,80},{80,64},{96,112},{112,96},{1... | collective-permute-start | bytes 3538952 | tf_op jit(solution)/shard_map/ppermute | solution.py:215
  95.5 30.3 %all-to-all-start.2 = ((bf16[128,8,768]{2,1,0:T(8,128)(2,1)}), bf16[128,8,768]{2,1,0:T(8,128)(2,1)S(1)}, u32[]{:S(2)}, u32[]{:S(2)}) async-start(bf16[128,8,768]{2,1,0:T(8,128)(2,1)} %bitcast.8), calls=%async_computation.2 | async-start | bytes 3145728 | tf_op jit(solution)/shard_map/all_to_all | solution.py:141
  152.6 8.4 %copy-start.10 = (s32[1,128]{1,0:T(1,128)S(1)}, s32[1,128]{1,0:T(1,128)}, u32[]{:S(2)}) copy-start(s32[1,128]{1,0:T(1,128)} %param.20) | copy-start | bytes 1540
  152.6 31.4 %all-to-all-start.1 = ((bf16[128,8,768]{2,1,0:T(8,128)(2,1)}), bf16[128,8,768]{2,1,0:T(8,128)(2,1)S(1)}, u32[]{:S(2)}, u32[]{:S(2)}) async-start(bf16[128,8,768]{2,1,0:T(8,128)(2,1)} %bitcast.5), calls=%async_computation.1 | async-start | bytes 3145728 | tf_op jit(solution)/shard_map/all_to_all | solution.py:141
  159.8 25.2 %collective-permute-start.1 = (bf16[6,768,128]{2,1,0:T(8,128)(2,1)}, bf16[6,768,128]{2,1,0:T(8,128)(2,1)}, u32[]{:S(2)}, u32[]{:S(2)}) collective-permute-start(bf16[6,768,128]{2,1,0:T(8,128)(2,1)} %bitcast.26), channel_id=1, source_target_pairs={{0,16},{16,0},{32,48},{48,32},{64,80},{80,64},{96,112},{112,96},{1... | collective-permute-start | bytes 3538952 | tf_op jit(solution)/shard_map/ppermute | solution.py:222
  183.9 1.1 copy-start.8
  196.7 3.2 %copy-start.9 = (bf16[128,8,768]{2,1,0:T(8,128)(2,1)S(1)}, bf16[128,8,768]{2,1,0:T(8,128)(2,1)}, u32[]{:S(2)}) copy-start(bf16[128,8,768]{2,1,0:T(8,128)(2,1)} %copy-done.8) | copy-start | bytes 4718596

commit v2 on v1

v2 whole, which is shorter than its diff:
```python
import functools
import math

import jax
import jax.numpy as jnp
from jax import lax
from jax.experimental import pallas as pl
from jax.experimental.pallas import tpu as pltpu
from jax.sharding import PartitionSpec as P

BOTH = ("px", "py")
LANES = 128
PACK, LOCAL, MAIN = 58, 62, 56
VMEM = pl.BlockSpec(memory_space=pltpu.VMEM)
HBM = pl.BlockSpec(memory_space=pltpu.HBM)
SMEM = pl.BlockSpec(memory_space=pltpu.SMEM)
INV_SQRT2 = 1.0 / math.sqrt(2.0)
INV_SQRT_2PI = 1.0 / math.sqrt(2.0 * math.pi)


def mm(a, b, dims=((1,), (0,))):
    return lax.dot_general(a, b, (dims, ((), ())), preferred_element_type=jnp.float32)


def fill_picks(idx_ref, pick_ref):
    rows = pick_ref.shape[1]
    lane = lax.broadcasted_iota(jnp.int32, (LANES, rows), 1)
    for j in range(idx_ref.shape[0]):
        across = jnp.broadcast_to(idx_ref[j : j + 1, :], (LANES, LANES))
        down = across.T
        wide = jnp.concatenate([down] * (rows // LANES), axis=1)
        hit = jnp.where(wide == lane, 1.0, 0.0)
        pick_ref[j * LANES : (j + 1) * LANES, :] = hit.astype(pick_ref.dtype)


def copies(sems, pairs):
    started = [
        pltpu.make_async_copy(src, dst, sems.at[i]) for i, (src, dst) in enumerate(pairs)
    ]
    for copy in started:
        copy.start()
    return started


def pack_kernel(idx_ref, features_hbm, out_hbm, features, picks, out, sems):
    width = features.shape[1]
    (fetch,) = copies(sems, [(features_hbm, features)])
    fill_picks(idx_ref, picks)
    for j in range(idx_ref.shape[0]):
        across = jnp.broadcast_to(idx_ref[j : j + 1, :], (LANES, LANES))
        used = jnp.where(across.T >= 0, 1.0, 0.0)
        out[j * LANES : (j + 1) * LANES, width:] = used.astype(out.dtype)
    fetch.wait()
    step = out.shape[0] // 4
    stores = []
    for k in range(4):
        at = pl.ds(k * step, step)
        out[at, :width] = mm(picks[at, :], features[...]).astype(out.dtype)
        store = pltpu.make_async_copy(out.at[at, :], out_hbm.at[at, :], sems.at[1 + k])
        store.start()
        stores.append(store)
    for store in stores:
        store.wait()


def local_kernel(
    rows_ref,
    cols_ref,
    count_ref,
    idx_ref,
    tiles_hbm,
    features_hbm,
    out_grad_hbm,
    weight_hbm,
    stale_grad_hbm,
    near_hbm,
    far_hbm,
    agg_hbm,
    hidden_grad_hbm,
    box_hbm,
    tiles,
    features,
    out_grad,
    weight,
    stale_grad,
    near32,
    far32,
    near,
    far,
    scatter,
    agg,
    hidden_grad,
    grad_out,
    sems,
):
    tile = tiles.shape[1]
    own = features.shape[0]
    fetches = copies(
        sems,
        [
            (tiles_hbm, tiles),
            (out_grad_hbm, out_grad),
            (weight_hbm, weight),
            (features_hbm, features),
            (stale_grad_hbm, stale_grad),
        ],
    )
    near32[...] = jnp.zeros_like(near32)
    far32[...] = jnp.zeros_like(far32)
    fetches[0].wait()

    @pl.loop(0, count_ref[0])
    def _(t):
        r = pl.multiple_of(rows_ref[t] * tile, tile)
        c = pl.multiple_of(cols_ref[t] * tile, tile)
        value = tiles[t].astype(jnp.float32)

        @pl.when(c < own)
        def _():
            near32[pl.ds(r, tile), pl.ds(c, tile)] += value

        @pl.when(c >= own)
        def _():
            far32[pl.ds(r, tile), pl.ds(pl.multiple_of(c - own, tile), tile)] += value

    near[...] = near32[...].astype(near.dtype)
    far[...] = far32[...].astype(far.dtype)
    saves = copies(sems.at[pl.ds(5, 2)], [(near, near_hbm), (far, far_hbm)])
    fetches[3].wait()
    agg[...] = mm(near[...], features[...])
    saves += copies(sems.at[pl.ds(7, 1)], [(agg, agg_hbm)])
    fetches[1].wait()
    fetches[2].wait()
    down = mm(out_grad[...], weight[...], ((1,), (1,))).astype(jnp.bfloat16)
    remote = mm(far[...], down, ((0,), (0,)))
    grad_out[...] = remote.reshape(grad_out.shape).astype(grad_out.dtype)
    slots = grad_out.shape[1]
    saves += copies(sems.at[pl.ds(8, 1)], [(grad_out, box_hbm.at[:, slots:, :])])
    place = lax.broadcasted_iota(jnp.int32, (own, LANES), 0)
    for j in range(idx_ref.shape[0]):
        across = jnp.broadcast_to(idx_ref[j : j + 1, :], (own, LANES))
        hit = jnp.where(across == place, 1.0, 0.0)
        scatter[:, j * LANES : (j + 1) * LANES] = hit.astype(scatter.dtype)
    fetches[4].wait()
    hidden_grad[...] = mm(near[...], down, ((0,), (0,))) + mm(scatter[...], stale_grad[...])
    saves += copies(sems.at[pl.ds(9, 1)], [(hidden_grad, hidden_grad_hbm)])
    for save in saves:
        save.wait()


def main_kernel(
    core_ref,
    idx_ref,
    arrived_hbm,
    near_hbm,
    far_hbm,
    agg_hbm,
    weight_hbm,
    hidden_grad_hbm,
    stale_hidden_hbm,
    out_grad_hbm,
    _,
    box_hbm,
    keep_hbm,
    send_hbm,
    arrived,
    near,
    far,
    agg,
    weight,
    hidden_grad,
    stale_hidden,
    out_grad,
    picks,
    hidden_out,
    keep,
    send,
    sems,
):
    own, width = agg.shape
    fetches = copies(
        sems,
        [
            (arrived_hbm, arrived),
            (far_hbm, far),
            (agg_hbm, agg),
            (weight_hbm, weight),
            (hidden_grad_hbm, hidden_grad),
            (near_hbm, near),
            (stale_hidden_hbm, stale_hidden),
            (out_grad_hbm, out_grad),
        ],
    )
    fill_picks(idx_ref, picks)
    for fetch in fetches[:3]:
        fetch.wait()
    agg_one = (agg[...] + mm(far[...], arrived[:, :width])).astype(jnp.bfloat16)
    fetches[3].wait()
    pre = mm(agg_one, weight[...])
    cdf = 0.5 * (1.0 + lax.erf(pre * INV_SQRT2))
    hidden = (pre * cdf).astype(jnp.bfloat16)
    picked = mm(picks[...], hidden).reshape(hidden_out.shape)
    hidden_out[...] = picked.astype(hidden_out.dtype)
    slots = hidden_out.shape[1]
    saves = copies(sems.at[pl.ds(8, 1)], [(hidden_out, box_hbm.at[:, :slots, :])])
    fetches[6].wait()
    heard = arrived[:, width:].astype(jnp.float32) > 0.5
    for k in range(width // LANES):
        at = slice(k * LANES, (k + 1) * LANES)
        stale = stale_hidden[:, at].astype(jnp.float32)
        stale_hidden[:, at] = jnp.where(heard, stale, 0.0).astype(stale_hidden.dtype)
    fetches[5].wait()
    agg_two = (mm(near[...], hidden) + mm(far[...], stale_hidden[...])).astype(jnp.bfloat16)
    fetches[7].wait()
    part_two = mm(agg_two, out_grad[...], ((0,), (0,)))
    slope = cdf + pre * (jnp.exp(-0.5 * pre * pre) * INV_SQRT_2PI)
    fetches[4].wait()
    pre_grad = (hidden_grad[...] * slope).astype(jnp.bfloat16)
    part_one = mm(agg_one, pre_grad, ((0,), (0,)))
    first = core_ref[0] == 0
    for k in range(width // LANES):
        at = slice(k * LANES, (k + 1) * LANES)
        one, two = part_one[:, at], part_two[:, at]
        lines = pl.ds(k * width, width)
        keep[lines, :] = jnp.where(first, one, two)
        send[lines, :] = jnp.where(first, two, one).astype(send.dtype)
    saves += copies(sems.at[pl.ds(9, 2)], [(send, send_hbm), (keep, keep_hbm)])
    for save in saves:
        save.wait()


def chunk(ref, base, index, size):
    return ref[pl.ds(pl.multiple_of(base + index * size, 8), size), :]


def split_kernel(at_ref, keep_ref, other_ref, own_a, own_b, *sends):
    size = own_a.shape[0]
    half = 4 * size
    for step in range(4):
        for side, (base, at, own) in enumerate(((0, at_ref[0], own_a), (half, at_ref[1], own_b))):
            index = (at + step) & 3
            value = chunk(keep_ref, base, index, size)
            value = value + chunk(other_ref, base, index, size).astype(jnp.float32)
            if step == 0:
                own[...] = value
            else:
                to = sends[side * 3 + step - 1]
                to[...] = value.astype(to.dtype)


def second_kernel(at_ref, own_a, own_b, a1, a2, a3, b1, b2, b3, next_a, next_b, *refs):
    sends, (sum_a, sum_b) = refs[:6], refs[6:]
    size = next_a.shape[0]
    for own, one, two, three, total in ((own_a, a1, a2, a3, sum_a), (own_b, b1, b2, b3, sum_b)):
        total[...] = own[...] + (
            one[...].astype(jnp.float32)
            + two[...].astype(jnp.float32)
            + three[...].astype(jnp.float32)
        )
    for step in range(4):
        for side, (at, total, own) in enumerate(
            ((at_ref[1], sum_a, next_a), (at_ref[0], sum_b, next_b))
        ):
            value = chunk(total, 0, (at + step) & 3, size)
            if step == 0:
                own[...] = value
            else:
                to = sends[side * 3 + step - 1]
                to[...] = value.astype(to.dtype)


def third_kernel(own_a, own_b, a1, a2, a3, b1, b2, b3, out_ref):
    size = own_a.shape[0]
    for base, own, one, two, three in ((0, own_a, a1, a2, a3), (size, own_b, b1, b2, b3)):
        total = own[...] + (
            one[...].astype(jnp.float32)
            + two[...].astype(jnp.float32)
            + three[...].astype(jnp.float32)
        )
        out_ref[base : base + size, :] = total.astype(out_ref.dtype)


def ring_kernel(own, one, two, three, out_a, out_b):
    f32 = jnp.float32
    total = (own[...].astype(f32) + two[...].astype(f32)) + (
        one[...].astype(f32) + three[...].astype(f32)
    )
    size = out_a.shape[0]
    out_a[...] = total[:size].astype(out_a.dtype)
    out_b[...] = total[size:].astype(out_b.dtype)


def place(out_ref, base, at, pieces):
    size = pieces[0].shape[0]
    for step, piece in enumerate(pieces):
        index = (at - step) & 3
        out_ref[pl.ds(pl.multiple_of(base + index * size, 8), size), :] = piece[...]


def join_kernel(at_ref, own_a, own_b, a1, a2, a3, b1, b2, b3, out_a, out_b):
    place(out_a, 0, at_ref[1], (own_a, a1, a2, a3))
    place(out_b, 0, at_ref[0], (own_b, b1, b2, b3))


def whole_kernel(at_ref, own_a, own_b, a1, a2, a3, b1, b2, b3, out_ref):
    place(out_ref, 0, at_ref[0], (own_a, a1, a2, a3))
    place(out_ref, out_ref.shape[0] // 2, at_ref[1], (own_b, b1, b2, b3))


def finish_kernel(scale, core_ref, mine_ref, other_ref, one_ref, two_ref):
    width = one_ref.shape[1]
    first = core_ref[0] == 0
    for k in range(width // LANES):
        lines = pl.ds(k * width, width)
        at = slice(k * LANES, (k + 1) * LANES)
        mine = mine_ref[lines, :].astype(jnp.float32) * scale
        other = other_ref[lines, :].astype(jnp.float32) * scale
        one_ref[:, at] = jnp.where(first, mine, other)
        two_ref[:, at] = jnp.where(first, other, mine)


def in_vmem(*refs):
    return [pltpu.VMEM(r.shape, r.dtype) for r in refs]


def call(kernel, out_shape, scalars, scratch=(), vmem=None, limit=6, aliases=None):
    def run(*args):
        n_vmem = len(args) - scalars if vmem is None else vmem
        size = sum(a.size * a.dtype.itemsize for a in (*args, *jax.tree.leaves(out_shape)))
        out_spec = VMEM if vmem is None else HBM
        return pl.pallas_call(
            kernel,
            out_shape=out_shape,
            in_specs=[SMEM] * scalars + [VMEM] * n_vmem + [HBM] * (len(args) - scalars - n_vmem),
            out_specs=jax.tree.map(lambda _: out_spec, out_shape),
            scratch_shapes=scratch,
            input_output_aliases=aliases or {},
            cost_estimate=pl.CostEstimate(flops=0, transcendentals=0, bytes_accessed=size),
            compiler_params=pltpu.CompilerParams(vmem_limit_bytes=limit * 1024 * 1024),
        )(*args)

    return run


def trade(value):
    return lax.all_to_all(value, BOTH, split_axis=0, concat_axis=0, tiled=True)


def along_x(value, step):
    n = lax.axis_size("py")
    return lax.ppermute(value, "py", [(i, (i & ~3) | ((i + step) & 3)) for i in range(n)])


def along_y(value, step):
    n = lax.axis_size("py")
    return lax.ppermute(value, "py", [(i, (i + 4 * step) % n) for i in range(n)])


def along_z(value, step):
    n = lax.axis_size("px")
    return lax.ppermute(value, "px", [(i, (i + 2 * step) % n) for i in range(n)])


def sibling(value):
    n = lax.axis_size("px")
    return lax.ppermute(value, "px", [(i, i ^ 1) for i in range(n)])


def local(
    features,
    weight_one,
    weight_two,
    tile_values,
    tile_rows,
    tile_cols,
    tile_count,
    send_rows,
    send_count,
    stale_hidden,
    stale_grad,
    out_grad,
):
    bf16, f32 = jnp.bfloat16, jnp.float32
    parts = lax.axis_size(BOTH)
    own, width = features.shape
    slots = send_rows.shape[2]
    boundary = parts * slots
    cols = own + boundary
    shape = jax.ShapeDtypeStruct
    slot_ids = jnp.arange(slots, dtype=jnp.int32)
    sent = slot_ids[None, :] < send_count[0][:, None]
    idx = jnp.where(sent, send_rows[0], -1).reshape(boundary // LANES, LANES)
    core = (lax.axis_index("px") % 2).astype(jnp.int32).reshape(1)
    py = lax.axis_index("py").astype(jnp.int32)
    at = jnp.stack([py % 4, py // 4])

    pack = shape((boundary, width + LANES), bf16)
    square, square32 = shape((own, width), bf16), shape((own, width), f32)
    near, far = shape((own, own), bf16), shape((own, boundary), bf16)
    near32, far32 = shape((own, own), f32), shape((own, boundary), f32)
    slab, slots_in = shape((boundary, width), bf16), shape((parts, slots, width), bf16)
    box = shape((parts, 2 * slots, width), bf16)
    weight = shape(weight_one.shape, bf16)
    picks = shape((boundary, own), bf16)
    semaphores = lambda count: [pltpu.SemaphoreType.DMA((count,))]
    lines = width * width // LANES
    keep, send = shape((lines, LANES), f32), shape((lines, LANES), bf16)

    outgoing = call(
        pack_kernel,
        pack,
        0,
        in_vmem(square, picks, pack) + semaphores(5),
        1,
        PACK,
    )(idx, features)
    arrived = trade(outgoing.reshape(parts, slots, -1)).reshape(boundary, -1)

    *kept, boxes = call(
        local_kernel,
        (near, far, square32, square32, box),
        3,
        in_vmem(
            tile_values, square, square, weight, slab, near32, far32, near, far, far, square32, square32, slots_in
        )
        + semaphores(10),
        1,
        LOCAL,
    )(tile_rows[0], tile_cols[0], tile_count, idx, tile_values, features, out_grad, weight_two, stale_grad)
    near_adj, far_adj, agg, hidden_grad = kept

    boxes, keep, send = call(
        main_kernel,
        (box, keep, send),
        1,
        in_vmem(
            pack, near, far, square32, weight, square32, slab, square, picks, slots_in, keep, send
        )
        + semaphores(11),
        1,
        MAIN,
        {10: 0},
    )(core, idx, arrived, near_adj, far_adj, agg, weight_one, hidden_grad, stale_hidden, out_grad, boxes)

    big, small = lines // 8, lines // 32
    six = lambda size: (shape((size, LANES), bf16),) * 6
    pair = lambda size, dtype: (shape((size, LANES), dtype),) * 2
    own_a, own_b, *out = call(split_kernel, pair(big, f32) + six(big), 1)(at, keep, sibling(send))
    got = [along_x(out[k], k + 1) for k in range(3)] + [along_y(out[3 + k], k + 1) for k in range(3)]
    own_a, own_b, *out = call(
        second_kernel,
        pair(small, f32) + six(small),
        1,
        [pltpu.VMEM((big, LANES), f32)] * 2,
    )(at, own_a, own_b, *got)
    got = [along_y(out[k], k + 1) for k in range(3)] + [along_x(out[3 + k], k + 1) for k in range(3)]
    total = call(third_kernel, shape((2 * small, LANES), bf16), 0)(own_a, own_b, *got)
    got = [along_z(total, k + 1) for k in range(3)]
    own_a, own_b = call(ring_kernel, pair(small, bf16), 0)(total, *got)
    got = [along_y(own_a, k + 1) for k in range(3)] + [along_x(own_b, k + 1) for k in range(3)]
    own_a, own_b = call(join_kernel, pair(big, bf16), 1)(at, own_a, own_b, *got)
    got = [along_x(own_a, k + 1) for k in range(3)] + [along_y(own_b, k + 1) for k in range(3)]
    mine = call(whole_kernel, shape((lines, LANES), bf16), 1)(at, own_a, own_b, *got)
    scale = 1.0 / math.sqrt(own * parts)
    one, two = call(
        functools.partial(finish_kernel, scale),
        (shape((width, width), f32),) * 2,
        1,
    )(core, mine, sibling(mine))

    boxes = trade(boxes)
    next_hidden = boxes[:, :slots].reshape(boundary, width)
    grads = boxes[:, slots:]
    next_grad = jnp.where(sent[:, :, None], grads, jnp.zeros_like(grads)).reshape(boundary, width)
    return next_hidden, next_grad, one, two


def solution(mesh):
    in_specs = (
        P(BOTH, None),
        P(),
        P(),
        P(BOTH, None, None),
        P(BOTH, None),
        P(BOTH, None),
        P(BOTH),
        P(BOTH, None, None),
        P(BOTH, None),
        P(BOTH, None),
        P(BOTH, None),
        P(BOTH, None),
    )
    out_specs = (P(BOTH, None), P(BOTH, None), P(), P())
    return jax.shard_map(local, mesh=mesh, in_specs=in_specs, out_specs=out_specs, check_vma=False)
```

time: 202 us -> 177 us (0.88)
  blocking collectives: 54.8 us -> 0 us
  starting transfers between devices: 27.6 us -> 67.8 us
  local copies, waits for them, and re-layouts: 19.2 us -> 3.03 us
  Pallas kernels: 28.2 us -> 39.6 us
  other arithmetic: 8.41 us -> 5.83 us
  waiting for transfers between devices: 61.3 us -> 59.1 us
    all_to_all x4 -> x0, blocking collectives: 54.8 us -> none  [trade(): lax.all_to_all(value, axis, split_axis=0, concat_axis=0, tiled=True, axis...]
    ppermute x2 -> x29, starting transfers between devices: 2.39 us -> 51.5 us  [the longest x12 17.3 us: along_x(): lax.ppermute(value, 'py', [(i, i & ~3 | i + step & 3) for i in range(n)])]
    all_to_all x3 -> x2, waiting for transfers between devices: 58.8 us -> 14 us  [trade(): return lax.all_to_all(value, BOTH, split_axis=0, concat_axis=0, tiled=True)]
    ppermute x2 -> x29, waiting for transfers between devices: 2.48 us -> 45.1 us  [the longest x12 33.5 us: along_x(): lax.ppermute(value, 'py', [(i, i & ~3 | i + step & 3) for i in range(n)])]
    pallas_call x3 -> x10, Pallas kernels: 28.2 us -> 39.6 us  [run(): pl.pallas_call(kernel, out_shape=out_shape, in_specs=[SMEM] * scalars + [...]
    unnamed x27 -> x8, local copies, waits for them, and re-layouts: 13.6 us -> 2.59 us
    all_to_all x3 -> x2, starting transfers between devices: 25.2 us -> 16.3 us  [trade(): return lax.all_to_all(value, BOTH, split_axis=0, concat_axis=0, tiled=True)]
    transpose x2 -> x0, local copies, waits for them, and re-layouts: 5.02 us -> none  [the longest x1 3.06 us: local(): one = jnp.moveaxis(one, 0, 1).reshape(width, width)]
  transfers between devices with their start and end apart: 5 -> 31, of which waited for: 4 -> 16; matrix products, arithmetic and copies ran while one was open for 1% -> 0% of each run, Pallas kernels for 5% -> 10%
where the time goes in v2:
time: 177 us
  starting transfers between devices  67.8 us (38%)
  waiting for transfers between devices  59.1 us (33%)
  Pallas kernels  39.6 us (22%)
  other arithmetic  5.83 us (3%)
  local copies, waits for them, and re-layouts  3.03 us (2%)
    pallas_call x10, Pallas kernels, run(): pl.pallas_call(kernel, out_shape=out_shape, in_specs=[SMEM] * scalars + [...  39.6 us
    ppermute x12, waiting for transfers between devices, along_x(): lax.ppermute(value, 'py', [(i, i & ~3 | i + step & 3) for i in range(n)])  33.5 us
    ppermute x12, starting transfers between devices, along_x(): lax.ppermute(value, 'py', [(i, i & ~3 | i + step & 3) for i in range(n)])  17.3 us
    ppermute x12, starting transfers between devices, along_y(): lax.ppermute(value, 'py', [(i, (i + 4 * step) % n) for i in range(n)])  16.8 us
    all_to_all x2, starting transfers between devices, trade(): return lax.all_to_all(value, BOTH, split_axis=0, concat_axis=0, tiled=True)  16.3 us
    all_to_all x2, waiting for transfers between devices, trade(): return lax.all_to_all(value, BOTH, split_axis=0, concat_axis=0, tiled=True)  14 us
    ppermute x2, starting transfers between devices, sibling(): return lax.ppermute(value, 'px', [(i, i ^ 1) for i in range(n)])  12.5 us
    ppermute x12, waiting for transfers between devices, along_y(): lax.ppermute(value, 'py', [(i, (i + 4 * step) % n) for i in range(n)])  6.87 us
  transfers between devices with their start and end apart: 31, of which 16 were waited for; matrix products, arithmetic and copies ran while one was open for 0% of the time, Pallas kernels for 10%

profile of v2, /device:TPU:1, one launch (start us, length us, event | category | flops | bytes accessed | tf_op | source)
XLA Modules:
  0.0 176.8 jit_solution(10741190505902523104)
XLA Ops:
  1.1 1.3 reduce.3
  2.7 0.8 copy.18
  3.7 0.6 compare_select_fusion.idx_ref
  4.3 4.2 %shard_map.147 = bf16[1024,896]{1,0:T(8,128)(2,1)} custom-call(s32[8,128]{1,0:T(8,128)} %compare_select_fusion.idx_ref, bf16[768,768]{1,0:T(8,128)(2,1)} %features_hbm.3), custom_call_target="tpu_custom_call" | custom-call | bytes 3018752 | tf_op jit(solution)/shard_map/pallas_call | solution.py:331
  8.5 11.5 %all-to-all-start = ((bf16[128,8,896]{2,1,0:T(8,128)(2,1)}), bf16[128,8,896]{2,1,0:T(8,128)(2,1)S(1)}, u32[]{:S(2)}, u32[]{:S(2)}) async-start(bf16[128,8,896]{2,1,0:T(8,128)(2,1)} %bitcast.12), calls=%async_computation | async-start | bytes 3670016 | tf_op jit(solution)/shard_map/all_to_all | solution.py:346
  20.6 12.2 %shard_map.148 = (bf16[768,768]{1,0:T(8,128)(2,1)}, bf16[768,1024]{1,0:T(8,128)(2,1)}, f32[768,768]{1,0:T(8,128)}, f32[768,768]{1,0:T(8,128)}, bf16[128,16,768]{2,1,0:T(8,128)(2,1)}) custom-call(s32[32]{0:T(128)} %bitcast.14, s32[32]{0:T(128)} %bitcast.15, s32[1]{0:T(128)S(6)} %copy.20.count_ref, s32[8,128]{1,0:T(8,128)} %compare_select_fusion.idx_ref, ...), custom_call_target="tpu_custom_call" | custom-call | bytes 16781572 | tf_op jit(solution)/shard_map/pallas_call | solution.py:331
  32.9 14.0 %all-to-all-done = bf16[128,8,896]{2,1,0:T(8,128)(2,1)S(1)} async-done(((bf16[128,8,896]{2,1,0:T(8,128)(2,1)}), bf16[128,8,896]{2,1,0:T(8,128)(2,1)S(1)}, u32[]{:S(2)}, u32[]{:S(2)}) %all-to-all-start) | async-done | bytes 1835040 | tf_op jit(solution)/shard_map/all_to_all | solution.py:346
  46.9 1.3 copy-done.1
  48.2 17.7 %shard_map.149 = (bf16[128,16,768]{2,1,0:T(8,128)(2,1)}, f32[4608,128]{1,0:T(8,128)}, bf16[4608,128]{1,0:T(8,128)(2,1)}) custom-call(s32[1]{0:T(128)} %bitcast.core_ref, s32[8,128]{1,0:T(8,128)} %compare_select_fusion.idx_ref, bf16[1024,896]{1,0:T(8,128)(2,1)} %bitcast.13, ...), custom_call_target="tpu_custom_call", output_to_operand_aliasing={{0}: (10, {})} | custom-call | bytes 23072772 | tf_op jit(solution)/shard_map/pallas_call | solution.py:331
  65.9 1.3 collective-permute-start
  67.2 4.8 %all-to-all-start.1 = ((bf16[128,16,768]{2,1,0:T(8,128)(2,1)}), bf16[128,16,768]{2,1,0:T(8,128)(2,1)}, u32[]{:S(2)}, u32[]{:S(2)}) async-start(bf16[128,16,768]{2,1,0:T(8,128)(2,1)} %get-tuple-element.39), calls=%async_computation.1 | async-start | bytes 6291456 | tf_op jit(solution)/shard_map/all_to_all | solution.py:346
  72.1 0.7 shard_map.150
  72.8 1.3 collective-permute-start.1
  74.1 2.4 %collective-permute-start.2 = (bf16[576,128]{1,0:T(8,128)(2,1)S(1)}, bf16[576,128]{1,0:T(8,128)(2,1)S(1)}, u32[]{:S(2)}, u32[]{:S(2)}) collective-permute-start(bf16[576,128]{1,0:T(8,128)(2,1)S(1)} %get-tuple-element.45), channel_id=1, source_target_pairs={{0,2},{1,3},{2,0},{3,1},{4,6},{5,7},{6,4},{7,5},{8,10},{9,11},{10,... | collective-permute-start | bytes 442376 | tf_op jit(solution)/shard_map/ppermute | solution.py:351
  76.6 1.2 collective-permute-start.3
  77.7 1.2 collective-permute-start.4
  79.0 2.5 %collective-permute-start.5 = (bf16[576,128]{1,0:T(8,128)(2,1)S(1)}, bf16[576,128]{1,0:T(8,128)(2,1)S(1)}, u32[]{:S(2)}, u32[]{:S(2)}) collective-permute-start(bf16[576,128]{1,0:T(8,128)(2,1)S(1)} %get-tuple-element.48), channel_id=1, source_target_pairs={{0,8},{1,9},{2,10},{3,11},{4,12},{5,13},{6,14},{7,15},{8,0},{9,1},... | collective-permute-start | bytes 442376 | tf_op jit(solution)/shard_map/ppermute | solution.py:356
  81.5 29.6 %collective-permute-done.1.a1 = bf16[576,128]{1,0:T(8,128)(2,1)S(1)} collective-permute-done((bf16[576,128]{1,0:T(8,128)(2,1)S(1)}, bf16[576,128]{1,0:T(8,128)(2,1)S(1)}, u32[]{:S(2)}, u32[]{:S(2)}) %collective-permute-start.1) | collective-permute-done | bytes 147488 | tf_op jit(solution)/shard_map/ppermute | solution.py:351
  111.1 2.6 %collective-permute-start.6 = (bf16[576,128]{1,0:T(8,128)(2,1)S(1)}, bf16[576,128]{1,0:T(8,128)(2,1)S(1)}, u32[]{:S(2)}, u32[]{:S(2)}) collective-permute-start(bf16[576,128]{1,0:T(8,128)(2,1)S(1)} %get-tuple-element.49), channel_id=1, source_target_pairs={{0,12},{1,13},{2,14},{3,15},{4,0},{5,1},{6,2},{7,3},{8,4},{9,5},{1... | collective-permute-start | bytes 442376 | tf_op jit(solution)/shard_map/ppermute | solution.py:356
  113.7 0.7 collective-permute-done.2.a2
  114.6 1.3 collective-permute-done.6.b3
  115.8 0.8 shard_map.151
  116.7 2.7 %collective-permute-start.11 = (bf16[144,128]{1,0:T(8,128)(2,1)S(1)}, bf16[144,128]{1,0:T(8,128)(2,1)S(1)}, u32[]{:S(2)}, u32[]{:S(2)}) collective-permute-start(bf16[144,128]{1,0:T(8,128)(2,1)S(1)} %get-tuple-element.56), channel_id=1, source_target_pairs={{0,2},{1,3},{2,0},{3,1},{4,6},{5,7},{6,4},{7,5},{8,10},{9,11},{10,... | collective-permute-start | bytes 110600 | tf_op jit(solution)/shard_map/ppermute | solution.py:351
  119.4 0.8 collective-permute-start.12
  120.3 3.7 %collective-permute-start.8 = (bf16[144,128]{1,0:T(8,128)(2,1)S(1)}, bf16[144,128]{1,0:T(8,128)(2,1)S(1)}, u32[]{:S(2)}, u32[]{:S(2)}) collective-permute-start(bf16[144,128]{1,0:T(8,128)(2,1)S(1)} %get-tuple-element.53), channel_id=1, source_target_pairs={{0,8},{1,9},{2,10},{3,11},{4,12},{5,13},{6,14},{7,15},{8,0},{9,1},... | collective-permute-start | bytes 110600 | tf_op jit(solution)/shard_map/ppermute | solution.py:356
  124.2 1.5 collective-permute-done.8.a2
  125.8 1.1 collective-permute-done.9.a3
  126.9 1.0 collective-permute-start.13
  127.9 2.9 %collective-permute-start.14 = (bf16[288,128]{1,0:T(8,128)(2,1)S(1)}, bf16[288,128]{1,0:T(8,128)(2,1)S(1)}, u32[]{:S(2)}, u32[]{:S(2)}) collective-permute-start(bf16[288,128]{1,0:T(8,128)(2,1)S(1)} %shard_map.152.own), channel_id=1, source_target_pairs={{0,64},{16,80},{32,96},{48,112},{64,0},{80,16},{96,32},{112,48},{1... | collective-permute-start | bytes 221192 | tf_op jit(solution)/shard_map/ppermute | solution.py:361
  130.8 0.9 collective-permute-start.15
  131.8 1.6 collective-permute-done.14.two
  133.4 0.7 collective-permute-done.15.three
  134.4 2.3 %collective-permute-start.17 = (bf16[144,128]{1,0:T(8,128)(2,1)S(1)}, bf16[144,128]{1,0:T(8,128)(2,1)S(1)}, u32[]{:S(2)}, u32[]{:S(2)}) collective-permute-start(bf16[144,128]{1,0:T(8,128)(2,1)S(1)} %get-tuple-element.58.own_a), channel_id=1, source_target_pairs={{0,8},{1,9},{2,10},{3,11},{4,12},{5,13},{6,14},{7,15},{8,0},{9,1},... | collective-permute-start | bytes 110600 | tf_op jit(solution)/shard_map/ppermute | solution.py:356
  136.7 1.4 collective-permute-start.18
  138.7 1.7 collective-permute-start.20
  140.4 2.1 %collective-permute-start.21 = (bf16[144,128]{1,0:T(8,128)(2,1)S(1)}, bf16[144,128]{1,0:T(8,128)(2,1)S(1)}, u32[]{:S(2)}, u32[]{:S(2)}) collective-permute-start(bf16[144,128]{1,0:T(8,128)(2,1)S(1)} %get-tuple-element.59.own_b), channel_id=1, source_target_pairs={{0,3},{1,0},{2,1},{3,2},{4,7},{5,4},{6,5},{7,6},{8,11},{9,8},{10,9... | collective-permute-start | bytes 110600 | tf_op jit(solution)/shard_map/ppermute | solution.py:351
  144.1 1.4 collective-permute-start.22
  145.5 3.1 %collective-permute-start.23 = (bf16[576,128]{1,0:T(8,128)(2,1)S(1)}, bf16[576,128]{1,0:T(8,128)(2,1)S(1)}, u32[]{:S(2)}, u32[]{:S(2)}) collective-permute-start(bf16[576,128]{1,0:T(8,128)(2,1)S(1)} %get-tuple-element.60.own_a), channel_id=1, source_target_pairs={{0,2},{1,3},{2,0},{3,1},{4,6},{5,7},{6,4},{7,5},{8,10},{9,11},{10,... | collective-permute-start | bytes 442376 | tf_op jit(solution)/shard_map/ppermute | solution.py:351
  148.6 1.2 collective-permute-start.26
  149.8 0.9 collective-permute-done.22.a1
  150.6 1.2 collective-permute-start.27
  151.8 1.3 collective-permute-done.23.a2
  153.1 2.3 %collective-permute-done.25.b1 = bf16[576,128]{1,0:T(8,128)(2,1)S(1)} collective-permute-done((bf16[576,128]{1,0:T(8,128)(2,1)S(1)}, bf16[576,128]{1,0:T(8,128)(2,1)S(1)}, u32[]{:S(2)}, u32[]{:S(2)}) %collective-permute-start.25) | collective-permute-done | bytes 147488 | tf_op jit(solution)/shard_map/ppermute | solution.py:356
  155.9 0.6 shard_map.155.mine_ref
  156.6 11.2 %collective-permute-start.28 = (bf16[4608,128]{1,0:T(8,128)(2,1)S(1)}, bf16[4608,128]{1,0:T(8,128)(2,1)S(1)}, u32[]{:S(2)}, u32[]{:S(2)}) collective-permute-start(bf16[4608,128]{1,0:T(8,128)(2,1)S(1)} %shard_map.155.mine_ref), channel_id=1, source_target_pairs={{0,16},{16,0},{32,48},{48,32},{64,80},{80,64},{96,112},{112,96},{1... | collective-permute-start | bytes 3538952 | tf_op jit(solution)/shard_map/ppermute | solution.py:366
  167.9 2.4 %collective-permute-done.28.other_ref = bf16[4608,128]{1,0:T(8,128)(2,1)S(1)} collective-permute-done((bf16[4608,128]{1,0:T(8,128)(2,1)S(1)}, bf16[4608,128]{1,0:T(8,128)(2,1)S(1)}, u32[]{:S(2)}, u32[]{:S(2)}) %collective-permute-start.28) | collective-permute-done | bytes 1179680 | tf_op jit(solution)/shard_map/ppermute | solution.py:366
  170.3 2.8 %shard_map.156 = (f32[768,768]{1,0:T(8,128)}, f32[768,768]{1,0:T(8,128)}) custom-call(s32[1]{0:T(128)} %bitcast.core_ref, bf16[4608,128]{1,0:T(8,128)(2,1)S(1)} %shard_map.155.mine_ref, bf16[4608,128]{1,0:T(8,128)(2,1)S(1)} %collective-permute-done.28.other_ref), custom_call_target="tpu_custom_call" | custom-call | bytes 7077892 | tf_op jit(solution)/shard_map/pallas_call | solution.py:331
  173.0 3.8 %fusion = (bf16[1024,768]{1,0:T(8,128)(2,1)}, bf16[1024,768]{1,0:T(8,128)(2,1)}) fusion(bf16[128,16,768]{2,1,0:T(8,128)(2,1)} %all-to-all-done.1, pred[128,8]{1,0:T(8,128)(4,1)S(1)} %iota_compare_fusion), kind=kLoop, calls=%fused_computation.1 | loop fusion | flops 786432 | bytes 6292480 | tf_op jit(solution)/shard_map/reshape | solution.py:474
  (43 shorter events, 4.8 us)
Async XLA Ops:
  8.5 38.4 %all-to-all-start = ((bf16[128,8,896]{2,1,0:T(8,128)(2,1)}), bf16[128,8,896]{2,1,0:T(8,128)(2,1)S(1)}, u32[]{:S(2)}, u32[]{:S(2)}) async-start(bf16[128,8,896]{2,1,0:T(8,128)(2,1)} %bitcast.12), calls=%async_computation | async-start | bytes 3670016 | tf_op jit(solution)/shard_map/all_to_all | solution.py:346
  46.9 1.3 copy-start.1
  65.9 6.2 %collective-permute-start = (bf16[4608,128]{1,0:T(8,128)(2,1)}, bf16[4608,128]{1,0:T(8,128)(2,1)S(1)}, u32[]{:S(2)}, u32[]{:S(2)}) collective-permute-start(bf16[4608,128]{1,0:T(8,128)(2,1)} %get-tuple-element.41), channel_id=1, source_target_pairs={{0,16},{16,0},{32,48},{48,32},{64,80},{80,64},{96,112},{112,96},{1... | collective-permute-start | bytes 3538952 | tf_op jit(solution)/shard_map/ppermute | solution.py:366
  67.2 4.9 %copy-start = (f32[4608,128]{1,0:T(8,128)S(1)}, f32[4608,128]{1,0:T(8,128)}, u32[]{:S(2)}) copy-start(f32[4608,128]{1,0:T(8,128)} %get-tuple-element.40.keep_ref) | copy-start | bytes 7077892
  67.2 105.9 %all-to-all-start.1 = ((bf16[128,16,768]{2,1,0:T(8,128)(2,1)}), bf16[128,16,768]{2,1,0:T(8,128)(2,1)}, u32[]{:S(2)}, u32[]{:S(2)}) async-start(bf16[128,16,768]{2,1,0:T(8,128)(2,1)} %get-tuple-element.39), calls=%async_computation.1 | async-start | bytes 6291456 | tf_op jit(solution)/shard_map/all_to_all | solution.py:346
  72.8 38.3 %collective-permute-start.1 = (bf16[576,128]{1,0:T(8,128)(2,1)S(1)}, bf16[576,128]{1,0:T(8,128)(2,1)S(1)}, u32[]{:S(2)}, u32[]{:S(2)}) collective-permute-start(bf16[576,128]{1,0:T(8,128)(2,1)S(1)} %get-tuple-element.44), channel_id=1, source_target_pairs={{0,1},{1,2},{2,3},{3,0},{4,5},{5,6},{6,7},{7,4},{8,9},{9,10},{10,1... | collective-permute-start | bytes 442376 | tf_op jit(solution)/shard_map/ppermute | solution.py:351
  74.1 40.3 %collective-permute-start.2 = (bf16[576,128]{1,0:T(8,128)(2,1)S(1)}, bf16[576,128]{1,0:T(8,128)(2,1)S(1)}, u32[]{:S(2)}, u32[]{:S(2)}) collective-permute-start(bf16[576,128]{1,0:T(8,128)(2,1)S(1)} %get-tuple-element.45), channel_id=1, source_target_pairs={{0,2},{1,3},{2,0},{3,1},{4,6},{5,7},{6,4},{7,5},{8,10},{9,11},{10,... | collective-permute-start | bytes 442376 | tf_op jit(solution)/shard_map/ppermute | solution.py:351
  76.6 37.9 %collective-permute-start.3 = (bf16[576,128]{1,0:T(8,128)(2,1)S(1)}, bf16[576,128]{1,0:T(8,128)(2,1)S(1)}, u32[]{:S(2)}, u32[]{:S(2)}) collective-permute-start(bf16[576,128]{1,0:T(8,128)(2,1)S(1)} %get-tuple-element.46), channel_id=1, source_target_pairs={{0,3},{1,0},{2,1},{3,2},{4,7},{5,4},{6,5},{7,6},{8,11},{9,8},{10,9... | collective-permute-start | bytes 442376 | tf_op jit(solution)/shard_map/ppermute | solution.py:351
  77.7 36.7 %collective-permute-start.4 = (bf16[576,128]{1,0:T(8,128)(2,1)S(1)}, bf16[576,128]{1,0:T(8,128)(2,1)S(1)}, u32[]{:S(2)}, u32[]{:S(2)}) collective-permute-start(bf16[576,128]{1,0:T(8,128)(2,1)S(1)} %get-tuple-element.47), channel_id=1, source_target_pairs={{0,4},{1,5},{2,6},{3,7},{4,8},{5,9},{6,10},{7,11},{8,12},{9,13},{1... | collective-permute-start | bytes 442376 | tf_op jit(solution)/shard_map/ppermute | solution.py:356
  79.0 35.6 %collective-permute-start.5 = (bf16[576,128]{1,0:T(8,128)(2,1)S(1)}, bf16[576,128]{1,0:T(8,128)(2,1)S(1)}, u32[]{:S(2)}, u32[]{:S(2)}) collective-permute-start(bf16[576,128]{1,0:T(8,128)(2,1)S(1)} %get-tuple-element.48), channel_id=1, source_target_pairs={{0,8},{1,9},{2,10},{3,11},{4,12},{5,13},{6,14},{7,15},{8,0},{9,1},... | collective-permute-start | bytes 442376 | tf_op jit(solution)/shard_map/ppermute | solution.py:356
  111.1 4.7 %collective-permute-start.6 = (bf16[576,128]{1,0:T(8,128)(2,1)S(1)}, bf16[576,128]{1,0:T(8,128)(2,1)S(1)}, u32[]{:S(2)}, u32[]{:S(2)}) collective-permute-start(bf16[576,128]{1,0:T(8,128)(2,1)S(1)} %get-tuple-element.49), channel_id=1, source_target_pairs={{0,12},{1,13},{2,14},{3,15},{4,0},{5,1},{6,2},{7,3},{8,4},{9,5},{1... | collective-permute-start | bytes 442376 | tf_op jit(solution)/shard_map/ppermute | solution.py:356
  116.6 7.4 %collective-permute-start.10 = (bf16[144,128]{1,0:T(8,128)(2,1)S(1)}, bf16[144,128]{1,0:T(8,128)(2,1)S(1)}, u32[]{:S(2)}, u32[]{:S(2)}) collective-permute-start(bf16[144,128]{1,0:T(8,128)(2,1)S(1)} %get-tuple-element.55), channel_id=1, source_target_pairs={{0,1},{1,2},{2,3},{3,0},{4,5},{5,6},{6,7},{7,4},{8,9},{9,10},{10,1... | collective-permute-start | bytes 110600 | tf_op jit(solution)/shard_map/ppermute | solution.py:351
  116.7 7.5 %collective-permute-start.11 = (bf16[144,128]{1,0:T(8,128)(2,1)S(1)}, bf16[144,128]{1,0:T(8,128)(2,1)S(1)}, u32[]{:S(2)}, u32[]{:S(2)}) collective-permute-start(bf16[144,128]{1,0:T(8,128)(2,1)S(1)} %get-tuple-element.56), channel_id=1, source_target_pairs={{0,2},{1,3},{2,0},{3,1},{4,6},{5,7},{6,4},{7,5},{8,10},{9,11},{10,... | collective-permute-start | bytes 110600 | tf_op jit(solution)/shard_map/ppermute | solution.py:351
  119.4 4.8 %collective-permute-start.12 = (bf16[144,128]{1,0:T(8,128)(2,1)S(1)}, bf16[144,128]{1,0:T(8,128)(2,1)S(1)}, u32[]{:S(2)}, u32[]{:S(2)}) collective-permute-start(bf16[144,128]{1,0:T(8,128)(2,1)S(1)} %get-tuple-element.57), channel_id=1, source_target_pairs={{0,3},{1,0},{2,1},{3,2},{4,7},{5,4},{6,5},{7,6},{8,11},{9,8},{10,9... | collective-permute-start | bytes 110600 | tf_op jit(solution)/shard_map/ppermute | solution.py:351
  120.2 4.0 %collective-permute-start.7 = (bf16[144,128]{1,0:T(8,128)(2,1)S(1)}, bf16[144,128]{1,0:T(8,128)(2,1)S(1)}, u32[]{:S(2)}, u32[]{:S(2)}) collective-permute-start(bf16[144,128]{1,0:T(8,128)(2,1)S(1)} %get-tuple-element.52), channel_id=1, source_target_pairs={{0,4},{1,5},{2,6},{3,7},{4,8},{5,9},{6,10},{7,11},{8,12},{9,13},{1... | collective-permute-start | bytes 110600 | tf_op jit(solution)/shard_map/ppermute | solution.py:356
  120.3 5.5 %collective-permute-start.8 = (bf16[144,128]{1,0:T(8,128)(2,1)S(1)}, bf16[144,128]{1,0:T(8,128)(2,1)S(1)}, u32[]{:S(2)}, u32[]{:S(2)}) collective-permute-start(bf16[144,128]{1,0:T(8,128)(2,1)S(1)} %get-tuple-element.53), channel_id=1, source_target_pairs={{0,8},{1,9},{2,10},{3,11},{4,12},{5,13},{6,14},{7,15},{8,0},{9,1},... | collective-permute-start | bytes 110600 | tf_op jit(solution)/shard_map/ppermute | solution.py:356
  124.0 2.8 %collective-permute-start.9 = (bf16[144,128]{1,0:T(8,128)(2,1)S(1)}, bf16[144,128]{1,0:T(8,128)(2,1)S(1)}, u32[]{:S(2)}, u32[]{:S(2)}) collective-permute-start(bf16[144,128]{1,0:T(8,128)(2,1)S(1)} %get-tuple-element.54), channel_id=1, source_target_pairs={{0,12},{1,13},{2,14},{3,15},{4,0},{5,1},{6,2},{7,3},{8,4},{9,5},{1... | collective-permute-start | bytes 110600 | tf_op jit(solution)/shard_map/ppermute | solution.py:356
  126.9 40.9 %copy-start.2 = (s32[1,128]{1,0:T(1,128)S(1)}, s32[1,128]{1,0:T(1,128)}, u32[]{:S(2)}) copy-start(s32[1,128]{1,0:T(1,128)} %param.20) | copy-start | bytes 1540
  126.9 4.9 %collective-permute-start.13 = (bf16[288,128]{1,0:T(8,128)(2,1)S(1)}, bf16[288,128]{1,0:T(8,128)(2,1)S(1)}, u32[]{:S(2)}, u32[]{:S(2)}) collective-permute-start(bf16[288,128]{1,0:T(8,128)(2,1)S(1)} %shard_map.152.own), channel_id=1, source_target_pairs={{0,32},{16,48},{32,64},{48,80},{64,96},{80,112},{96,0},{112,16},{1... | collective-permute-start | bytes 221192 | tf_op jit(solution)/shard_map/ppermute | solution.py:361
  127.9 5.5 %collective-permute-start.14 = (bf16[288,128]{1,0:T(8,128)(2,1)S(1)}, bf16[288,128]{1,0:T(8,128)(2,1)S(1)}, u32[]{:S(2)}, u32[]{:S(2)}) collective-permute-start(bf16[288,128]{1,0:T(8,128)(2,1)S(1)} %shard_map.152.own), channel_id=1, source_target_pairs={{0,64},{16,80},{32,96},{48,112},{64,0},{80,16},{96,32},{112,48},{1... | collective-permute-start | bytes 221192 | tf_op jit(solution)/shard_map/ppermute | solution.py:361
  130.8 3.2 %collective-permute-start.15 = (bf16[288,128]{1,0:T(8,128)(2,1)S(1)}, bf16[288,128]{1,0:T(8,128)(2,1)S(1)}, u32[]{:S(2)}, u32[]{:S(2)}) collective-permute-start(bf16[288,128]{1,0:T(8,128)(2,1)S(1)} %shard_map.152.own), channel_id=1, source_target_pairs={{0,96},{16,112},{32,0},{48,16},{64,32},{80,48},{96,64},{112,80},{1... | collective-permute-start | bytes 221192 | tf_op jit(solution)/shard_map/ppermute | solution.py:361
  134.1 6.3 %collective-permute-start.16 = (bf16[144,128]{1,0:T(8,128)(2,1)S(1)}, bf16[144,128]{1,0:T(8,128)(2,1)S(1)}, u32[]{:S(2)}, u32[]{:S(2)}) collective-permute-start(bf16[144,128]{1,0:T(8,128)(2,1)S(1)} %get-tuple-element.58.own_a), channel_id=1, source_target_pairs={{0,4},{1,5},{2,6},{3,7},{4,8},{5,9},{6,10},{7,11},{8,12},{9,13},{1... | collective-permute-start | bytes 110600 | tf_op jit(solution)/shard_map/ppermute | solution.py:356
  134.4 8.1 %collective-permute-start.17 = (bf16[144,128]{1,0:T(8,128)(2,1)S(1)}, bf16[144,128]{1,0:T(8,128)(2,1)S(1)}, u32[]{:S(2)}, u32[]{:S(2)}) collective-permute-start(bf16[144,128]{1,0:T(8,128)(2,1)S(1)} %get-tuple-element.58.own_a), channel_id=1, source_target_pairs={{0,8},{1,9},{2,10},{3,11},{4,12},{5,13},{6,14},{7,15},{8,0},{9,1},... | collective-permute-start | bytes 110600 | tf_op jit(solution)/shard_map/ppermute | solution.py:356
  136.7 5.8 %collective-permute-start.18 = (bf16[144,128]{1,0:T(8,128)(2,1)S(1)}, bf16[144,128]{1,0:T(8,128)(2,1)S(1)}, u32[]{:S(2)}, u32[]{:S(2)}) collective-permute-start(bf16[144,128]{1,0:T(8,128)(2,1)S(1)} %get-tuple-element.58.own_a), channel_id=1, source_target_pairs={{0,12},{1,13},{2,14},{3,15},{4,0},{5,1},{6,2},{7,3},{8,4},{9,5},{1... | collective-permute-start | bytes 110600 | tf_op jit(solution)/shard_map/ppermute | solution.py:356
  138.1 4.4 %collective-permute-start.19 = (bf16[144,128]{1,0:T(8,128)(2,1)S(1)}, bf16[144,128]{1,0:T(8,128)(2,1)S(1)}, u32[]{:S(2)}, u32[]{:S(2)}) collective-permute-start(bf16[144,128]{1,0:T(8,128)(2,1)S(1)} %get-tuple-element.59.own_b), channel_id=1, source_target_pairs={{0,1},{1,2},{2,3},{3,0},{4,5},{5,6},{6,7},{7,4},{8,9},{9,10},{10,1... | collective-permute-start | bytes 110600 | tf_op jit(solution)/shard_map/ppermute | solution.py:351
  138.7 4.3 %collective-permute-start.20 = (bf16[144,128]{1,0:T(8,128)(2,1)S(1)}, bf16[144,128]{1,0:T(8,128)(2,1)S(1)}, u32[]{:S(2)}, u32[]{:S(2)}) collective-permute-start(bf16[144,128]{1,0:T(8,128)(2,1)S(1)} %get-tuple-element.59.own_b), channel_id=1, source_target_pairs={{0,2},{1,3},{2,0},{3,1},{4,6},{5,7},{6,4},{7,5},{8,10},{9,11},{10,... | collective-permute-start | bytes 110600 | tf_op jit(solution)/shard_map/ppermute | solution.py:351
  140.4 3.1 %collective-permute-start.21 = (bf16[144,128]{1,0:T(8,128)(2,1)S(1)}, bf16[144,128]{1,0:T(8,128)(2,1)S(1)}, u32[]{:S(2)}, u32[]{:S(2)}) collective-permute-start(bf16[144,128]{1,0:T(8,128)(2,1)S(1)} %get-tuple-element.59.own_b), channel_id=1, source_target_pairs={{0,3},{1,0},{2,1},{3,2},{4,7},{5,4},{6,5},{7,6},{8,11},{9,8},{10,9... | collective-permute-start | bytes 110600 | tf_op jit(solution)/shard_map/ppermute | solution.py:351
  144.1 6.5 %collective-permute-start.22 = (bf16[576,128]{1,0:T(8,128)(2,1)S(1)}, bf16[576,128]{1,0:T(8,128)(2,1)S(1)}, u32[]{:S(2)}, u32[]{:S(2)}) collective-permute-start(bf16[576,128]{1,0:T(8,128)(2,1)S(1)} %get-tuple-element.60.own_a), channel_id=1, source_target_pairs={{0,1},{1,2},{2,3},{3,0},{4,5},{5,6},{6,7},{7,4},{8,9},{9,10},{10,1... | collective-permute-start | bytes 442376 | tf_op jit(solution)/shard_map/ppermute | solution.py:351
  145.5 7.6 %collective-permute-start.23 = (bf16[576,128]{1,0:T(8,128)(2,1)S(1)}, bf16[576,128]{1,0:T(8,128)(2,1)S(1)}, u32[]{:S(2)}, u32[]{:S(2)}) collective-permute-start(bf16[576,128]{1,0:T(8,128)(2,1)S(1)} %get-tuple-element.60.own_a), channel_id=1, source_target_pairs={{0,2},{1,3},{2,0},{3,1},{4,6},{5,7},{6,4},{7,5},{8,10},{9,11},{10,... | collective-permute-start | bytes 442376 | tf_op jit(solution)/shard_map/ppermute | solution.py:351
  148.6 4.5 %collective-permute-start.24 = (bf16[576,128]{1,0:T(8,128)(2,1)S(1)}, bf16[576,128]{1,0:T(8,128)(2,1)S(1)}, u32[]{:S(2)}, u32[]{:S(2)}) collective-permute-start(bf16[576,128]{1,0:T(8,128)(2,1)S(1)} %get-tuple-element.60.own_a), channel_id=1, source_target_pairs={{0,3},{1,0},{2,1},{3,2},{4,7},{5,4},{6,5},{7,6},{8,11},{9,8},{10,9... | collective-permute-start | bytes 442376 | tf_op jit(solution)/shard_map/ppermute | solution.py:351
  148.6 6.8 %collective-permute-start.25 = (bf16[576,128]{1,0:T(8,128)(2,1)S(1)}, bf16[576,128]{1,0:T(8,128)(2,1)S(1)}, u32[]{:S(2)}, u32[]{:S(2)}) collective-permute-start(bf16[576,128]{1,0:T(8,128)(2,1)S(1)} %get-tuple-element.61.own_b), channel_id=1, source_target_pairs={{0,4},{1,5},{2,6},{3,7},{4,8},{5,9},{6,10},{7,11},{8,12},{9,13},{1... | collective-permute-start | bytes 442376 | tf_op jit(solution)/shard_map/ppermute | solution.py:356
  148.6 6.8 %collective-permute-start.26 = (bf16[576,128]{1,0:T(8,128)(2,1)S(1)}, bf16[576,128]{1,0:T(8,128)(2,1)S(1)}, u32[]{:S(2)}, u32[]{:S(2)}) collective-permute-start(bf16[576,128]{1,0:T(8,128)(2,1)S(1)} %get-tuple-element.61.own_b), channel_id=1, source_target_pairs={{0,8},{1,9},{2,10},{3,11},{4,12},{5,13},{6,14},{7,15},{8,0},{9,1},... | collective-permute-start | bytes 442376 | tf_op jit(solution)/shard_map/ppermute | solution.py:356
  150.6 5.3 %collective-permute-start.27 = (bf16[576,128]{1,0:T(8,128)(2,1)S(1)}, bf16[576,128]{1,0:T(8,128)(2,1)S(1)}, u32[]{:S(2)}, u32[]{:S(2)}) collective-permute-start(bf16[576,128]{1,0:T(8,128)(2,1)S(1)} %get-tuple-element.61.own_b), channel_id=1, source_target_pairs={{0,12},{1,13},{2,14},{3,15},{4,0},{5,1},{6,2},{7,3},{8,4},{9,5},{1... | collective-permute-start | bytes 442376 | tf_op jit(solution)/shard_map/ppermute | solution.py:356
  156.6 13.7 %collective-permute-start.28 = (bf16[4608,128]{1,0:T(8,128)(2,1)S(1)}, bf16[4608,128]{1,0:T(8,128)(2,1)S(1)}, u32[]{:S(2)}, u32[]{:S(2)}) collective-permute-start(bf16[4608,128]{1,0:T(8,128)(2,1)S(1)} %shard_map.155.mine_ref), channel_id=1, source_target_pairs={{0,16},{16,0},{32,48},{48,32},{64,80},{80,64},{96,112},{112,96},{1... | collective-permute-start | bytes 3538952 | tf_op jit(solution)/shard_map/ppermute | solution.py:366

commit v3 on v2

v3 whole, which is shorter than its diff:
```python
import functools
import math

import jax
import jax.numpy as jnp
from jax import lax
from jax.experimental import pallas as pl
from jax.experimental.pallas import tpu as pltpu
from jax.sharding import PartitionSpec as P

BOTH = ("px", "py")
LANES = 128
PACK, LOCAL, MAIN = 58, 62, 56
BOX, PIECE, SUM, FINISH = 20, 12, 8, 12
VMEM = pl.BlockSpec(memory_space=pltpu.VMEM)
HBM = pl.BlockSpec(memory_space=pltpu.HBM)
SMEM = pl.BlockSpec(memory_space=pltpu.SMEM)
INV_SQRT2 = 1.0 / math.sqrt(2.0)
INV_SQRT_2PI = 1.0 / math.sqrt(2.0 * math.pi)


def mm(a, b, dims=((1,), (0,))):
    return lax.dot_general(a, b, (dims, ((), ())), preferred_element_type=jnp.float32)


def fill_picks(idx_ref, pick_ref):
    rows = pick_ref.shape[1]
    lane = lax.broadcasted_iota(jnp.int32, (LANES, rows), 1)
    for j in range(idx_ref.shape[0]):
        across = jnp.broadcast_to(idx_ref[j : j + 1, :], (LANES, LANES))
        down = across.T
        wide = jnp.concatenate([down] * (rows // LANES), axis=1)
        hit = jnp.where(wide == lane, 1.0, 0.0)
        pick_ref[j * LANES : (j + 1) * LANES, :] = hit.astype(pick_ref.dtype)


def copies(sems, pairs):
    started = [
        pltpu.make_async_copy(src, dst, sems.at[i]) for i, (src, dst) in enumerate(pairs)
    ]
    for copy in started:
        copy.start()
    return started


def pack_kernel(rows_ref, counts_ref, features_hbm, out_hbm, idx_ref, features, picks, out, sems):
    width = features.shape[1]
    (fetch,) = copies(sems, [(features_hbm, features)])
    groups, parts = rows_ref.shape[0], counts_ref.shape[1]
    slots = groups * LANES // parts
    peers = parts // groups
    group = lax.broadcasted_iota(jnp.int32, (groups, parts), 0)
    peer = lax.broadcasted_iota(jnp.int32, (groups, parts), 1)
    counts = jnp.broadcast_to(counts_ref[...].astype(jnp.float32), (groups, parts))
    counts = jnp.where(peer // peers == group, counts, 0.0).astype(jnp.bfloat16)
    down = lax.broadcasted_iota(jnp.int32, (parts, LANES), 0)
    lane = lax.broadcasted_iota(jnp.int32, (parts, LANES), 1)
    expand = jnp.where(down % peers == lane // slots, 1.0, 0.0).astype(jnp.bfloat16)
    limit = mm(counts, expand)
    slot = (lax.broadcasted_iota(jnp.int32, (groups, LANES), 1) % slots).astype(jnp.float32)
    idx_ref[...] = jnp.where(slot < limit, rows_ref[...], -1)
    fill_picks(idx_ref, picks)
    for j in range(idx_ref.shape[0]):
        across = jnp.broadcast_to(idx_ref[j : j + 1, :], (LANES, LANES))
        used = jnp.where(across.T >= 0, 1.0, 0.0)
        out[j * LANES : (j + 1) * LANES, width:] = used.astype(out.dtype)
    fetch.wait()
    step = out.shape[0] // 4
    stores = []
    for k in range(4):
        at = pl.ds(k * step, step)
        out[at, :width] = mm(picks[at, :], features[...]).astype(out.dtype)
        store = pltpu.make_async_copy(out.at[at, :], out_hbm.at[at, :], sems.at[1 + k])
        store.start()
        stores.append(store)
    for store in stores:
        store.wait()


def local_kernel(
    rows_ref,
    cols_ref,
    count_ref,
    idx_ref,
    tiles_hbm,
    features_hbm,
    out_grad_hbm,
    weight_hbm,
    stale_grad_hbm,
    near_hbm,
    far_hbm,
    agg_hbm,
    hidden_grad_hbm,
    grad_out_hbm,
    tiles,
    features,
    out_grad,
    weight,
    stale_grad,
    near32,
    far32,
    near,
    far,
    scatter,
    agg,
    hidden_grad,
    grad_out,
    sems,
):
    tile = tiles.shape[1]
    own = features.shape[0]
    fetches = copies(
        sems,
        [
            (tiles_hbm, tiles),
            (out_grad_hbm, out_grad),
            (weight_hbm, weight),
            (features_hbm, features),
            (stale_grad_hbm, stale_grad),
        ],
    )
    near32[...] = jnp.zeros_like(near32)
    far32[...] = jnp.zeros_like(far32)
    fetches[0].wait()

    @pl.loop(0, count_ref[0])
    def _(t):
        r = pl.multiple_of(rows_ref[t] * tile, tile)
        c = pl.multiple_of(cols_ref[t] * tile, tile)
        value = tiles[t].astype(jnp.float32)

        @pl.when(c < own)
        def _():
            near32[pl.ds(r, tile), pl.ds(c, tile)] += value

        @pl.when(c >= own)
        def _():
            far32[pl.ds(r, tile), pl.ds(pl.multiple_of(c - own, tile), tile)] += value

    near[...] = near32[...].astype(near.dtype)
    far[...] = far32[...].astype(far.dtype)
    saves = copies(sems.at[pl.ds(5, 2)], [(near, near_hbm), (far, far_hbm)])
    fetches[3].wait()
    agg[...] = mm(near[...], features[...])
    saves += copies(sems.at[pl.ds(7, 1)], [(agg, agg_hbm)])
    fetches[1].wait()
    fetches[2].wait()
    down = mm(out_grad[...], weight[...], ((1,), (1,))).astype(jnp.bfloat16)
    remote = mm(far[...], down, ((0,), (0,)))
    grad_out[...] = remote.reshape(grad_out.shape).astype(grad_out.dtype)
    saves += copies(sems.at[pl.ds(8, 1)], [(grad_out, grad_out_hbm)])
    place = lax.broadcasted_iota(jnp.int32, (own, LANES), 0)
    for j in range(idx_ref.shape[0]):
        across = jnp.broadcast_to(idx_ref[j : j + 1, :], (own, LANES))
        hit = jnp.where(across == place, 1.0, 0.0)
        scatter[:, j * LANES : (j + 1) * LANES] = hit.astype(scatter.dtype)
    fetches[4].wait()
    hidden_grad[...] = mm(near[...], down, ((0,), (0,))) + mm(scatter[...], stale_grad[...])
    saves += copies(sems.at[pl.ds(9, 1)], [(hidden_grad, hidden_grad_hbm)])
    for save in saves:
        save.wait()


def main_kernel(
    core_ref,
    arrived_hbm,
    near_hbm,
    far_hbm,
    agg_hbm,
    weight_hbm,
    hidden_grad_hbm,
    stale_hidden_hbm,
    out_grad_hbm,
    hidden_hbm,
    keep_hbm,
    send_hbm,
    arrived,
    near,
    far,
    agg,
    weight,
    hidden_grad,
    stale_hidden,
    out_grad,
    hidden,
    keep,
    send,
    sems,
):
    own, width = agg.shape
    fetches = copies(
        sems,
        [
            (arrived_hbm, arrived),
            (far_hbm, far),
            (agg_hbm, agg),
            (weight_hbm, weight),
            (stale_hidden_hbm, stale_hidden),
            (near_hbm, near),
            (out_grad_hbm, out_grad),
            (hidden_grad_hbm, hidden_grad),
        ],
    )
    for fetch in fetches[:3]:
        fetch.wait()
    agg_one = (agg[...] + mm(far[...], arrived[:, :width])).astype(jnp.bfloat16)
    fetches[3].wait()
    pre = mm(agg_one, weight[...])
    cdf = 0.5 * (1.0 + lax.erf(pre * INV_SQRT2))
    hidden[...] = (pre * cdf).astype(jnp.bfloat16)
    saves = copies(sems.at[pl.ds(8, 1)], [(hidden, hidden_hbm)])
    fetches[4].wait()
    heard = arrived[:, width:].astype(jnp.float32) > 0.5
    for k in range(width // LANES):
        at = slice(k * LANES, (k + 1) * LANES)
        stale = stale_hidden[:, at].astype(jnp.float32)
        stale_hidden[:, at] = jnp.where(heard, stale, 0.0).astype(stale_hidden.dtype)
    fetches[5].wait()
    agg_two = mm(near[...], hidden[...]) + mm(far[...], stale_hidden[...])
    fetches[6].wait()
    part_two = mm(agg_two.astype(jnp.bfloat16), out_grad[...], ((0,), (0,)))
    slope = cdf + pre * (jnp.exp(-0.5 * pre * pre) * INV_SQRT_2PI)
    fetches[7].wait()
    pre_grad = (hidden_grad[...] * slope).astype(jnp.bfloat16)
    part_one = mm(agg_one, pre_grad, ((0,), (0,)))
    first = core_ref[0] == 0
    for k in range(width // LANES):
        at = slice(k * LANES, (k + 1) * LANES)
        one, two = part_one[:, at], part_two[:, at]
        lines = pl.ds(k * width, width)
        keep[lines, :] = jnp.where(first, one, two)
        send[lines, :] = jnp.where(first, two, one).astype(send.dtype)
    saves += copies(sems.at[pl.ds(9, 2)], [(send, send_hbm), (keep, keep_hbm)])
    for save in saves:
        save.wait()


def box_kernel(idx_ref, hidden_hbm, mail_hbm, hidden, picks, box, sems):
    (fetch,) = copies(sems, [(hidden_hbm, hidden)])
    fill_picks(idx_ref, picks)
    fetch.wait()
    parts, blocks = box.shape[0], hidden.shape[1] // LANES
    slots = box.shape[1] // blocks
    picked = mm(picks[...], hidden[...])
    for k in range(blocks):
        block = picked[:, k * LANES : (k + 1) * LANES].reshape(parts, slots, LANES)
        box[:, k * slots : (k + 1) * slots, :] = block.astype(box.dtype)
    (save,) = copies(sems.at[pl.ds(1, 1)], [(box, mail_hbm.at[:, : box.shape[1], :])])
    save.wait()


def piece_kernel(keep_ref, other_ref, _, mail_hbm, pieces, sems):
    parts, size = pieces.shape[0], pieces.shape[1]
    total = keep_ref[...] + other_ref[...].astype(jnp.float32)
    whole = total.shape[0] // size
    rest = total.shape[0] - whole * size
    pieces[:whole] = total[: whole * size].reshape(whole, size, LANES).astype(pieces.dtype)
    pieces[whole:] = jnp.zeros((parts - whole, size, LANES), pieces.dtype)
    if rest:
        pieces[whole, :rest] = total[whole * size :].astype(pieces.dtype)
    start = mail_hbm.shape[1] - size
    (save,) = copies(sems, [(pieces, mail_hbm.at[:, start:, :])])
    save.wait()


def sum_kernel(n_z, n_py, mail_hbm, out_ref, pieces, sems):
    parts, size = pieces.shape[0], pieces.shape[1]
    start = mail_hbm.shape[1] - size
    (fetch,) = copies(sems, [(mail_hbm.at[:, start:, :], pieces)])
    fetch.wait()
    for c in range(2):
        total = None
        for z in range(n_z):
            first = (z * 2 + c) * n_py
            block = pieces[first : first + n_py].astype(jnp.float32).sum(0)
            total = block if total is None else total + block
        rounded = total.astype(out_ref.dtype)
        out_ref[:, c * size : (c + 1) * size, :] = jnp.broadcast_to(
            rounded[None], (out_ref.shape[0], size, LANES)
        )


def finish_kernel(scale, n_py, core_ref, mine_ref, other_ref, one_ref, two_ref):
    size = mine_ref.shape[1] // 2
    width = one_ref.shape[0]
    lines = width * width // LANES

    def fill(sources):
        for q in range(2 * mine_ref.shape[0]):
            row, py = divmod(q, n_py)
            z, c = divmod(row, 2)
            for g, out_ref in enumerate((one_ref, two_ref)):
                line = q * size
                end = min(line + size, lines)
                while line < end:
                    k, r = divmod(line, width)
                    count = min(end - line, width - r)
                    at = g * size + line - q * size
                    value = sources[c][z * n_py + py, at : at + count, :]
                    out_ref[r : r + count, k * LANES : (k + 1) * LANES] = (
                        value.astype(jnp.float32) * scale
                    )
                    line += count

    @pl.when(core_ref[0] == 0)
    def _():
        fill((mine_ref, other_ref))

    @pl.when(core_ref[0] != 0)
    def _():
        fill((other_ref, mine_ref))


def in_vmem(*refs):
    return [pltpu.VMEM(r.shape, r.dtype) for r in refs]


def call(kernel, out_shape, scalars, scratch=(), vmem=None, limit=6, aliases=None, out=None):
    def run(*args):
        n_vmem = len(args) - scalars if vmem is None else vmem
        size = sum(a.size * a.dtype.itemsize for a in (*args, *jax.tree.leaves(out_shape)))
        out_spec = (VMEM if vmem is None else HBM) if out is None else out
        return pl.pallas_call(
            kernel,
            out_shape=out_shape,
            in_specs=[SMEM] * scalars + [VMEM] * n_vmem + [HBM] * (len(args) - scalars - n_vmem),
            out_specs=jax.tree.map(lambda _: out_spec, out_shape) if out is None else out,
            scratch_shapes=scratch,
            input_output_aliases=aliases or {},
            cost_estimate=pl.CostEstimate(flops=0, transcendentals=0, bytes_accessed=size),
            compiler_params=pltpu.CompilerParams(vmem_limit_bytes=limit * 1024 * 1024),
        )(*args)

    return run


def trade(value, groups=None):
    return lax.all_to_all(
        value, BOTH, split_axis=0, concat_axis=0, tiled=True, axis_index_groups=groups
    )


def sibling(value):
    n = lax.axis_size("px")
    return lax.ppermute(value, "px", [(i, i ^ 1) for i in range(n)])


def local(
    features,
    weight_one,
    weight_two,
    tile_values,
    tile_rows,
    tile_cols,
    tile_count,
    send_rows,
    send_count,
    stale_hidden,
    stale_grad,
    out_grad,
):
    bf16, f32 = jnp.bfloat16, jnp.float32
    parts = lax.axis_size(BOTH)
    own, width = features.shape
    slots = send_rows.shape[2]
    boundary = parts * slots
    shape = jax.ShapeDtypeStruct
    slot_ids = jnp.arange(slots, dtype=jnp.int32)
    core = (lax.axis_index("px") % 2).astype(jnp.int32).reshape(1)
    n_z, n_py = lax.axis_size("px") // 2, lax.axis_size("py")

    pack = shape((boundary, width + LANES), bf16)
    square, square32 = shape((own, width), bf16), shape((own, width), f32)
    near, far = shape((own, own), bf16), shape((own, boundary), bf16)
    near32, far32 = shape((own, own), f32), shape((own, boundary), f32)
    slab, slots_in = shape((boundary, width), bf16), shape((parts, slots, width), bf16)
    weight = shape(weight_one.shape, bf16)
    picks = shape((boundary, own), bf16)
    semaphores = lambda count: [pltpu.SemaphoreType.DMA((count,))]
    lines = width * width // LANES
    keep, send = shape((lines, LANES), f32), shape((lines, LANES), bf16)
    groups = boundary // LANES

    outgoing, idx = call(
        pack_kernel,
        (pack, shape((groups, LANES), jnp.int32)),
        0,
        in_vmem(square, picks, pack) + semaphores(5),
        2,
        PACK,
        None,
        (HBM, VMEM),
    )(send_rows.reshape(groups, LANES), send_count, features)
    arrived = trade(outgoing.reshape(parts, slots, -1)).reshape(boundary, -1)

    near_adj, far_adj, agg, hidden_grad, grad_out = call(
        local_kernel,
        (near, far, square32, square32, slots_in),
        3,
        in_vmem(
            tile_values, square, square, weight, slab, near32, far32, near, far, far, square32, square32, slots_in
        )
        + semaphores(10),
        1,
        LOCAL,
    )(tile_rows[0], tile_cols[0], tile_count, idx, tile_values, features, out_grad, weight_two, stale_grad)

    arrived, grad_out = lax.optimization_barrier((arrived, grad_out))
    grads = trade(grad_out)
    hidden, keep, send = call(
        main_kernel,
        (square, keep, send),
        1,
        in_vmem(pack, near, far, square32, weight, square32, slab, square, square, keep, send)
        + semaphores(11),
        0,
        MAIN,
    )(core, arrived, near_adj, far_adj, agg, weight_one, hidden_grad, stale_hidden, out_grad)

    other = sibling(send)
    size = -(-lines // (parts * 8)) * 8
    rows = slots * width // LANES
    mail = call(
        box_kernel,
        shape((parts, rows + size, LANES), bf16),
        0,
        in_vmem(square, picks, shape((parts, rows, LANES), bf16)) + semaphores(2),
        1,
        BOX,
    )(idx, hidden)
    mail = call(
        piece_kernel,
        shape(mail.shape, bf16),
        0,
        in_vmem(shape((parts, size, LANES), bf16)) + semaphores(1),
        2,
        PIECE,
        {2: 0},
    )(keep, other, mail)
    mail, grads = lax.optimization_barrier((mail, grads))
    mail = trade(mail)
    chips = parts // 2
    mine = call(
        functools.partial(sum_kernel, n_z, n_py),
        shape((chips, 2 * size, LANES), bf16),
        0,
        in_vmem(shape((parts, size, LANES), bf16)) + semaphores(1),
        0,
        SUM,
        None,
        VMEM,
    )(mail)
    same_core = [[(2 * z + c) * n_py + i for z in range(n_z) for i in range(n_py)] for c in range(2)]
    mine = trade(mine, same_core)
    next_hidden = mail[:, :rows].reshape(parts, width // LANES, slots, LANES)
    next_hidden = jnp.swapaxes(next_hidden, 1, 2).reshape(boundary, width)
    sent = slot_ids[None, :] < send_count[0][:, None]
    next_grad = jnp.where(sent[:, :, None], grads, jnp.zeros_like(grads)).reshape(boundary, width)
    mine, next_hidden, next_grad = lax.optimization_barrier((mine, next_hidden, next_grad))
    scale = 1.0 / math.sqrt(own * parts)
    one, two = call(
        functools.partial(finish_kernel, scale, n_py),
        (shape((width, width), f32),) * 2,
        1,
        (),
        None,
        FINISH,
    )(core, mine, sibling(mine))

    return next_hidden, next_grad, one, two


def solution(mesh):
    in_specs = (
        P(BOTH, None),
        P(),
        P(),
        P(BOTH, None, None),
        P(BOTH, None),
        P(BOTH, None),
        P(BOTH),
        P(BOTH, None, None),
        P(BOTH, None),
        P(BOTH, None),
        P(BOTH, None),
        P(BOTH, None),
    )
    out_specs = (P(BOTH, None), P(BOTH, None), P(), P())
    return jax.shard_map(local, mesh=mesh, in_specs=in_specs, out_specs=out_specs, check_vma=False)
```

time: 177 us -> 156 us (0.88)
  blocking collectives: 0 us -> 43.7 us
  starting transfers between devices: 67.8 us -> 26.5 us
  waiting for transfers between devices: 59.1 us -> 35.4 us
  local copies, waits for them, and re-layouts: 3.03 us -> 6.81 us
  other arithmetic: 5.83 us -> 3 us
    all_to_all x0 -> x1, blocking collectives: none -> 43.7 us  [trade(): lax.all_to_all(value, BOTH, split_axis=0, concat_axis=0, tiled=True, axis...]
    ppermute x27 -> x0, waiting for transfers between devices: 42.7 us -> none  [the longest x12 33.5 us: along_x(): lax.ppermute(value, 'py', [(i, i & ~3 | i + step & 3) for i in range(n)])]
    ppermute x27 -> x0, starting transfers between devices: 38.9 us -> none  [the longest x12 17.3 us: along_x(): lax.ppermute(value, 'py', [(i, i & ~3 | i + step & 3) for i in range(n)])]
    all_to_all x2 -> x3, waiting for transfers between devices: 14 us -> 32.7 us  [trade(): lax.all_to_all(value, BOTH, split_axis=0, concat_axis=0, tiled=True, axis...]
    ppermute x2, starting transfers between devices: 12.5 us -> 4.07 us  [sibling(): return lax.ppermute(value, 'px', [(i, i ^ 1) for i in range(n)])]
    all_to_all x2 -> x3, starting transfers between devices: 16.3 us -> 22.4 us  [trade(): lax.all_to_all(value, BOTH, split_axis=0, concat_axis=0, tiled=True, axis...]
    unnamed x8 -> x15, local copies, waits for them, and re-layouts: 2.59 us -> 4.88 us
    reshape x0 -> x2, local copies, waits for them, and re-layouts: none -> 1.93 us  [the longest x1 1.24 us: local(): next_hidden = jnp.swapaxes(next_hidden, 1, 2).reshape(boundary, width)]
  transfers between devices with their start and end apart: 31 -> 5, of which waited for: 16 -> 4; matrix products, arithmetic and copies ran while one was open for 0% -> 3% of each run, Pallas kernels for 10% -> 19%
where the time goes in v3:
time: 156 us
  blocking collectives  43.7 us (28%)
  Pallas kernels  39.1 us (25%)
  waiting for transfers between devices  35.4 us (23%)
  starting transfers between devices  26.5 us (17%)
  local copies, waits for them, and re-layouts  6.81 us (4%)
  other arithmetic  3 us (2%)
    all_to_all x1, blocking collectives, trade(): lax.all_to_all(value, BOTH, split_axis=0, concat_axis=0, tiled=True, axis...  43.7 us
    pallas_call x7, Pallas kernels, run(): pl.pallas_call(kernel, out_shape=out_shape, in_specs=[SMEM] * scalars + [...  39.1 us
    all_to_all x3, waiting for transfers between devices, trade(): lax.all_to_all(value, BOTH, split_axis=0, concat_axis=0, tiled=True, axis...  32.7 us
    all_to_all x3, starting transfers between devices, trade(): lax.all_to_all(value, BOTH, split_axis=0, concat_axis=0, tiled=True, axis...  22.4 us
    unnamed x15, local copies, waits for them, and re-layouts  4.88 us
    ppermute x2, starting transfers between devices, sibling(): return lax.ppermute(value, 'px', [(i, i ^ 1) for i in range(n)])  4.07 us
  transfers between devices with their start and end apart: 5, of which 4 were waited for; matrix products, arithmetic and copies ran while one was open for 3% of the time, Pallas kernels for 19%

profile of v3, /device:TPU:1, one launch (start us, length us, event | category | flops | bytes accessed | tf_op | source)
XLA Modules:
  0.0 155.9 jit_solution(3916053173027763817)
XLA Ops:
  0.6 0.8 copy.18
  1.4 0.7 reshape.54.rows_ref
  2.1 4.8 %shard_map.147 = (bf16[1024,896]{1,0:T(8,128)(2,1)}, s32[8,128]{1,0:T(8,128)}) custom-call(s32[8,128]{1,0:T(8,128)} %reshape.54.rows_ref, s32[1,128]{1,0:T(1,128)} %counts_ref.1, bf16[768,768]{1,0:T(8,128)(2,1)} %features_hbm.3), custom_call_target="tpu_custom_call" | custom-call | bytes 3023360 | tf_op jit(solution)/shard_map/pallas_call | solution.py:323
  6.9 11.5 %all-to-all-start = ((bf16[128,8,896]{2,1,0:T(8,128)(2,1)}), bf16[128,8,896]{2,1,0:T(8,128)(2,1)S(1)}, u32[]{:S(2)}, u32[]{:S(2)}) async-start(bf16[128,8,896]{2,1,0:T(8,128)(2,1)} %bitcast.15), calls=%async_computation | async-start | bytes 3670016 | tf_op jit(solution)/shard_map/all_to_all | solution.py:338
  19.0 12.2 %shard_map.148 = (bf16[768,768]{1,0:T(8,128)(2,1)}, bf16[768,1024]{1,0:T(8,128)(2,1)}, f32[768,768]{1,0:T(8,128)}, f32[768,768]{1,0:T(8,128)}, bf16[128,8,768]{2,1,0:T(8,128)(2,1)}) custom-call(s32[32]{0:T(128)} %bitcast.17, s32[32]{0:T(128)} %bitcast.18, s32[1]{0:T(128)S(6)} %copy.20.count_ref, s32[8,128]{1,0:T(8,128)} %get-tuple-element.24.idx_ref, ...), custom_call_target="tpu_custom_call" | custom-call | bytes 15208708 | tf_op jit(solution)/shard_map/pallas_call | solution.py:323
  31.3 14.0 %all-to-all-done = bf16[128,8,896]{2,1,0:T(8,128)(2,1)S(1)} async-done(((bf16[128,8,896]{2,1,0:T(8,128)(2,1)}), bf16[128,8,896]{2,1,0:T(8,128)(2,1)S(1)}, u32[]{:S(2)}, u32[]{:S(2)}) %all-to-all-start) | async-done | bytes 1835040 | tf_op jit(solution)/shard_map/all_to_all | solution.py:338
  45.3 0.0 copy-start.5
  45.3 1.2 copy-done.5
  46.5 5.7 %all-to-all-start.1 = ((bf16[128,8,768]{2,1,0:T(8,128)(2,1)}), bf16[128,8,768]{2,1,0:T(8,128)(2,1)}, u32[]{:S(2)}, u32[]{:S(2)}) async-start(bf16[128,8,768]{2,1,0:T(8,128)(2,1)} %get-tuple-element.34), calls=%async_computation.1 | async-start | bytes 3145728 | tf_op jit(solution)/shard_map/all_to_all | solution.py:338
  52.2 0.0 copy-start.4
  52.2 15.5 %shard_map.149 = (bf16[768,768]{1,0:T(8,128)(2,1)}, f32[4608,128]{1,0:T(8,128)}, bf16[4608,128]{1,0:T(8,128)(2,1)}) custom-call(s32[1]{0:T(128)} %bitcast.core_ref, bf16[1024,896]{1,0:T(8,128)(2,1)} %bitcast.14, bf16[768,768]{1,0:T(8,128)(2,1)} %get-tuple-element.27.near_hbm, bf16[768,1024]{1,0:T(8,128)(2,1)} %get-tuple-element.28.far_hbm, ...), custom_call_target="tpu_custom_call" | custom-call | bytes 17956868 | tf_op jit(solution)/shard_map/pallas_call | solution.py:323
  67.8 1.5 collective-permute-start
  69.3 0.0 copy-done.4
  69.3 0.0 copy-start.3
  69.3 1.3 copy-done.3
  70.6 0.0 copy-start.2
  70.6 2.2 %shard_map.150._ = bf16[128,88,128]{2,1,0:T(8,128)(2,1)S(1)} custom-call(s32[8,128]{1,0:T(8,128)S(1)} %copy-done.4, bf16[768,768]{1,0:T(8,128)(2,1)S(1)} %copy-done.3), custom_call_target="tpu_custom_call" | custom-call | bytes 4067328 | tf_op jit(solution)/shard_map/pallas_call | solution.py:323
  72.8 0.0 collective-permute-done.other_ref
  72.8 0.0 copy-done.2
  72.8 0.4 shard_map.151
  73.2 2.9 %all-to-all-done.1 = bf16[128,8,768]{2,1,0:T(8,128)(2,1)} async-done(((bf16[128,8,768]{2,1,0:T(8,128)(2,1)}), bf16[128,8,768]{2,1,0:T(8,128)(2,1)}, u32[]{:S(2)}, u32[]{:S(2)}) %all-to-all-start.1) | async-done | bytes 1572896 | tf_op jit(solution)/shard_map/all_to_all | solution.py:338
  76.1 43.7 %all_to_all.20.mail_hbm = bf16[128,88,128]{2,1,0:T(8,128)(2,1)S(1)} all-to-all(bf16[128,88,128]{2,1,0:T(8,128)(2,1)S(1)} %shard_map.151), channel_id=1, replica_groups=mesh['px'=8,'py'=16] {'px','py'}, dimensions={0} | all-to-all | bytes 5767168 | tf_op jit(solution)/shard_map/all_to_all | solution.py:338
  119.8 1.4 shard_map.152
  121.2 0.0 copy-start
  121.2 1.6 %copy-done = bf16[128,88,128]{2,1,0:T(8,128)(2,1)} copy-done((bf16[128,88,128]{2,1,0:T(8,128)(2,1)}, bf16[128,88,128]{2,1,0:T(8,128)(2,1)S(1)}, u32[]{:S(2)}) %copy-start) | copy-done | bytes 2883608
  122.8 0.0 copy-start.6
  122.8 5.2 %all-to-all-start.3 = ((bf16[64,80,128]{2,1,0:T(8,128)(2,1)}), bf16[64,80,128]{2,1,0:T(8,128)(2,1)S(1)}, u32[]{:S(2)}, u32[]{:S(2)}) async-start(bf16[64,80,128]{2,1,0:T(8,128)(2,1)} %shard_map.152), calls=%async_computation.3 | async-start | bytes 2621440 | tf_op jit(solution)/shard_map/all_to_all | solution.py:338
  128.0 0.0 copy-done.6
  128.1 0.1 iota_compare_fusion
  128.1 0.0 copy-start.1
  128.2 2.9 %select_bitcast_fusion = bf16[1024,768]{1,0:T(8,128)(2,1)} fusion(bf16[128,8,768]{2,1,0:T(8,128)(2,1)} %all-to-all-done.1, pred[128,8]{1,0:T(8,128)(4,1)S(1)} %iota_compare_fusion), kind=kLoop, calls=%fused_computation.1 | loop fusion | flops 786432 | bytes 3146752 | tf_op jit(solution)/shard_map/reshape | solution.py:458
  131.1 0.0 copy-done.1
  131.1 1.2 slice_bitcast_fusion
  132.3 15.8 %all-to-all-done.3.mine_ref = bf16[64,80,128]{2,1,0:T(8,128)(2,1)S(1)} async-done(((bf16[64,80,128]{2,1,0:T(8,128)(2,1)}), bf16[64,80,128]{2,1,0:T(8,128)(2,1)S(1)}, u32[]{:S(2)}, u32[]{:S(2)}) %all-to-all-start.3) | async-done | bytes 1310752 | tf_op jit(solution)/shard_map/all_to_all | solution.py:338
  148.1 2.5 %collective-permute-start.1 = (bf16[64,80,128]{2,1,0:T(8,128)(2,1)S(1)}, bf16[64,80,128]{2,1,0:T(8,128)(2,1)S(1)}, u32[]{:S(2)}, u32[]{:S(2)}) collective-permute-start(bf16[64,80,128]{2,1,0:T(8,128)(2,1)S(1)} %all-to-all-done.3.mine_ref), channel_id=1, source_target_pairs={{0,16},{16,0},{32,48},{48,32},{64,80},{80,64},{96,112},{112,96},{1... | collective-permute-start | bytes 3932168 | tf_op jit(solution)/shard_map/ppermute | solution.py:345
  150.7 2.7 %collective-permute-done.1.other_ref = bf16[64,80,128]{2,1,0:T(8,128)(2,1)S(1)} collective-permute-done((bf16[64,80,128]{2,1,0:T(8,128)(2,1)S(1)}, bf16[64,80,128]{2,1,0:T(8,128)(2,1)S(1)}, u32[]{:S(2)}, u32[]{:S(2)}) %collective-permute-start.1) | collective-permute-done | bytes 1310752 | tf_op jit(solution)/shard_map/ppermute | solution.py:345
  153.3 2.6 %shard_map.153 = (f32[768,768]{1,0:T(8,128)}, f32[768,768]{1,0:T(8,128)}) custom-call(s32[1]{0:T(128)} %bitcast.core_ref, bf16[64,80,128]{2,1,0:T(8,128)(2,1)S(1)} %all-to-all-done.3.mine_ref, bf16[64,80,128]{2,1,0:T(8,128)(2,1)S(1)} %collective-permute-done.1.other_ref), custom_call_target="tpu_custom_call" | custom-call | bytes 7340036 | tf_op jit(solution)/shard_map/pallas_call | solution.py:323
Async XLA Ops:
  6.9 38.4 %all-to-all-start = ((bf16[128,8,896]{2,1,0:T(8,128)(2,1)}), bf16[128,8,896]{2,1,0:T(8,128)(2,1)S(1)}, u32[]{:S(2)}, u32[]{:S(2)}) async-start(bf16[128,8,896]{2,1,0:T(8,128)(2,1)} %bitcast.15), calls=%async_computation | async-start | bytes 3670016 | tf_op jit(solution)/shard_map/all_to_all | solution.py:338
  45.3 1.2 copy-start.5
  46.5 29.6 %all-to-all-start.1 = ((bf16[128,8,768]{2,1,0:T(8,128)(2,1)}), bf16[128,8,768]{2,1,0:T(8,128)(2,1)}, u32[]{:S(2)}, u32[]{:S(2)}) async-start(bf16[128,8,768]{2,1,0:T(8,128)(2,1)} %get-tuple-element.34), calls=%async_computation.1 | async-start | bytes 3145728 | tf_op jit(solution)/shard_map/all_to_all | solution.py:338
  52.2 17.1 %copy-start.4 = (s32[8,128]{1,0:T(8,128)S(1)}, s32[8,128]{1,0:T(8,128)}, u32[]{:S(2)}) copy-start(s32[8,128]{1,0:T(8,128)} %get-tuple-element.24.idx_ref) | copy-start | bytes 12292
  67.8 5.0 %collective-permute-start = (bf16[4608,128]{1,0:T(8,128)(2,1)}, bf16[4608,128]{1,0:T(8,128)(2,1)S(1)}, u32[]{:S(2)}, u32[]{:S(2)}) collective-permute-start(bf16[4608,128]{1,0:T(8,128)(2,1)} %get-tuple-element.32), channel_id=1, source_target_pairs={{0,16},{16,0},{32,48},{48,32},{64,80},{80,64},{96,112},{112,96},{1... | collective-permute-start | bytes 3538952 | tf_op jit(solution)/shard_map/ppermute | solution.py:345
  69.3 1.3 copy-start.3
  70.6 2.2 %copy-start.2 = (f32[4608,128]{1,0:T(8,128)S(1)}, f32[4608,128]{1,0:T(8,128)}, u32[]{:S(2)}) copy-start(f32[4608,128]{1,0:T(8,128)} %get-tuple-element.31.keep_ref) | copy-start | bytes 7077892
  121.2 1.6 %copy-start = (bf16[128,88,128]{2,1,0:T(8,128)(2,1)}, bf16[128,88,128]{2,1,0:T(8,128)(2,1)S(1)}, u32[]{:S(2)}) copy-start(bf16[128,88,128]{2,1,0:T(8,128)(2,1)S(1)} %all_to_all.20.mail_hbm) | copy-start | bytes 8650756
  122.8 5.2 %copy-start.6 = (s32[1,128]{1,0:T(1,128)S(1)}, s32[1,128]{1,0:T(1,128)}, u32[]{:S(2)}) copy-start(s32[1,128]{1,0:T(1,128)} %counts_ref.1) | copy-start | bytes 1540
  122.8 25.3 %all-to-all-start.3 = ((bf16[64,80,128]{2,1,0:T(8,128)(2,1)}), bf16[64,80,128]{2,1,0:T(8,128)(2,1)S(1)}, u32[]{:S(2)}, u32[]{:S(2)}) async-start(bf16[64,80,128]{2,1,0:T(8,128)(2,1)} %shard_map.152), calls=%async_computation.3 | async-start | bytes 2621440 | tf_op jit(solution)/shard_map/all_to_all | solution.py:338
  128.1 2.9 %copy-start.1 = (bf16[128,88,128]{2,1,0:T(8,128)(2,1)S(1)}, bf16[128,88,128]{2,1,0:T(8,128)(2,1)}, u32[]{:S(2)}) copy-start(bf16[128,88,128]{2,1,0:T(8,128)(2,1)} %copy-done) | copy-start | bytes 8650756
  148.1 5.2 %collective-permute-start.1 = (bf16[64,80,128]{2,1,0:T(8,128)(2,1)S(1)}, bf16[64,80,128]{2,1,0:T(8,128)(2,1)S(1)}, u32[]{:S(2)}, u32[]{:S(2)}) collective-permute-start(bf16[64,80,128]{2,1,0:T(8,128)(2,1)S(1)} %all-to-all-done.3.mine_ref), channel_id=1, source_target_pairs={{0,16},{16,0},{32,48},{48,32},{64,80},{80,64},{96,112},{112,96},{1... | collective-permute-start | bytes 3932168 | tf_op jit(solution)/shard_map/ppermute | solution.py:345

commit v4 on v3

v4 whole, which is shorter than its diff:
```python
import functools
import math

import jax
import jax.numpy as jnp
from jax import lax
from jax.experimental import pallas as pl
from jax.experimental.pallas import tpu as pltpu
from jax.sharding import PartitionSpec as P

BOTH = ("px", "py")
LANES = 128
UNUSED = 2.0**126
PACK, LOCAL, MAIN = 58, 63, 56
BOX, PIECE, SUM, FINISH = 63, 63, 63, 16
VMEM = pl.BlockSpec(memory_space=pltpu.VMEM)
HBM = pl.BlockSpec(memory_space=pltpu.HBM)
SMEM = pl.BlockSpec(memory_space=pltpu.SMEM)
INV_SQRT2 = 1.0 / math.sqrt(2.0)
INV_SQRT_2PI = 1.0 / math.sqrt(2.0 * math.pi)


def mm(a, b, dims=((1,), (0,))):
    return lax.dot_general(a, b, (dims, ((), ())), preferred_element_type=jnp.float32)


def copies(sems, pairs):
    started = [
        pltpu.make_async_copy(src, dst, sems.at[i]) for i, (src, dst) in enumerate(pairs)
    ]
    for copy in started:
        copy.start()
    return started


def pack_kernel(
    rows_ref, counts_ref, features_hbm, out_hbm, picks_hbm, features, listed, wanted, picks, out, sems
):
    f32, bf16 = jnp.float32, jnp.bfloat16
    (fetch,) = copies(sems, [(features_hbm, features)])
    parts, slots = rows_ref.shape[1:]
    boundary, own = picks.shape
    counts = jnp.broadcast_to(counts_ref[...], (LANES, parts)).T
    listed[...] = jnp.zeros_like(listed)
    listed[:, :slots] = rows_ref[0] + 1
    lane = lax.broadcasted_iota(jnp.int32, (parts, LANES), 1)
    value = jnp.where(lane < counts, listed[...], 0)
    step = boundary // 4
    slot = lax.broadcasted_iota(jnp.int32, (step, LANES), 0)
    lane = lax.broadcasted_iota(jnp.int32, (step, LANES), 1)
    mine = lane == slot % slots
    ones = jnp.ones((LANES, LANES), bf16)
    across = lax.broadcasted_iota(jnp.int32, (step, own), 1).astype(f32)
    saves = []
    for k in range(4):
        at = pl.ds(k * step, step)
        peer = jnp.where(lane == slot // slots + k * (step // slots), 1.0, 0.0).astype(bf16)
        index = jnp.full((step, LANES), -1.0, f32)
        for part, weight in ((value >> 5, 32.0), (value & 31, 1.0)):
            spread = mm(peer, part.astype(f32).astype(bf16))
            index += weight * mm(jnp.where(mine, spread, 0.0).astype(bf16), ones)
        wanted[at, :] = index
        wide = jnp.concatenate([index] * (own // LANES), axis=1)
        picks[at, :] = jnp.where(wide == across, 1.0, 0.0).astype(bf16)
        saves += copies(sems.at[pl.ds(1 + k, 1)], [(picks.at[at, :], picks_hbm.at[at, :])])
    fetch.wait()
    for k in range(4):
        at = pl.ds(k * step, step)
        row = mm(picks[at, :], features[...])
        unused = wanted[at, :] < 0.0
        for j in range(own // LANES):
            block = slice(j * LANES, (j + 1) * LANES)
            out[at, block] = jnp.where(unused, UNUSED, row[:, block]).astype(bf16)
        saves += copies(sems.at[pl.ds(5 + k, 1)], [(out.at[at, :], out_hbm.at[at, :])])
    for save in saves:
        save.wait()


def local_kernel(
    rows_ref,
    cols_ref,
    count_ref,
    tiles_hbm,
    features_hbm,
    out_grad_hbm,
    weight_hbm,
    stale_grad_hbm,
    picks_hbm,
    near_hbm,
    far_hbm,
    agg_hbm,
    hidden_grad_hbm,
    grad_out_hbm,
    tiles,
    features,
    out_grad,
    weight,
    stale_grad,
    near32,
    far32,
    near,
    far,
    picks,
    agg,
    hidden_grad,
    grad_out,
    sems,
):
    tile = tiles.shape[1]
    own = features.shape[0]
    fetches = copies(
        sems,
        [
            (tiles_hbm, tiles),
            (out_grad_hbm, out_grad),
            (weight_hbm, weight),
            (features_hbm, features),
            (stale_grad_hbm, stale_grad),
            (picks_hbm, picks),
        ],
    )
    near32[...] = jnp.zeros_like(near32)
    far32[...] = jnp.zeros_like(far32)
    fetches[0].wait()

    @pl.loop(0, count_ref[0])
    def _(t):
        r = pl.multiple_of(rows_ref[t] * tile, tile)
        c = pl.multiple_of(cols_ref[t] * tile, tile)
        value = tiles[t].astype(jnp.float32)

        @pl.when(c < own)
        def _():
            near32[pl.ds(r, tile), pl.ds(c, tile)] += value

        @pl.when(c >= own)
        def _():
            far32[pl.ds(r, tile), pl.ds(pl.multiple_of(c - own, tile), tile)] += value

    near[...] = near32[...].astype(near.dtype)
    far[...] = far32[...].astype(far.dtype)
    saves = copies(sems.at[pl.ds(6, 2)], [(near, near_hbm), (far, far_hbm)])
    fetches[3].wait()
    agg[...] = mm(near[...], features[...])
    saves += copies(sems.at[pl.ds(8, 1)], [(agg, agg_hbm)])
    fetches[1].wait()
    fetches[2].wait()
    down = mm(out_grad[...], weight[...], ((1,), (1,))).astype(jnp.bfloat16)
    remote = mm(far[...], down, ((0,), (0,)))
    grad_out[...] = remote.reshape(grad_out.shape).astype(grad_out.dtype)
    saves += copies(sems.at[pl.ds(9, 1)], [(grad_out, grad_out_hbm)])
    fetches[4].wait()
    fetches[5].wait()
    hidden_grad[...] = mm(near[...], down, ((0,), (0,))) + mm(
        picks[...], stale_grad[...], ((0,), (0,))
    )
    saves += copies(sems.at[pl.ds(10, 1)], [(hidden_grad, hidden_grad_hbm)])
    for save in saves:
        save.wait()


def main_kernel(
    core_ref,
    arrived_hbm,
    near_hbm,
    far_hbm,
    agg_hbm,
    weight_hbm,
    hidden_grad_hbm,
    stale_hidden_hbm,
    out_grad_hbm,
    hidden_hbm,
    keep_hbm,
    send_hbm,
    arrived,
    near,
    far,
    agg,
    weight,
    hidden_grad,
    stale_hidden,
    out_grad,
    hidden,
    keep,
    send,
    first_agg,
    pre_grad,
    sems,
):
    own, width = agg.shape
    step = 256
    blocks = own // step
    loads = [(arrived_hbm, arrived)]
    for i in range(blocks):
        at = pl.ds(i * step, step)
        loads += [(far_hbm.at[at, :], far.at[at, :]), (agg_hbm.at[at, :], agg.at[at, :])]
        if i == 0:
            loads += [(weight_hbm, weight)]
    loads += [
        (stale_hidden_hbm, stale_hidden),
        (hidden_grad_hbm, hidden_grad),
        (near_hbm, near),
        (out_grad_hbm, out_grad),
    ]
    fetches = copies(sems, loads)
    n = len(fetches)
    fetches[0].wait()
    fetches[n - 4].wait()
    for k in range(width // LANES):
        at = slice(k * LANES, (k + 1) * LANES)
        came = arrived[:, at].astype(jnp.float32)
        heard = came != UNUSED
        arrived[:, at] = jnp.where(heard, came, 0.0).astype(arrived.dtype)
        stale = stale_hidden[:, at].astype(jnp.float32)
        stale_hidden[:, at] = jnp.where(heard, stale, 0.0).astype(stale_hidden.dtype)
    for i in range(blocks):
        at = pl.ds(i * step, step)
        for fetch in fetches[1:4] if i == 0 else fetches[2 + 2 * i : 4 + 2 * i]:
            fetch.wait()
        agg_one = (agg[at, :] + mm(far[at, :], arrived[...])).astype(jnp.bfloat16)
        first_agg[at, :] = agg_one
        pre = mm(agg_one, weight[...])
        cdf = 0.5 * (1.0 + lax.erf(pre * INV_SQRT2))
        hidden[at, :] = (pre * cdf).astype(jnp.bfloat16)
        slope = cdf + pre * (jnp.exp(-0.5 * pre * pre) * INV_SQRT_2PI)
        if i == 0:
            fetches[n - 3].wait()
        pre_grad[at, :] = (hidden_grad[at, :] * slope).astype(jnp.bfloat16)
    saves = copies(sems.at[pl.ds(n, 1)], [(hidden, hidden_hbm)])
    fetches[n - 2].wait()
    agg_two = (mm(far[...], stale_hidden[...]) + mm(near[...], hidden[...])).astype(jnp.bfloat16)
    fetches[n - 1].wait()
    part_two = mm(agg_two, out_grad[...], ((0,), (0,)))
    part_one = mm(first_agg[...], pre_grad[...], ((0,), (0,)))
    first = core_ref[0] == 0
    for k in range(width // LANES):
        at = slice(k * LANES, (k + 1) * LANES)
        one, two = part_one[:, at], part_two[:, at]
        rows = pl.ds(k * width, width)
        keep[rows, :] = jnp.where(first, one, two)
        send[rows, :] = jnp.where(first, two, one).astype(send.dtype)
        saves += copies(
            sems.at[pl.ds(n + 1 + 2 * k, 2)],
            [(send.at[rows, :], send_hbm.at[rows, :]), (keep.at[rows, :], keep_hbm.at[rows, :])],
        )
    for save in saves:
        save.wait()


def box_kernel(picks_hbm, hidden_hbm, mail_hbm, hidden, picks, box, sems):
    for fetch in copies(sems, [(hidden_hbm, hidden), (picks_hbm, picks)]):
        fetch.wait()
    parts, blocks = box.shape[0], hidden.shape[1] // LANES
    slots = box.shape[1] // blocks
    picked = mm(picks[...], hidden[...])
    for k in range(blocks):
        block = picked[:, k * LANES : (k + 1) * LANES].reshape(parts, slots, LANES)
        box[:, k * slots : (k + 1) * slots, :] = block.astype(box.dtype)
    (save,) = copies(sems.at[pl.ds(2, 1)], [(box, mail_hbm.at[:, : box.shape[1], :])])
    save.wait()


def piece_kernel(keep_ref, other_ref, _, mail_hbm, pieces, sems):
    parts, size = pieces.shape[0], pieces.shape[1]
    total = keep_ref[...] + other_ref[...].astype(jnp.float32)
    whole = total.shape[0] // size
    rest = total.shape[0] - whole * size
    pieces[:whole] = total[: whole * size].reshape(whole, size, LANES).astype(pieces.dtype)
    pieces[whole:] = jnp.zeros((parts - whole, size, LANES), pieces.dtype)
    if rest:
        pieces[whole, :rest] = total[whole * size :].astype(pieces.dtype)
    start = mail_hbm.shape[1] - size
    (save,) = copies(sems, [(pieces, mail_hbm.at[:, start:, :])])
    save.wait()


def sum_kernel(n_z, n_py, mail_hbm, out_ref, pieces, sems):
    parts, size = pieces.shape[0], pieces.shape[1]
    start = mail_hbm.shape[1] - size
    (fetch,) = copies(sems, [(mail_hbm.at[:, start:, :], pieces)])
    fetch.wait()
    for c in range(2):
        total = None
        for z in range(n_z):
            first = (z * 2 + c) * n_py
            block = pieces[first : first + n_py].astype(jnp.float32).sum(0)
            total = block if total is None else total + block
        rounded = total.astype(out_ref.dtype)
        out_ref[:, c * size : (c + 1) * size, :] = jnp.broadcast_to(
            rounded[None], (out_ref.shape[0], size, LANES)
        )


def finish_kernel(scale, n_py, core_ref, mine_ref, other_ref, one_hbm, two_hbm, one, two, sems):
    size = mine_ref.shape[1] // 2
    width = one.shape[0]
    lines = width * width // LANES

    def fill(sources):
        saves = []
        for q in range(2 * mine_ref.shape[0]):
            row, py = divmod(q, n_py)
            z, c = divmod(row, 2)
            line = q * size
            end = min(line + size, lines)
            while line < end:
                k, r = divmod(line, width)
                block = slice(k * LANES, (k + 1) * LANES)
                count = min(end - line, width - r)
                for g, out in enumerate((one, two)):
                    at = g * size + line - q * size
                    value = sources[c][z * n_py + py, at : at + count, :]
                    out[r : r + count, block] = value.astype(jnp.float32) * scale
                line += count
                if r + count == width:
                    saves += copies(
                        sems.at[pl.ds(2 * k, 2)],
                        [(one.at[:, block], one_hbm.at[:, block]), (two.at[:, block], two_hbm.at[:, block])],
                    )
        for save in saves:
            save.wait()

    @pl.when(core_ref[0] == 0)
    def _():
        fill((mine_ref, other_ref))

    @pl.when(core_ref[0] != 0)
    def _():
        fill((other_ref, mine_ref))


def in_vmem(*refs):
    return [pltpu.VMEM(r.shape, r.dtype) for r in refs]


def call(kernel, out_shape, scalars, scratch=(), vmem=None, limit=6, aliases=None, out=None):
    def run(*args):
        n_vmem = len(args) - scalars if vmem is None else vmem
        size = sum(a.size * a.dtype.itemsize for a in (*args, *jax.tree.leaves(out_shape)))
        out_spec = (VMEM if vmem is None else HBM) if out is None else out
        return pl.pallas_call(
            kernel,
            out_shape=out_shape,
            in_specs=[SMEM] * scalars + [VMEM] * n_vmem + [HBM] * (len(args) - scalars - n_vmem),
            out_specs=jax.tree.map(lambda _: out_spec, out_shape),
            scratch_shapes=scratch,
            input_output_aliases=aliases or {},
            cost_estimate=pl.CostEstimate(flops=0, transcendentals=0, bytes_accessed=size),
            compiler_params=pltpu.CompilerParams(vmem_limit_bytes=limit * 1024 * 1024),
        )(*args)

    return run


def trade(value, groups=None):
    return lax.all_to_all(
        value, BOTH, split_axis=0, concat_axis=0, tiled=True, axis_index_groups=groups
    )


def sibling(value):
    n = lax.axis_size("px")
    return lax.ppermute(value, "px", [(i, i ^ 1) for i in range(n)])


def local(
    features,
    weight_one,
    weight_two,
    tile_values,
    tile_rows,
    tile_cols,
    tile_count,
    send_rows,
    send_count,
    stale_hidden,
    stale_grad,
    out_grad,
):
    bf16, f32 = jnp.bfloat16, jnp.float32
    parts = lax.axis_size(BOTH)
    own, width = features.shape
    slots = send_rows.shape[2]
    boundary = parts * slots
    shape = jax.ShapeDtypeStruct
    slot_ids = jnp.arange(slots, dtype=jnp.int32)
    core = (lax.axis_index("px") % 2).astype(jnp.int32).reshape(1)
    n_z, n_py = lax.axis_size("px") // 2, lax.axis_size("py")

    square, square32 = shape((own, width), bf16), shape((own, width), f32)
    near, far = shape((own, own), bf16), shape((own, boundary), bf16)
    near32, far32 = shape((own, own), f32), shape((own, boundary), f32)
    slab, slots_in = shape((boundary, width), bf16), shape((parts, slots, width), bf16)
    weight = shape(weight_one.shape, bf16)
    picks = shape((boundary, own), bf16)
    semaphores = lambda count: [pltpu.SemaphoreType.DMA((count,))]
    lines = width * width // LANES
    keep, send = shape((lines, LANES), f32), shape((lines, LANES), bf16)

    outgoing, picked = call(
        pack_kernel,
        (slab, picks),
        0,
        in_vmem(
            square, shape((parts, LANES), jnp.int32), shape((boundary, LANES), f32), picks, slab
        )
        + semaphores(9),
        2,
        PACK,
    )(send_rows, send_count, features)
    arrived = trade(outgoing.reshape(parts, slots, -1)).reshape(boundary, -1)

    near_adj, far_adj, agg, hidden_grad, grad_out = call(
        local_kernel,
        (near, far, square32, square32, slots_in),
        3,
        in_vmem(
            tile_values, square, square, weight, slab, near32, far32, near, far, picks, square32, square32, slots_in
        )
        + semaphores(11),
        0,
        LOCAL,
    )(tile_rows[0], tile_cols[0], tile_count, tile_values, features, out_grad, weight_two, stale_grad, picked)

    arrived, grad_out = lax.optimization_barrier((arrived, grad_out))
    grads = trade(grad_out)
    hidden, keep, send = call(
        main_kernel,
        (square, keep, send),
        1,
        in_vmem(
            slab, near, far, square32, weight, square32, slab, square, square, keep, send, square, square
        )
        + semaphores(32),
        0,
        MAIN,
    )(core, arrived, near_adj, far_adj, agg, weight_one, hidden_grad, stale_hidden, out_grad)

    other = sibling(send)
    size = -(-lines // (parts * 8)) * 8
    rows = slots * width // LANES
    mail = call(
        box_kernel,
        shape((parts, rows + size, LANES), bf16),
        0,
        in_vmem(square, picks, shape((parts, rows, LANES), bf16)) + semaphores(3),
        0,
        BOX,
    )(picked, hidden)
    mail = call(
        piece_kernel,
        shape(mail.shape, bf16),
        0,
        in_vmem(shape((parts, size, LANES), bf16)) + semaphores(1),
        2,
        PIECE,
        {2: 0},
    )(keep, other, mail)
    mail, grads = lax.optimization_barrier((mail, grads))
    mail = trade(mail)
    chips = parts // 2
    mine = call(
        functools.partial(sum_kernel, n_z, n_py),
        shape((chips, 2 * size, LANES), bf16),
        0,
        in_vmem(shape((parts, size, LANES), bf16)) + semaphores(1),
        0,
        SUM,
        None,
        VMEM,
    )(mail)
    same_core = [[(2 * z + c) * n_py + i for z in range(n_z) for i in range(n_py)] for c in range(2)]
    mine = trade(mine, same_core)
    next_hidden = mail[:, :rows].reshape(parts, width // LANES, slots, LANES)
    next_hidden = jnp.swapaxes(next_hidden, 1, 2).reshape(boundary, width)
    sent = slot_ids[None, :] < send_count[0][:, None]
    next_grad = jnp.where(sent[:, :, None], grads, jnp.zeros_like(grads)).reshape(boundary, width)
    mine, next_hidden, next_grad = lax.optimization_barrier((mine, next_hidden, next_grad))
    scale = 1.0 / math.sqrt(own * parts)
    one, two = call(
        functools.partial(finish_kernel, scale, n_py),
        (shape((width, width), f32),) * 2,
        1,
        in_vmem(*(shape((width, width), f32),) * 2) + semaphores(2 * (width // LANES)),
        None,
        FINISH,
        None,
        HBM,
    )(core, mine, sibling(mine))

    return next_hidden, next_grad, one, two


def solution(mesh):
    in_specs = (
        P(BOTH, None),
        P(),
        P(),
        P(BOTH, None, None),
        P(BOTH, None),
        P(BOTH, None),
        P(BOTH),
        P(BOTH, None, None),
        P(BOTH, None),
        P(BOTH, None),
        P(BOTH, None),
        P(BOTH, None),
    )
    out_specs = (P(BOTH, None), P(BOTH, None), P(), P())
    return jax.shard_map(local, mesh=mesh, in_specs=in_specs, out_specs=out_specs, check_vma=False)
```

time: 156 us -> 156 us (level)
  waiting for transfers between devices: 35.4 us -> 30 us
  Pallas kernels: 39.1 us -> 43.9 us
  local copies, waits for them, and re-layouts: 6.81 us -> 2.67 us
  blocking collectives: 43.7 us -> 46.9 us
    all_to_all x3, waiting for transfers between devices: 32.7 us -> 27.3 us  [trade(): lax.all_to_all(value, BOTH, split_axis=0, concat_axis=0, tiled=True, axis...]
    pallas_call x7, Pallas kernels: 39.1 us -> 43.9 us  [run(): pl.pallas_call(kernel, out_shape=out_shape, in_specs=[SMEM] * scalars + [...]
    unnamed x15 -> x5, local copies, waits for them, and re-layouts: 4.88 us -> 1.43 us
    all_to_all x1, blocking collectives: 43.7 us -> 46.9 us  [trade(): lax.all_to_all(value, BOTH, split_axis=0, concat_axis=0, tiled=True, axis...]
  transfers between devices with their start and end apart: 5 -> 5, of which waited for: 4 -> 3; matrix products, arithmetic and copies ran while one was open for 3% -> 3% of each run, Pallas kernels for 19% -> 22%
where the time goes in v4:
time: 156 us; the launch traced here: 155 us
  blocking collectives  46.9 us (30%)
  Pallas kernels  43.9 us (28%)
  waiting for transfers between devices  30 us (19%)
  starting transfers between devices  26.9 us (17%)
  other arithmetic  3 us (2%)
  local copies, waits for them, and re-layouts  2.67 us (2%)
  between operations  1.57 us (1%)
    all_to_all x1, blocking collectives, trade(): lax.all_to_all(value, BOTH, split_axis=0, concat_axis=0, tiled=True, axis...  46.9 us
    pallas_call x7, Pallas kernels, run(): pl.pallas_call(kernel, out_shape=out_shape, in_specs=[SMEM] * scalars + [...  43.9 us
    all_to_all x3, waiting for transfers between devices, trade(): lax.all_to_all(value, BOTH, split_axis=0, concat_axis=0, tiled=True, axis...  27.3 us
    all_to_all x3, starting transfers between devices, trade(): lax.all_to_all(value, BOTH, split_axis=0, concat_axis=0, tiled=True, axis...  22.9 us
    ppermute x2, starting transfers between devices, sibling(): return lax.ppermute(value, 'px', [(i, i ^ 1) for i in range(n)])  4.07 us
  transfers between devices with their start and end apart: 5, of which 3 were waited for; matrix products, arithmetic and copies ran while one was open for 3% of the time, Pallas kernels for 22%

profile of v4, /device:TPU:1, one launch (start us, length us, event | category | flops | bytes accessed | tf_op | source)
XLA Modules:
  0.0 154.9 jit_solution(923636179928055302)
XLA Ops:
  0.6 1.4 copy.17.rows_ref
  2.0 4.4 %shard_map.147 = (bf16[1024,768]{1,0:T(8,128)(2,1)}, bf16[1024,768]{1,0:T(8,128)(2,1)}) custom-call(s32[1,128,8]{2,1,0:T(8,128)} %copy.17.rows_ref, s32[1,128]{1,0:T(1,128)} %counts_ref.1, bf16[768,768]{1,0:T(8,128)(2,1)} %features_hbm.3), custom_call_target="tpu_custom_call" | custom-call | bytes 4329984 | tf_op jit(solution)/shard_map/pallas_call | solution.py:341
  6.4 11.9 %all-to-all-start = ((bf16[128,8,768]{2,1,0:T(8,128)(2,1)}), bf16[128,8,768]{2,1,0:T(8,128)(2,1)}, u32[]{:S(2)}, u32[]{:S(2)}) async-start(bf16[128,8,768]{2,1,0:T(8,128)(2,1)} %bitcast.14), calls=%async_computation | async-start | bytes 3145728 | tf_op jit(solution)/shard_map/all_to_all | solution.py:356
  19.0 11.6 %shard_map.148 = (bf16[768,768]{1,0:T(8,128)(2,1)}, bf16[768,1024]{1,0:T(8,128)(2,1)}, f32[768,768]{1,0:T(8,128)}, f32[768,768]{1,0:T(8,128)}, bf16[128,8,768]{2,1,0:T(8,128)(2,1)}) custom-call(s32[32]{0:T(128)} %bitcast.16, s32[32]{0:T(128)} %bitcast.17, s32[1]{0:T(128)S(6)} %copy.19.count_ref, bf16[32,128,128]{2,1,0:T(8,128)(2,1)} %tiles_hbm.1, ...), custom_call_target="tpu_custom_call" | custom-call | bytes 16777476 | tf_op jit(solution)/shard_map/pallas_call | solution.py:341
  30.6 11.5 %all-to-all-done = bf16[128,8,768]{2,1,0:T(8,128)(2,1)} async-done(((bf16[128,8,768]{2,1,0:T(8,128)(2,1)}), bf16[128,8,768]{2,1,0:T(8,128)(2,1)}, u32[]{:S(2)}, u32[]{:S(2)}) %all-to-all-start) | async-done | bytes 1572896 | tf_op jit(solution)/shard_map/all_to_all | solution.py:356
  42.1 5.9 %all-to-all-start.1 = ((bf16[128,8,768]{2,1,0:T(8,128)(2,1)}), bf16[128,8,768]{2,1,0:T(8,128)(2,1)}, u32[]{:S(2)}, u32[]{:S(2)}) async-start(bf16[128,8,768]{2,1,0:T(8,128)(2,1)} %get-tuple-element.34), calls=%async_computation.1 | async-start | bytes 3145728 | tf_op jit(solution)/shard_map/all_to_all | solution.py:356
  48.0 15.2 %shard_map.149 = (bf16[768,768]{1,0:T(8,128)(2,1)}, f32[4608,128]{1,0:T(8,128)}, bf16[4608,128]{1,0:T(8,128)(2,1)}) custom-call(s32[1]{0:T(128)} %bitcast.core_ref, bf16[1024,768]{1,0:T(8,128)(2,1)} %bitcast.2.arrived_hbm, bf16[768,768]{1,0:T(8,128)(2,1)} %get-tuple-element.27.near_hbm, bf16[768,1024]{1,0:T(8,128)(2,1)} %get-tuple-element.28.far_hbm, ...), custom_call_target="tpu_custom_call" | custom-call | bytes 17694724 | tf_op jit(solution)/shard_map/pallas_call | solution.py:341
  63.2 1.5 collective-permute-start
  64.8 4.4 %shard_map.150._ = bf16[128,88,128]{2,1,0:T(8,128)(2,1)} custom-call(bf16[1024,768]{1,0:T(8,128)(2,1)} %get-tuple-element.24.picks_hbm, bf16[768,768]{1,0:T(8,128)(2,1)} %get-tuple-element.33.hidden_hbm), custom_call_target="tpu_custom_call" | custom-call | bytes 5636096 | tf_op jit(solution)/shard_map/pallas_call | solution.py:341
  69.2 0.0 collective-permute-done.other_ref
  69.2 3.3 %shard_map.151 = bf16[128,88,128]{2,1,0:T(8,128)(2,1)} custom-call(f32[4608,128]{1,0:T(8,128)} %get-tuple-element.31.keep_ref, bf16[4608,128]{1,0:T(8,128)(2,1)} %collective-permute-done.other_ref, bf16[128,88,128]{2,1,0:T(8,128)(2,1)} %shard_map.150._), custom_call_target="tpu_custom_call", output_to_operand_aliasing={{}: (2, {})} | custom-call | bytes 9306112 | tf_op jit(solution)/shard_map/pallas_call | solution.py:341
  72.5 0.0 all-to-all-done.1
  72.6 46.9 %all_to_all.20.mail_hbm = bf16[128,88,128]{2,1,0:T(8,128)(2,1)} all-to-all(bf16[128,88,128]{2,1,0:T(8,128)(2,1)} %shard_map.151), channel_id=1, replica_groups=mesh['px'=8,'py'=16] {'px','py'}, dimensions={0} | all-to-all | bytes 5767168 | tf_op jit(solution)/shard_map/all_to_all | solution.py:356
  119.4 2.6 %shard_map.152 = bf16[64,80,128]{2,1,0:T(8,128)(2,1)} custom-call(bf16[128,88,128]{2,1,0:T(8,128)(2,1)} %all_to_all.20.mail_hbm), custom_call_target="tpu_custom_call" | custom-call | bytes 4194304 | tf_op jit(solution)/shard_map/pallas_call | solution.py:341
  122.1 0.0 copy-start.1
  122.1 5.1 %all-to-all-start.3 = ((bf16[64,80,128]{2,1,0:T(8,128)(2,1)}), bf16[64,80,128]{2,1,0:T(8,128)(2,1)S(1)}, u32[]{:S(2)}, u32[]{:S(2)}) async-start(bf16[64,80,128]{2,1,0:T(8,128)(2,1)} %shard_map.152), calls=%async_computation.3 | async-start | bytes 2621440 | tf_op jit(solution)/shard_map/all_to_all | solution.py:356
  127.2 0.0 copy-done.1
  127.2 0.1 iota_compare_fusion
  127.3 0.0 copy-start
  127.3 2.9 %select_bitcast_fusion = bf16[1024,768]{1,0:T(8,128)(2,1)} fusion(bf16[128,8,768]{2,1,0:T(8,128)(2,1)} %all-to-all-done.1, pred[128,8]{1,0:T(8,128)(4,1)S(1)} %iota_compare_fusion), kind=kLoop, calls=%fused_computation.1 | loop fusion | flops 786432 | bytes 3146752 | tf_op jit(solution)/shard_map/reshape | solution.py:477
  130.2 0.0 copy-done
  130.2 1.2 slice_bitcast_fusion
  131.5 15.8 %all-to-all-done.3.mine_ref = bf16[64,80,128]{2,1,0:T(8,128)(2,1)S(1)} async-done(((bf16[64,80,128]{2,1,0:T(8,128)(2,1)}), bf16[64,80,128]{2,1,0:T(8,128)(2,1)S(1)}, u32[]{:S(2)}, u32[]{:S(2)}) %all-to-all-start.3) | async-done | bytes 1310752 | tf_op jit(solution)/shard_map/all_to_all | solution.py:356
  147.3 2.5 %collective-permute-start.1 = (bf16[64,80,128]{2,1,0:T(8,128)(2,1)S(1)}, bf16[64,80,128]{2,1,0:T(8,128)(2,1)S(1)}, u32[]{:S(2)}, u32[]{:S(2)}) collective-permute-start(bf16[64,80,128]{2,1,0:T(8,128)(2,1)S(1)} %all-to-all-done.3.mine_ref), channel_id=1, source_target_pairs={{0,16},{16,0},{32,48},{48,32},{64,80},{80,64},{96,112},{112,96},{1... | collective-permute-start | bytes 3932168 | tf_op jit(solution)/shard_map/ppermute | solution.py:363
  149.8 2.7 %collective-permute-done.1.other_ref = bf16[64,80,128]{2,1,0:T(8,128)(2,1)S(1)} collective-permute-done((bf16[64,80,128]{2,1,0:T(8,128)(2,1)S(1)}, bf16[64,80,128]{2,1,0:T(8,128)(2,1)S(1)}, u32[]{:S(2)}, u32[]{:S(2)}) %collective-permute-start.1) | collective-permute-done | bytes 1310752 | tf_op jit(solution)/shard_map/ppermute | solution.py:363
  152.5 2.3 %shard_map.153 = (f32[768,768]{1,0:T(8,128)}, f32[768,768]{1,0:T(8,128)}) custom-call(s32[1]{0:T(128)} %bitcast.core_ref, bf16[64,80,128]{2,1,0:T(8,128)(2,1)S(1)} %all-to-all-done.3.mine_ref, bf16[64,80,128]{2,1,0:T(8,128)(2,1)S(1)} %collective-permute-done.1.other_ref), custom_call_target="tpu_custom_call" | custom-call | bytes 7340036 | tf_op jit(solution)/shard_map/pallas_call | solution.py:341
Async XLA Ops:
  6.4 35.7 %all-to-all-start = ((bf16[128,8,768]{2,1,0:T(8,128)(2,1)}), bf16[128,8,768]{2,1,0:T(8,128)(2,1)}, u32[]{:S(2)}, u32[]{:S(2)}) async-start(bf16[128,8,768]{2,1,0:T(8,128)(2,1)} %bitcast.14), calls=%async_computation | async-start | bytes 3145728 | tf_op jit(solution)/shard_map/all_to_all | solution.py:356
  42.1 30.4 %all-to-all-start.1 = ((bf16[128,8,768]{2,1,0:T(8,128)(2,1)}), bf16[128,8,768]{2,1,0:T(8,128)(2,1)}, u32[]{:S(2)}, u32[]{:S(2)}) async-start(bf16[128,8,768]{2,1,0:T(8,128)(2,1)} %get-tuple-element.34), calls=%async_computation.1 | async-start | bytes 3145728 | tf_op jit(solution)/shard_map/all_to_all | solution.py:356
  63.2 5.9 %collective-permute-start = (bf16[4608,128]{1,0:T(8,128)(2,1)}, bf16[4608,128]{1,0:T(8,128)(2,1)}, u32[]{:S(2)}, u32[]{:S(2)}) collective-permute-start(bf16[4608,128]{1,0:T(8,128)(2,1)} %get-tuple-element.32), channel_id=1, source_target_pairs={{0,16},{16,0},{32,48},{48,32},{64,80},{80,64},{96,112},{112,96},{1... | collective-permute-start | bytes 3538952 | tf_op jit(solution)/shard_map/ppermute | solution.py:363
  122.1 5.1 %copy-start.1 = (s32[1,128]{1,0:T(1,128)S(1)}, s32[1,128]{1,0:T(1,128)}, u32[]{:S(2)}) copy-start(s32[1,128]{1,0:T(1,128)} %counts_ref.1) | copy-start | bytes 1540
  122.1 25.2 %all-to-all-start.3 = ((bf16[64,80,128]{2,1,0:T(8,128)(2,1)}), bf16[64,80,128]{2,1,0:T(8,128)(2,1)S(1)}, u32[]{:S(2)}, u32[]{:S(2)}) async-start(bf16[64,80,128]{2,1,0:T(8,128)(2,1)} %shard_map.152), calls=%async_computation.3 | async-start | bytes 2621440 | tf_op jit(solution)/shard_map/all_to_all | solution.py:356
  127.3 2.9 %copy-start = (bf16[128,88,128]{2,1,0:T(8,128)(2,1)S(1)}, bf16[128,88,128]{2,1,0:T(8,128)(2,1)}, u32[]{:S(2)}) copy-start(bf16[128,88,128]{2,1,0:T(8,128)(2,1)} %all_to_all.20.mail_hbm) | copy-start | bytes 8650756
  147.3 5.2 %collective-permute-start.1 = (bf16[64,80,128]{2,1,0:T(8,128)(2,1)S(1)}, bf16[64,80,128]{2,1,0:T(8,128)(2,1)S(1)}, u32[]{:S(2)}, u32[]{:S(2)}) collective-permute-start(bf16[64,80,128]{2,1,0:T(8,128)(2,1)S(1)} %all-to-all-done.3.mine_ref), channel_id=1, source_target_pairs={{0,16},{16,0},{32,48},{48,32},{64,80},{80,64},{96,112},{112,96},{1... | collective-permute-start | bytes 3932168 | tf_op jit(solution)/shard_map/ppermute | solution.py:363

commit v5 on v4

--- a/solution.py
+++ b/solution.py
@@ -12,7 +12,7 @@
 LANES = 128
 UNUSED = 2.0**126
 PACK, LOCAL, MAIN = 58, 63, 56
-BOX, PIECE, SUM, FINISH = 63, 63, 63, 16
+BOX, PIECE, SUM, FINISH = 20, 12, 8, 16
 VMEM = pl.BlockSpec(memory_space=pltpu.VMEM)
 HBM = pl.BlockSpec(memory_space=pltpu.HBM)
 SMEM = pl.BlockSpec(memory_space=pltpu.SMEM)
@@ -38,13 +38,13 @@
 ):
     f32, bf16 = jnp.float32, jnp.bfloat16
     (fetch,) = copies(sems, [(features_hbm, features)])
-    parts, slots = rows_ref.shape[1:]
+    slots, parts = rows_ref.shape
     boundary, own = picks.shape
-    counts = jnp.broadcast_to(counts_ref[...], (LANES, parts)).T
     listed[...] = jnp.zeros_like(listed)
-    listed[:, :slots] = rows_ref[0] + 1
-    lane = lax.broadcasted_iota(jnp.int32, (parts, LANES), 1)
-    value = jnp.where(lane < counts, listed[...], 0)
+    place = lax.broadcasted_iota(jnp.int32, (slots, parts), 0)
+    counts = jnp.broadcast_to(counts_ref[...], (slots, parts))
+    listed[:slots, :] = jnp.where(place < counts, rows_ref[...] + 1, 0)
+    value = listed[...]
     step = boundary // 4
     slot = lax.broadcasted_iota(jnp.int32, (step, LANES), 0)
     lane = lax.broadcasted_iota(jnp.int32, (step, LANES), 1)
@@ -57,7 +57,7 @@
         peer = jnp.where(lane == slot // slots + k * (step // slots), 1.0, 0.0).astype(bf16)
         index = jnp.full((step, LANES), -1.0, f32)
         for part, weight in ((value >> 5, 32.0), (value & 31, 1.0)):
-            spread = mm(peer, part.astype(f32).astype(bf16))
+            spread = mm(peer, part.astype(f32).astype(bf16), ((1,), (1,)))
             index += weight * mm(jnp.where(mine, spread, 0.0).astype(bf16), ones)
         wanted[at, :] = index
         wide = jnp.concatenate([index] * (own // LANES), axis=1)
@@ -274,21 +274,29 @@
     save.wait()
 
 
-def sum_kernel(n_z, n_py, mail_hbm, out_ref, pieces, sems):
-    parts, size = pieces.shape[0], pieces.shape[1]
-    start = mail_hbm.shape[1] - size
-    (fetch,) = copies(sems, [(mail_hbm.at[:, start:, :], pieces)])
-    fetch.wait()
+def sum_kernel(n_z, n_py, mail_ref, out_ref, hidden_hbm, sems):
+    parts, slots, width = hidden_hbm.shape
+    size = out_ref.shape[1] // 2
+    start = mail_ref.shape[1] - size
+    saves = copies(
+        sems,
+        [
+            (mail_ref.at[:, pl.ds(k * slots, slots), :], hidden_hbm.at[:, :, pl.ds(k * LANES, LANES)])
+            for k in range(width // LANES)
+        ],
+    )
     for c in range(2):
         total = None
         for z in range(n_z):
             first = (z * 2 + c) * n_py
-            block = pieces[first : first + n_py].astype(jnp.float32).sum(0)
+            block = mail_ref[first : first + n_py, start:, :].astype(jnp.float32).sum(0)
             total = block if total is None else total + block
         rounded = total.astype(out_ref.dtype)
         out_ref[:, c * size : (c + 1) * size, :] = jnp.broadcast_to(
             rounded[None], (out_ref.shape[0], size, LANES)
         )
+    for save in saves:
+        save.wait()
 
 
 def finish_kernel(scale, n_py, core_ref, mine_ref, other_ref, one_hbm, two_hbm, one, two, sems):
@@ -342,7 +350,7 @@
             kernel,
             out_shape=out_shape,
             in_specs=[SMEM] * scalars + [VMEM] * n_vmem + [HBM] * (len(args) - scalars - n_vmem),
-            out_specs=jax.tree.map(lambda _: out_spec, out_shape),
+            out_specs=out_spec if isinstance(out, tuple) else jax.tree.map(lambda _: out_spec, out_shape),
             scratch_shapes=scratch,
             input_output_aliases=aliases or {},
             cost_estimate=pl.CostEstimate(flops=0, transcendentals=0, bytes_accessed=size),
@@ -402,12 +410,12 @@
         (slab, picks),
         0,
         in_vmem(
-            square, shape((parts, LANES), jnp.int32), shape((boundary, LANES), f32), picks, slab
+            square, shape((LANES, parts), jnp.int32), shape((boundary, LANES), f32), picks, slab
         )
         + semaphores(9),
         2,
         PACK,
-    )(send_rows, send_count, features)
+    )(send_rows[0].T, send_count, features)
     arrived = trade(outgoing.reshape(parts, slots, -1)).reshape(boundary, -1)
 
     near_adj, far_adj, agg, hidden_grad, grad_out = call(
@@ -459,23 +467,22 @@
     mail, grads = lax.optimization_barrier((mail, grads))
     mail = trade(mail)
     chips = parts // 2
-    mine = call(
+    mine, next_hidden = call(
         functools.partial(sum_kernel, n_z, n_py),
-        shape((chips, 2 * size, LANES), bf16),
-        0,
-        in_vmem(shape((parts, size, LANES), bf16)) + semaphores(1),
-        0,
+        (shape((chips, 2 * size, LANES), bf16), slots_in),
+        0,
+        semaphores(width // LANES),
+        1,
         SUM,
         None,
-        VMEM,
+        (VMEM, HBM),
     )(mail)
+    next_hidden = next_hidden.reshape(boundary, width)
     same_core = [[(2 * z + c) * n_py + i for z in range(n_z) for i in range(n_py)] for c in range(2)]
     mine = trade(mine, same_core)
-    next_hidden = mail[:, :rows].reshape(parts, width // LANES, slots, LANES)
-    next_hidden = jnp.swapaxes(next_hidden, 1, 2).reshape(boundary, width)
     sent = slot_ids[None, :] < send_count[0][:, None]
     next_grad = jnp.where(sent[:, :, None], grads, jnp.zeros_like(grads)).reshape(boundary, width)
-    mine, next_hidden, next_grad = lax.optimization_barrier((mine, next_hidden, next_grad))
+    mine, next_grad = lax.optimization_barrier((mine, next_grad))
     scale = 1.0 / math.sqrt(own * parts)
     one, two = call(
         functools.partial(finish_kernel, scale, n_py),

time: 156 us -> 149 us (0.955)
  Pallas kernels: 43.9 us -> 38 us
  waiting for transfers between devices: 30 us -> 34.8 us
  blocking collectives: 46.9 us -> 43.1 us
    pallas_call x7, Pallas kernels: 43.9 us -> 38 us  [run(): pl.pallas_call(kernel, out_shape=out_shape, in_specs=[SMEM] * scalars + [...]
    all_to_all x3, waiting for transfers between devices: 27.3 us -> 32.2 us  [trade(): lax.all_to_all(value, BOTH, split_axis=0, concat_axis=0, tiled=True, axis...]
    all_to_all x1, blocking collectives: 46.9 us -> 43.1 us  [trade(): lax.all_to_all(value, BOTH, split_axis=0, concat_axis=0, tiled=True, axis...]
  transfers between devices with their start and end apart: 5 -> 5, of which waited for: 3 -> 4; matrix products, arithmetic and copies ran while one was open for 3% -> 2% of each run, Pallas kernels for 22% -> 20%
where the time goes in v5:
time: 149 us
  blocking collectives  43.1 us (29%)
  Pallas kernels  38 us (26%)
  waiting for transfers between devices  34.8 us (23%)
  starting transfers between devices  26.9 us (18%)
  other arithmetic  2.85 us (2%)
  between operations  1.57 us (1%)
    all_to_all x1, blocking collectives, trade(): lax.all_to_all(value, BOTH, split_axis=0, concat_axis=0, tiled=True, axis...  43.1 us
    pallas_call x7, Pallas kernels, run(): pl.pallas_call(kernel, out_shape=out_shape, in_specs=[SMEM] * scalars + [...  38 us
    all_to_all x3, waiting for transfers between devices, trade(): lax.all_to_all(value, BOTH, split_axis=0, concat_axis=0, tiled=True, axis...  32.2 us
    all_to_all x3, starting transfers between devices, trade(): lax.all_to_all(value, BOTH, split_axis=0, concat_axis=0, tiled=True, axis...  22.9 us
    ppermute x2, starting transfers between devices, sibling(): return lax.ppermute(value, 'px', [(i, i ^ 1) for i in range(n)])  4.07 us
  transfers between devices with their start and end apart: 5, of which 4 were waited for; matrix products, arithmetic and copies ran while one was open for 2% of the time, Pallas kernels for 20%

profile of v5, /device:TPU:1, one launch (start us, length us, event | category | flops | bytes accessed | tf_op | source)
XLA Modules:
  0.0 148.6 jit_solution(8959610371375433383)
XLA Ops:
  0.6 4.2 %shard_map.147 = (bf16[1024,768]{1,0:T(8,128)(2,1)}, bf16[1024,768]{1,0:T(8,128)(2,1)}) custom-call(s32[8,128]{1,0:T(8,128)} %bitcast.13, s32[1,128]{1,0:T(1,128)} %counts_ref.1, bf16[768,768]{1,0:T(8,128)(2,1)} %features_hbm.3), custom_call_target="tpu_custom_call" | custom-call | bytes 4329984 | tf_op jit(solution)/shard_map/pallas_call | solution.py:349
  4.8 11.9 %all-to-all-start = ((bf16[128,8,768]{2,1,0:T(8,128)(2,1)}), bf16[128,8,768]{2,1,0:T(8,128)(2,1)}, u32[]{:S(2)}, u32[]{:S(2)}) async-start(bf16[128,8,768]{2,1,0:T(8,128)(2,1)} %bitcast.12), calls=%async_computation | async-start | bytes 3145728 | tf_op jit(solution)/shard_map/all_to_all | solution.py:364
  17.4 11.6 %shard_map.148 = (bf16[768,768]{1,0:T(8,128)(2,1)}, bf16[768,1024]{1,0:T(8,128)(2,1)}, f32[768,768]{1,0:T(8,128)}, f32[768,768]{1,0:T(8,128)}, bf16[128,8,768]{2,1,0:T(8,128)(2,1)}) custom-call(s32[32]{0:T(128)} %bitcast.15, s32[32]{0:T(128)} %bitcast.16, s32[1]{0:T(128)S(6)} %copy.18.count_ref, bf16[32,128,128]{2,1,0:T(8,128)(2,1)} %tiles_hbm.1, ...), custom_call_target="tpu_custom_call" | custom-call | bytes 16777476 | tf_op jit(solution)/shard_map/pallas_call | solution.py:349
  29.1 11.5 %all-to-all-done = bf16[128,8,768]{2,1,0:T(8,128)(2,1)} async-done(((bf16[128,8,768]{2,1,0:T(8,128)(2,1)}), bf16[128,8,768]{2,1,0:T(8,128)(2,1)}, u32[]{:S(2)}, u32[]{:S(2)}) %all-to-all-start) | async-done | bytes 1572896 | tf_op jit(solution)/shard_map/all_to_all | solution.py:364
  40.6 5.9 %all-to-all-start.1 = ((bf16[128,8,768]{2,1,0:T(8,128)(2,1)}), bf16[128,8,768]{2,1,0:T(8,128)(2,1)}, u32[]{:S(2)}, u32[]{:S(2)}) async-start(bf16[128,8,768]{2,1,0:T(8,128)(2,1)} %get-tuple-element.35), calls=%async_computation.1 | async-start | bytes 3145728 | tf_op jit(solution)/shard_map/all_to_all | solution.py:364
  46.4 0.0 copy-start
  46.4 15.4 %shard_map.149 = (bf16[768,768]{1,0:T(8,128)(2,1)}, f32[4608,128]{1,0:T(8,128)}, bf16[4608,128]{1,0:T(8,128)(2,1)}) custom-call(s32[1]{0:T(128)} %bitcast.core_ref, bf16[1024,768]{1,0:T(8,128)(2,1)} %bitcast.4.arrived_hbm, bf16[768,768]{1,0:T(8,128)(2,1)} %get-tuple-element.28.near_hbm, bf16[768,1024]{1,0:T(8,128)(2,1)} %get-tuple-element.29.far_hbm, ...), custom_call_target="tpu_custom_call" | custom-call | bytes 17694724 | tf_op jit(solution)/shard_map/pallas_call | solution.py:349
  61.8 1.5 %collective-permute-start = (bf16[4608,128]{1,0:T(8,128)(2,1)}, bf16[4608,128]{1,0:T(8,128)(2,1)S(1)}, u32[]{:S(2)}, u32[]{:S(2)}) collective-permute-start(bf16[4608,128]{1,0:T(8,128)(2,1)} %get-tuple-element.33), channel_id=1, source_target_pairs={{0,16},{16,0},{32,48},{48,32},{64,80},{80,64},{96,112},{112,96},{1... | collective-permute-start | bytes 3538952 | tf_op jit(solution)/shard_map/ppermute | solution.py:371
  63.4 0.0 copy-done
  63.4 0.0 copy-start.2
  63.4 1.3 copy-done.2
  64.6 0.0 copy-start.1
  64.6 1.9 %shard_map.150._ = bf16[128,88,128]{2,1,0:T(8,128)(2,1)S(1)} custom-call(bf16[1024,768]{1,0:T(8,128)(2,1)S(1)} %copy-done, bf16[768,768]{1,0:T(8,128)(2,1)S(1)} %copy-done.2), custom_call_target="tpu_custom_call" | custom-call | bytes 5636096 | tf_op jit(solution)/shard_map/pallas_call | solution.py:349
  66.5 0.0 collective-permute-done.other_ref
  66.5 0.0 copy-done.1
  66.5 0.3 shard_map.151
  66.9 3.5 %all-to-all-done.1 = bf16[128,8,768]{2,1,0:T(8,128)(2,1)} async-done(((bf16[128,8,768]{2,1,0:T(8,128)(2,1)}), bf16[128,8,768]{2,1,0:T(8,128)(2,1)}, u32[]{:S(2)}, u32[]{:S(2)}) %all-to-all-start.1) | async-done | bytes 1572896 | tf_op jit(solution)/shard_map/all_to_all | solution.py:364
  70.3 43.1 %all_to_all.20.mail_ref = bf16[128,88,128]{2,1,0:T(8,128)(2,1)S(1)} all-to-all(bf16[128,88,128]{2,1,0:T(8,128)(2,1)S(1)} %shard_map.151), channel_id=1, replica_groups=mesh['px'=8,'py'=16] {'px','py'}, dimensions={0} | all-to-all | bytes 5767168 | tf_op jit(solution)/shard_map/all_to_all | solution.py:364
  113.4 2.2 %shard_map.152 = (bf16[64,80,128]{2,1,0:T(8,128)(2,1)}, bf16[128,8,768]{2,1,0:T(8,128)(2,1)}) custom-call(bf16[128,88,128]{2,1,0:T(8,128)(2,1)S(1)} %all_to_all.20.mail_ref), custom_call_target="tpu_custom_call" | custom-call | bytes 5767168 | tf_op jit(solution)/shard_map/pallas_call | solution.py:349
  115.7 0.0 copy-start.3
  115.7 5.1 %all-to-all-start.3 = ((bf16[64,80,128]{2,1,0:T(8,128)(2,1)}), bf16[64,80,128]{2,1,0:T(8,128)(2,1)S(1)}, u32[]{:S(2)}, u32[]{:S(2)}) async-start(bf16[64,80,128]{2,1,0:T(8,128)(2,1)} %get-tuple-element.38), calls=%async_computation.3 | async-start | bytes 2621440 | tf_op jit(solution)/shard_map/all_to_all | solution.py:364
  120.8 0.0 copy-done.3
  120.8 0.1 iota_compare_fusion
  120.9 2.8 %select_bitcast_fusion = bf16[1024,768]{1,0:T(8,128)(2,1)} fusion(bf16[128,8,768]{2,1,0:T(8,128)(2,1)} %all-to-all-done.1, pred[128,8]{1,0:T(8,128)(4,1)S(1)} %iota_compare_fusion), kind=kLoop, calls=%fused_computation | loop fusion | flops 786432 | bytes 3146752 | tf_op jit(solution)/shard_map/reshape | solution.py:484
  123.7 17.2 %all-to-all-done.3.mine_ref = bf16[64,80,128]{2,1,0:T(8,128)(2,1)S(1)} async-done(((bf16[64,80,128]{2,1,0:T(8,128)(2,1)}), bf16[64,80,128]{2,1,0:T(8,128)(2,1)S(1)}, u32[]{:S(2)}, u32[]{:S(2)}) %all-to-all-start.3) | async-done | bytes 1310752 | tf_op jit(solution)/shard_map/all_to_all | solution.py:364
  140.9 2.5 %collective-permute-start.1 = (bf16[64,80,128]{2,1,0:T(8,128)(2,1)S(1)}, bf16[64,80,128]{2,1,0:T(8,128)(2,1)S(1)}, u32[]{:S(2)}, u32[]{:S(2)}) collective-permute-start(bf16[64,80,128]{2,1,0:T(8,128)(2,1)S(1)} %all-to-all-done.3.mine_ref), channel_id=1, source_target_pairs={{0,16},{16,0},{32,48},{48,32},{64,80},{80,64},{96,112},{112,96},{1... | collective-permute-start | bytes 3932168 | tf_op jit(solution)/shard_map/ppermute | solution.py:371
  143.4 2.7 %collective-permute-done.1.other_ref = bf16[64,80,128]{2,1,0:T(8,128)(2,1)S(1)} collective-permute-done((bf16[64,80,128]{2,1,0:T(8,128)(2,1)S(1)}, bf16[64,80,128]{2,1,0:T(8,128)(2,1)S(1)}, u32[]{:S(2)}, u32[]{:S(2)}) %collective-permute-start.1) | collective-permute-done | bytes 1310752 | tf_op jit(solution)/shard_map/ppermute | solution.py:371
  146.1 2.3 %shard_map.153 = (f32[768,768]{1,0:T(8,128)}, f32[768,768]{1,0:T(8,128)}) custom-call(s32[1]{0:T(128)} %bitcast.core_ref, bf16[64,80,128]{2,1,0:T(8,128)(2,1)S(1)} %all-to-all-done.3.mine_ref, bf16[64,80,128]{2,1,0:T(8,128)(2,1)S(1)} %collective-permute-done.1.other_ref), custom_call_target="tpu_custom_call" | custom-call | bytes 7340036 | tf_op jit(solution)/shard_map/pallas_call | solution.py:349
Async XLA Ops:
  4.8 35.7 %all-to-all-start = ((bf16[128,8,768]{2,1,0:T(8,128)(2,1)}), bf16[128,8,768]{2,1,0:T(8,128)(2,1)}, u32[]{:S(2)}, u32[]{:S(2)}) async-start(bf16[128,8,768]{2,1,0:T(8,128)(2,1)} %bitcast.12), calls=%async_computation | async-start | bytes 3145728 | tf_op jit(solution)/shard_map/all_to_all | solution.py:364
  40.6 29.8 %all-to-all-start.1 = ((bf16[128,8,768]{2,1,0:T(8,128)(2,1)}), bf16[128,8,768]{2,1,0:T(8,128)(2,1)}, u32[]{:S(2)}, u32[]{:S(2)}) async-start(bf16[128,8,768]{2,1,0:T(8,128)(2,1)} %get-tuple-element.35), calls=%async_computation.1 | async-start | bytes 3145728 | tf_op jit(solution)/shard_map/all_to_all | solution.py:364
  46.4 16.9 %copy-start = (bf16[1024,768]{1,0:T(8,128)(2,1)S(1)}, bf16[1024,768]{1,0:T(8,128)(2,1)}, u32[]{:S(2)}) copy-start(bf16[1024,768]{1,0:T(8,128)(2,1)} %get-tuple-element.25.picks_hbm) | copy-start | bytes 4718596
  61.8 4.7 %collective-permute-start = (bf16[4608,128]{1,0:T(8,128)(2,1)}, bf16[4608,128]{1,0:T(8,128)(2,1)S(1)}, u32[]{:S(2)}, u32[]{:S(2)}) collective-permute-start(bf16[4608,128]{1,0:T(8,128)(2,1)} %get-tuple-element.33), channel_id=1, source_target_pairs={{0,16},{16,0},{32,48},{48,32},{64,80},{80,64},{96,112},{112,96},{1... | collective-permute-start | bytes 3538952 | tf_op jit(solution)/shard_map/ppermute | solution.py:371
  63.4 1.3 copy-start.2
  64.6 1.9 %copy-start.1 = (f32[4608,128]{1,0:T(8,128)S(1)}, f32[4608,128]{1,0:T(8,128)}, u32[]{:S(2)}) copy-start(f32[4608,128]{1,0:T(8,128)} %get-tuple-element.32.keep_ref) | copy-start | bytes 7077892
  115.7 5.1 %copy-start.3 = (s32[1,128]{1,0:T(1,128)S(1)}, s32[1,128]{1,0:T(1,128)}, u32[]{:S(2)}) copy-start(s32[1,128]{1,0:T(1,128)} %counts_ref.1) | copy-start | bytes 1540
  115.7 25.2 %all-to-all-start.3 = ((bf16[64,80,128]{2,1,0:T(8,128)(2,1)}), bf16[64,80,128]{2,1,0:T(8,128)(2,1)S(1)}, u32[]{:S(2)}, u32[]{:S(2)}) async-start(bf16[64,80,128]{2,1,0:T(8,128)(2,1)} %get-tuple-element.38), calls=%async_computation.3 | async-start | bytes 2621440 | tf_op jit(solution)/shard_map/all_to_all | solution.py:364
  140.9 5.2 %collective-permute-start.1 = (bf16[64,80,128]{2,1,0:T(8,128)(2,1)S(1)}, bf16[64,80,128]{2,1,0:T(8,128)(2,1)S(1)}, u32[]{:S(2)}, u32[]{:S(2)}) collective-permute-start(bf16[64,80,128]{2,1,0:T(8,128)(2,1)S(1)} %all-to-all-done.3.mine_ref), channel_id=1, source_target_pairs={{0,16},{16,0},{32,48},{48,32},{64,80},{80,64},{96,112},{112,96},{1... | collective-permute-start | bytes 3932168 | tf_op jit(solution)/shard_map/ppermute | solution.py:371

commit v6 on v5

--- a/solution.py
+++ b/solution.py
@@ -275,16 +275,9 @@
 
 
 def sum_kernel(n_z, n_py, mail_ref, out_ref, hidden_hbm, sems):
-    parts, slots, width = hidden_hbm.shape
     size = out_ref.shape[1] // 2
     start = mail_ref.shape[1] - size
-    saves = copies(
-        sems,
-        [
-            (mail_ref.at[:, pl.ds(k * slots, slots), :], hidden_hbm.at[:, :, pl.ds(k * LANES, LANES)])
-            for k in range(width // LANES)
-        ],
-    )
+    saves = copies(sems, [(mail_ref.at[:, pl.ds(0, start), :], hidden_hbm)])
     for c in range(2):
         total = None
         for z in range(n_z):
@@ -391,7 +384,6 @@
     slots = send_rows.shape[2]
     boundary = parts * slots
     shape = jax.ShapeDtypeStruct
-    slot_ids = jnp.arange(slots, dtype=jnp.int32)
     core = (lax.axis_index("px") % 2).astype(jnp.int32).reshape(1)
     n_z, n_py = lax.axis_size("px") // 2, lax.axis_size("py")
 
@@ -469,20 +461,20 @@
     chips = parts // 2
     mine, next_hidden = call(
         functools.partial(sum_kernel, n_z, n_py),
-        (shape((chips, 2 * size, LANES), bf16), slots_in),
-        0,
-        semaphores(width // LANES),
+        (shape((chips, 2 * size, LANES), bf16), shape((parts, rows, LANES), bf16)),
+        0,
+        semaphores(1),
         1,
         SUM,
         None,
         (VMEM, HBM),
     )(mail)
-    next_hidden = next_hidden.reshape(boundary, width)
+    next_hidden = next_hidden.reshape(parts, width // LANES, slots, LANES)
+    next_hidden = jnp.swapaxes(next_hidden, 1, 2).reshape(boundary, width)
     same_core = [[(2 * z + c) * n_py + i for z in range(n_z) for i in range(n_py)] for c in range(2)]
     mine = trade(mine, same_core)
-    sent = slot_ids[None, :] < send_count[0][:, None]
-    next_grad = jnp.where(sent[:, :, None], grads, jnp.zeros_like(grads)).reshape(boundary, width)
-    mine, next_grad = lax.optimization_barrier((mine, next_grad))
+    grads = grads.reshape(boundary, width)
+    next_grad = jnp.where(outgoing == UNUSED, jnp.zeros_like(grads), grads)
     scale = 1.0 / math.sqrt(own * parts)
     one, two = call(
         functools.partial(finish_kernel, scale, n_py),

time: 149 us -> 148 us (level)
  blocking collectives: 43.1 us -> 68.2 us
  waiting for transfers between devices: 34.8 us -> 15 us
  starting transfers between devices: 26.9 us -> 21.8 us
    all_to_all x1 -> x2, blocking collectives: 43.1 us -> 68.2 us  [trade(): lax.all_to_all(value, BOTH, split_axis=0, concat_axis=0, tiled=True, axis...]
    all_to_all x3 -> x2, waiting for transfers between devices: 32.2 us -> 15 us  [trade(): lax.all_to_all(value, BOTH, split_axis=0, concat_axis=0, tiled=True, axis...]
    all_to_all x3 -> x2, starting transfers between devices: 22.9 us -> 17.8 us  [trade(): lax.all_to_all(value, BOTH, split_axis=0, concat_axis=0, tiled=True, axis...]
    reshape x1 -> x0, other arithmetic: 2.76 us -> none  [local(): jnp.where(sent[:, :, None], grads, jnp.zeros_like(grads))]
    select_n x0 -> x1, other arithmetic: none -> 2.75 us  [local(): next_grad = jnp.where(outgoing == UNUSED, jnp.zeros_like(grads), grads)]
    ppermute x2, waiting for transfers between devices: 2.66 us -> 0.01 us  [sibling(): return lax.ppermute(value, 'px', [(i, i ^ 1) for i in range(n)])]
  transfers between devices with their start and end apart: 5 -> 4, of which waited for: 4 -> 2; matrix products, arithmetic and copies ran while one was open for 2% -> 2% of each run, Pallas kernels for 20% -> 20%
where the time goes in v6:
time: 148 us
  blocking collectives  68.2 us (46%)
  Pallas kernels  36.9 us (25%)
  starting transfers between devices  21.8 us (15%)
  waiting for transfers between devices  15 us (10%)
  other arithmetic  2.75 us (2%)
  between operations  1.55 us (1%)
    all_to_all x2, blocking collectives, trade(): lax.all_to_all(value, BOTH, split_axis=0, concat_axis=0, tiled=True, axis...  68.2 us
    pallas_call x7, Pallas kernels, run(): pl.pallas_call(kernel, out_shape=out_shape, in_specs=[SMEM] * scalars + [...  36.9 us
    all_to_all x2, starting transfers between devices, trade(): lax.all_to_all(value, BOTH, split_axis=0, concat_axis=0, tiled=True, axis...  17.8 us
    all_to_all x2, waiting for transfers between devices, trade(): lax.all_to_all(value, BOTH, split_axis=0, concat_axis=0, tiled=True, axis...  15 us
    ppermute x2, starting transfers between devices, sibling(): return lax.ppermute(value, 'px', [(i, i ^ 1) for i in range(n)])  4.07 us
  transfers between devices with their start and end apart: 4, of which 2 were waited for; matrix products, arithmetic and copies ran while one was open for 2% of the time, Pallas kernels for 20%

profile of v6, /device:TPU:1, one launch (start us, length us, event | category | flops | bytes accessed | tf_op | source)
XLA Modules:
  0.0 147.5 jit_solution(9208330708836852896)
XLA Ops:
  0.6 4.2 %shard_map.147 = (bf16[1024,768]{1,0:T(8,128)(2,1)}, bf16[1024,768]{1,0:T(8,128)(2,1)}) custom-call(s32[8,128]{1,0:T(8,128)} %bitcast.16, s32[1,128]{1,0:T(1,128)} %counts_ref.1, bf16[768,768]{1,0:T(8,128)(2,1)} %features_hbm.3), custom_call_target="tpu_custom_call" | custom-call | bytes 4329984 | tf_op jit(solution)/shard_map/pallas_call | solution.py:342
  4.8 11.9 %all-to-all-start = ((bf16[128,8,768]{2,1,0:T(8,128)(2,1)}), bf16[128,8,768]{2,1,0:T(8,128)(2,1)}, u32[]{:S(2)}, u32[]{:S(2)}) async-start(bf16[128,8,768]{2,1,0:T(8,128)(2,1)} %bitcast.15), calls=%async_computation | async-start | bytes 3145728 | tf_op jit(solution)/shard_map/all_to_all | solution.py:357
  17.4 11.6 %shard_map.148 = (bf16[768,768]{1,0:T(8,128)(2,1)}, bf16[768,1024]{1,0:T(8,128)(2,1)}, f32[768,768]{1,0:T(8,128)}, f32[768,768]{1,0:T(8,128)}, bf16[128,8,768]{2,1,0:T(8,128)(2,1)}) custom-call(s32[32]{0:T(128)} %bitcast.17, s32[32]{0:T(128)} %bitcast.18, s32[1]{0:T(128)S(6)} %copy.18.count_ref, bf16[32,128,128]{2,1,0:T(8,128)(2,1)} %tiles_hbm.1, ...), custom_call_target="tpu_custom_call" | custom-call | bytes 16777476 | tf_op jit(solution)/shard_map/pallas_call | solution.py:342
  29.1 11.5 %all-to-all-done = bf16[128,8,768]{2,1,0:T(8,128)(2,1)} async-done(((bf16[128,8,768]{2,1,0:T(8,128)(2,1)}), bf16[128,8,768]{2,1,0:T(8,128)(2,1)}, u32[]{:S(2)}, u32[]{:S(2)}) %all-to-all-start) | async-done | bytes 1572896 | tf_op jit(solution)/shard_map/all_to_all | solution.py:357
  40.6 5.9 %all-to-all-start.1 = ((bf16[128,8,768]{2,1,0:T(8,128)(2,1)}), bf16[128,8,768]{2,1,0:T(8,128)(2,1)}, u32[]{:S(2)}, u32[]{:S(2)}) async-start(bf16[128,8,768]{2,1,0:T(8,128)(2,1)} %get-tuple-element.33), calls=%async_computation.1 | async-start | bytes 3145728 | tf_op jit(solution)/shard_map/all_to_all | solution.py:357
  46.4 0.0 copy-start
  46.4 15.4 %shard_map.149 = (bf16[768,768]{1,0:T(8,128)(2,1)}, f32[4608,128]{1,0:T(8,128)}, bf16[4608,128]{1,0:T(8,128)(2,1)}) custom-call(s32[1]{0:T(128)} %bitcast.core_ref, bf16[1024,768]{1,0:T(8,128)(2,1)} %bitcast.4.arrived_hbm, bf16[768,768]{1,0:T(8,128)(2,1)} %get-tuple-element.26.near_hbm, bf16[768,1024]{1,0:T(8,128)(2,1)} %get-tuple-element.27.far_hbm, ...), custom_call_target="tpu_custom_call" | custom-call | bytes 17694724 | tf_op jit(solution)/shard_map/pallas_call | solution.py:342
  61.9 1.5 %collective-permute-start = (bf16[4608,128]{1,0:T(8,128)(2,1)}, bf16[4608,128]{1,0:T(8,128)(2,1)S(1)}, u32[]{:S(2)}, u32[]{:S(2)}) collective-permute-start(bf16[4608,128]{1,0:T(8,128)(2,1)} %get-tuple-element.31), channel_id=1, source_target_pairs={{0,16},{16,0},{32,48},{48,32},{64,80},{80,64},{96,112},{112,96},{1... | collective-permute-start | bytes 3538952 | tf_op jit(solution)/shard_map/ppermute | solution.py:364
  63.4 0.0 copy-done
  63.4 0.0 copy-start.2
  63.4 1.3 copy-done.2
  64.7 0.0 copy-start.1
  64.7 1.9 %shard_map.150._ = bf16[128,88,128]{2,1,0:T(8,128)(2,1)S(1)} custom-call(bf16[1024,768]{1,0:T(8,128)(2,1)S(1)} %copy-done, bf16[768,768]{1,0:T(8,128)(2,1)S(1)} %copy-done.2), custom_call_target="tpu_custom_call" | custom-call | bytes 5636096 | tf_op jit(solution)/shard_map/pallas_call | solution.py:342
  66.5 0.0 collective-permute-done.other_ref
  66.5 0.0 copy-done.1
  66.6 0.3 shard_map.151
  66.9 3.5 %all-to-all-done.1 = bf16[128,8,768]{2,1,0:T(8,128)(2,1)} async-done(((bf16[128,8,768]{2,1,0:T(8,128)(2,1)}), bf16[128,8,768]{2,1,0:T(8,128)(2,1)}, u32[]{:S(2)}, u32[]{:S(2)}) %all-to-all-start.1) | async-done | bytes 1572896 | tf_op jit(solution)/shard_map/all_to_all | solution.py:357
  70.3 43.1 %all_to_all.20.mail_ref = bf16[128,88,128]{2,1,0:T(8,128)(2,1)S(1)} all-to-all(bf16[128,88,128]{2,1,0:T(8,128)(2,1)S(1)} %shard_map.151), channel_id=1, replica_groups=mesh['px'=8,'py'=16] {'px','py'}, dimensions={0} | all-to-all | bytes 5767168 | tf_op jit(solution)/shard_map/all_to_all | solution.py:357
  113.5 1.2 shard_map.152
  114.6 0.0 copy-start.3
  114.6 25.1 %all_to_all.21.mine_ref = bf16[64,80,128]{2,1,0:T(8,128)(2,1)S(1)} all-to-all(bf16[64,80,128]{2,1,0:T(8,128)(2,1)S(1)} %get-tuple-element.37), channel_id=1, replica_groups={{0,1,2,3,4,5,6,7,8,9,10,11,12,13,14,15,32,33,34,35,36,37,38,39,40,41,42..., dimensions={0} | all-to-all | bytes 2621440 | tf_op jit(solution)/shard_map/all_to_all | solution.py:357
  139.7 2.5 %collective-permute-start.1 = (bf16[64,80,128]{2,1,0:T(8,128)(2,1)S(1)}, bf16[64,80,128]{2,1,0:T(8,128)(2,1)S(1)}, u32[]{:S(2)}, u32[]{:S(2)}) collective-permute-start(bf16[64,80,128]{2,1,0:T(8,128)(2,1)S(1)} %all_to_all.21.mine_ref), channel_id=1, source_target_pairs={{0,16},{16,0},{32,48},{48,32},{64,80},{80,64},{96,112},{112,96},{1... | collective-permute-start | bytes 3932168 | tf_op jit(solution)/shard_map/ppermute | solution.py:364
  142.3 0.0 copy-done.3
  142.3 2.8 %compare_select_fusion = bf16[1024,768]{1,0:T(8,128)(2,1)} fusion(bf16[1024,768]{1,0:T(8,128)(2,1)S(1)} %copy-done.3, bf16[128,8,768]{2,1,0:T(8,128)(2,1)} %all-to-all-done.1), kind=kLoop, calls=%fused_computation | loop fusion | flops 1572864 | bytes 4718592 | tf_op jit(solution)/shard_map/jit(_where)/select_n | solution.py:477
  145.0 0.0 collective-permute-done.1.other_ref
  145.0 2.3 %shard_map.153 = (f32[768,768]{1,0:T(8,128)}, f32[768,768]{1,0:T(8,128)}) custom-call(s32[1]{0:T(128)} %bitcast.core_ref, bf16[64,80,128]{2,1,0:T(8,128)(2,1)S(1)} %all_to_all.21.mine_ref, bf16[64,80,128]{2,1,0:T(8,128)(2,1)S(1)} %collective-permute-done.1.other_ref), custom_call_target="tpu_custom_call" | custom-call | bytes 7340036 | tf_op jit(solution)/shard_map/pallas_call | solution.py:342
Async XLA Ops:
  4.8 35.7 %all-to-all-start = ((bf16[128,8,768]{2,1,0:T(8,128)(2,1)}), bf16[128,8,768]{2,1,0:T(8,128)(2,1)}, u32[]{:S(2)}, u32[]{:S(2)}) async-start(bf16[128,8,768]{2,1,0:T(8,128)(2,1)} %bitcast.15), calls=%async_computation | async-start | bytes 3145728 | tf_op jit(solution)/shard_map/all_to_all | solution.py:357
  40.6 29.8 %all-to-all-start.1 = ((bf16[128,8,768]{2,1,0:T(8,128)(2,1)}), bf16[128,8,768]{2,1,0:T(8,128)(2,1)}, u32[]{:S(2)}, u32[]{:S(2)}) async-start(bf16[128,8,768]{2,1,0:T(8,128)(2,1)} %get-tuple-element.33), calls=%async_computation.1 | async-start | bytes 3145728 | tf_op jit(solution)/shard_map/all_to_all | solution.py:357
  46.4 16.9 %copy-start = (bf16[1024,768]{1,0:T(8,128)(2,1)S(1)}, bf16[1024,768]{1,0:T(8,128)(2,1)}, u32[]{:S(2)}) copy-start(bf16[1024,768]{1,0:T(8,128)(2,1)} %get-tuple-element.23.picks_hbm) | copy-start | bytes 4718596
  61.9 4.7 %collective-permute-start = (bf16[4608,128]{1,0:T(8,128)(2,1)}, bf16[4608,128]{1,0:T(8,128)(2,1)S(1)}, u32[]{:S(2)}, u32[]{:S(2)}) collective-permute-start(bf16[4608,128]{1,0:T(8,128)(2,1)} %get-tuple-element.31), channel_id=1, source_target_pairs={{0,16},{16,0},{32,48},{48,32},{64,80},{80,64},{96,112},{112,96},{1... | collective-permute-start | bytes 3538952 | tf_op jit(solution)/shard_map/ppermute | solution.py:364
  63.4 1.3 copy-start.2
  64.7 1.9 %copy-start.1 = (f32[4608,128]{1,0:T(8,128)S(1)}, f32[4608,128]{1,0:T(8,128)}, u32[]{:S(2)}) copy-start(f32[4608,128]{1,0:T(8,128)} %get-tuple-element.30.keep_ref) | copy-start | bytes 7077892
  114.6 27.7 %copy-start.3 = (bf16[1024,768]{1,0:T(8,128)(2,1)S(1)}, bf16[1024,768]{1,0:T(8,128)(2,1)}, u32[]{:S(2)}) copy-start(bf16[1024,768]{1,0:T(8,128)(2,1)} %get-tuple-element.22) | copy-start | bytes 4718596
  139.7 5.3 %collective-permute-start.1 = (bf16[64,80,128]{2,1,0:T(8,128)(2,1)S(1)}, bf16[64,80,128]{2,1,0:T(8,128)(2,1)S(1)}, u32[]{:S(2)}, u32[]{:S(2)}) collective-permute-start(bf16[64,80,128]{2,1,0:T(8,128)(2,1)S(1)} %all_to_all.21.mine_ref), channel_id=1, source_target_pairs={{0,16},{16,0},{32,48},{48,32},{64,80},{80,64},{96,112},{112,96},{1... | collective-permute-start | bytes 3932168 | tf_op jit(solution)/shard_map/ppermute | solution.py:364

commit v7 on v6

--- a/solution.py
+++ b/solution.py
@@ -262,62 +262,79 @@
 
 def piece_kernel(keep_ref, other_ref, _, mail_hbm, pieces, sems):
     parts, size = pieces.shape[0], pieces.shape[1]
-    total = keep_ref[...] + other_ref[...].astype(jnp.float32)
-    whole = total.shape[0] // size
-    rest = total.shape[0] - whole * size
-    pieces[:whole] = total[: whole * size].reshape(whole, size, LANES).astype(pieces.dtype)
-    pieces[whole:] = jnp.zeros((parts - whole, size, LANES), pieces.dtype)
-    if rest:
-        pieces[whole, :rest] = total[whole * size :].astype(pieces.dtype)
+    share = 2 * keep_ref.shape[0] // parts
+    for j in range(parts // 2):
+        lines = pl.ds(j * share, share)
+        total = keep_ref[lines, :] + other_ref[lines, :].astype(jnp.float32)
+        pieces[2 * j] = total[:size].astype(pieces.dtype)
+        pieces[2 * j + 1] = total[share - size :].astype(pieces.dtype)
     start = mail_hbm.shape[1] - size
     (save,) = copies(sems, [(pieces, mail_hbm.at[:, start:, :])])
     save.wait()
 
 
-def sum_kernel(n_z, n_py, mail_ref, out_ref, hidden_hbm, sems):
-    size = out_ref.shape[1] // 2
-    start = mail_ref.shape[1] - size
+def sum_kernel(n_z, n_py, odd_ref, mail_ref, out_ref, hidden_hbm, sems):
+    chips, share = out_ref.shape[:2]
+    start = hidden_hbm.shape[1]
+    size = mail_ref.shape[1] - start
     saves = copies(sems, [(mail_ref.at[:, pl.ds(0, start), :], hidden_hbm)])
+    sums = []
     for c in range(2):
         total = None
         for z in range(n_z):
             first = (z * 2 + c) * n_py
             block = mail_ref[first : first + n_py, start:, :].astype(jnp.float32).sum(0)
             total = block if total is None else total + block
-        rounded = total.astype(out_ref.dtype)
-        out_ref[:, c * size : (c + 1) * size, :] = jnp.broadcast_to(
-            rounded[None], (out_ref.shape[0], size, LANES)
-        )
+        sums.append(total)
+    rest = share - size
+
+    def give(one, two):
+        both = jnp.concatenate([one, two], axis=0).astype(out_ref.dtype)
+        out_ref[...] = jnp.broadcast_to(both[None], (chips, share, LANES))
+
+    @pl.when(odd_ref[0] == 0)
+    def _():
+        give(sums[0], sums[1][:rest])
+
+    @pl.when(odd_ref[0] != 0)
+    def _():
+        give(sums[0][size - rest :], sums[1])
+
     for save in saves:
         save.wait()
 
 
-def finish_kernel(scale, n_py, core_ref, mine_ref, other_ref, one_hbm, two_hbm, one, two, sems):
-    size = mine_ref.shape[1] // 2
+def finish_kernel(scale, size, n_py, core_ref, mine_ref, other_ref, one_hbm, two_hbm, one, two, sems):
+    chips, share = mine_ref.shape[:2]
+    rest = share - size
     width = one.shape[0]
-    lines = width * width // LANES
 
     def fill(sources):
         saves = []
-        for q in range(2 * mine_ref.shape[0]):
+        for q in range(2 * chips):
             row, py = divmod(q, n_py)
             z, c = divmod(row, 2)
-            line = q * size
-            end = min(line + size, lines)
-            while line < end:
-                k, r = divmod(line, width)
+            pair, odd = divmod(q, 2)
+            spans = ((size, rest, one), (rest, size, two)) if odd else ((0, size, one), (0, rest, two))
+            at = 0
+            for skip, count, out in spans:
+                line = pair * share + skip
+                end = line + count
+                while line < end:
+                    k, r = divmod(line, width)
+                    run = min(end - line, width - r)
+                    value = sources[c][z * n_py + py, at : at + run, :]
+                    block = slice(k * LANES, (k + 1) * LANES)
+                    out[r : r + run, block] = value.astype(jnp.float32) * scale
+                    line += run
+                    at += run
+            done, before = (pair + 1) * share // width, pair * share // width
+            for k in range(before, done if odd else before):
                 block = slice(k * LANES, (k + 1) * LANES)
-                count = min(end - line, width - r)
-                for g, out in enumerate((one, two)):
-                    at = g * size + line - q * size
-                    value = sources[c][z * n_py + py, at : at + count, :]
-                    out[r : r + count, block] = value.astype(jnp.float32) * scale
-                line += count
-                if r + count == width:
-                    saves += copies(
-                        sems.at[pl.ds(2 * k, 2)],
-                        [(one.at[:, block], one_hbm.at[:, block]), (two.at[:, block], two_hbm.at[:, block])],
-                    )
+                saves += copies(
+                    sems.at[pl.ds(2 * k, 2)],
+                    [(one.at[:, block], one_hbm.at[:, block]), (two.at[:, block], two_hbm.at[:, block])],
+                )
         for save in saves:
             save.wait()
 
@@ -437,7 +454,8 @@
     )(core, arrived, near_adj, far_adj, agg, weight_one, hidden_grad, stale_hidden, out_grad)
 
     other = sibling(send)
-    size = -(-lines // (parts * 8)) * 8
+    share = 2 * lines // parts
+    size = -(-share // 16) * 8
     rows = slots * width // LANES
     mail = call(
         box_kernel,
@@ -456,19 +474,20 @@
         PIECE,
         {2: 0},
     )(keep, other, mail)
-    mail, grads = lax.optimization_barrier((mail, grads))
+    odd = lax.axis_index("py").astype(jnp.int32).reshape(1) % 2
+    mail, grads, odd = lax.optimization_barrier((mail, grads, odd))
     mail = trade(mail)
     chips = parts // 2
     mine, next_hidden = call(
         functools.partial(sum_kernel, n_z, n_py),
-        (shape((chips, 2 * size, LANES), bf16), shape((parts, rows, LANES), bf16)),
-        0,
+        (shape((chips, share, LANES), bf16), shape((parts, rows, LANES), bf16)),
+        1,
         semaphores(1),
         1,
         SUM,
         None,
         (VMEM, HBM),
-    )(mail)
+    )(odd, mail)
     next_hidden = next_hidden.reshape(parts, width // LANES, slots, LANES)
     next_hidden = jnp.swapaxes(next_hidden, 1, 2).reshape(boundary, width)
     same_core = [[(2 * z + c) * n_py + i for z in range(n_z) for i in range(n_py)] for c in range(2)]
@@ -477,7 +496,7 @@
     next_grad = jnp.where(outgoing == UNUSED, jnp.zeros_like(grads), grads)
     scale = 1.0 / math.sqrt(own * parts)
     one, two = call(
-        functools.partial(finish_kernel, scale, n_py),
+        functools.partial(finish_kernel, scale, size, n_py),
         (shape((width, width), f32),) * 2,
         1,
         in_vmem(*(shape((width, width), f32),) * 2) + semaphores(2 * (width // LANES)),

time: 148 us -> 149 us (level)
  waiting for transfers between devices: 15 us -> 12.4 us
    all_to_all x2, waiting for transfers between devices: 15 us -> 12.4 us  [trade(): lax.all_to_all(value, BOTH, split_axis=0, concat_axis=0, tiled=True, axis...]
where the time goes in v7:
time: 149 us
  blocking collectives  69.4 us (47%)
  Pallas kernels  38.1 us (26%)
  starting transfers between devices  21.8 us (15%)
  waiting for transfers between devices  12.4 us (8%)
  other arithmetic  2.75 us (2%)
  local copies, waits for them, and re-layouts  2.69 us (2%)
  between operations  1.54 us (1%)
    all_to_all x2, blocking collectives, trade(): lax.all_to_all(value, BOTH, split_axis=0, concat_axis=0, tiled=True, axis...  69.4 us
    pallas_call x7, Pallas kernels, run(): pl.pallas_call(kernel, out_shape=out_shape, in_specs=[SMEM] * scalars + [...  38.1 us
    all_to_all x2, starting transfers between devices, trade(): lax.all_to_all(value, BOTH, split_axis=0, concat_axis=0, tiled=True, axis...  17.8 us
    all_to_all x2, waiting for transfers between devices, trade(): lax.all_to_all(value, BOTH, split_axis=0, concat_axis=0, tiled=True, axis...  12.4 us
    ppermute x2, starting transfers between devices, sibling(): return lax.ppermute(value, 'px', [(i, i ^ 1) for i in range(n)])  4.05 us
  transfers between devices with their start and end apart: 4, of which 2 were waited for; matrix products, arithmetic and copies ran while one was open for 2% of the time, Pallas kernels for 20%

profile of v7, /device:TPU:1, one launch (start us, length us, event | category | flops | bytes accessed | tf_op | source)
XLA Modules:
  0.0 148.7 jit_solution(15149456658487715835)
XLA Ops:
  0.6 4.2 %shard_map.147 = (bf16[1024,768]{1,0:T(8,128)(2,1)}, bf16[1024,768]{1,0:T(8,128)(2,1)}) custom-call(s32[8,128]{1,0:T(8,128)} %bitcast.17, s32[1,128]{1,0:T(1,128)} %counts_ref.1, bf16[768,768]{1,0:T(8,128)(2,1)} %features_hbm.3), custom_call_target="tpu_custom_call" | custom-call | bytes 4329984 | tf_op jit(solution)/shard_map/pallas_call | solution.py:359
  4.8 11.9 %all-to-all-start = ((bf16[128,8,768]{2,1,0:T(8,128)(2,1)}), bf16[128,8,768]{2,1,0:T(8,128)(2,1)}, u32[]{:S(2)}, u32[]{:S(2)}) async-start(bf16[128,8,768]{2,1,0:T(8,128)(2,1)} %bitcast.16), calls=%async_computation | async-start | bytes 3145728 | tf_op jit(solution)/shard_map/all_to_all | solution.py:374
  17.4 11.6 %shard_map.148 = (bf16[768,768]{1,0:T(8,128)(2,1)}, bf16[768,1024]{1,0:T(8,128)(2,1)}, f32[768,768]{1,0:T(8,128)}, f32[768,768]{1,0:T(8,128)}, bf16[128,8,768]{2,1,0:T(8,128)(2,1)}) custom-call(s32[32]{0:T(128)} %bitcast.18, s32[32]{0:T(128)} %bitcast.19, s32[1]{0:T(128)S(6)} %copy.18.count_ref, bf16[32,128,128]{2,1,0:T(8,128)(2,1)} %tiles_hbm.1, ...), custom_call_target="tpu_custom_call" | custom-call | bytes 16777476 | tf_op jit(solution)/shard_map/pallas_call | solution.py:359
  29.1 11.5 %all-to-all-done = bf16[128,8,768]{2,1,0:T(8,128)(2,1)} async-done(((bf16[128,8,768]{2,1,0:T(8,128)(2,1)}), bf16[128,8,768]{2,1,0:T(8,128)(2,1)}, u32[]{:S(2)}, u32[]{:S(2)}) %all-to-all-start) | async-done | bytes 1572896 | tf_op jit(solution)/shard_map/all_to_all | solution.py:374
  40.6 5.9 %all-to-all-start.1 = ((bf16[128,8,768]{2,1,0:T(8,128)(2,1)}), bf16[128,8,768]{2,1,0:T(8,128)(2,1)}, u32[]{:S(2)}, u32[]{:S(2)}) async-start(bf16[128,8,768]{2,1,0:T(8,128)(2,1)} %get-tuple-element.34), calls=%async_computation.1 | async-start | bytes 3145728 | tf_op jit(solution)/shard_map/all_to_all | solution.py:374
  46.4 15.3 %shard_map.149 = (bf16[768,768]{1,0:T(8,128)(2,1)}, f32[4608,128]{1,0:T(8,128)}, bf16[4608,128]{1,0:T(8,128)(2,1)}) custom-call(s32[1]{0:T(128)} %bitcast.core_ref, bf16[1024,768]{1,0:T(8,128)(2,1)} %bitcast.4.arrived_hbm, bf16[768,768]{1,0:T(8,128)(2,1)} %get-tuple-element.27.near_hbm, bf16[768,1024]{1,0:T(8,128)(2,1)} %get-tuple-element.28.far_hbm, ...), custom_call_target="tpu_custom_call" | custom-call | bytes 17694724 | tf_op jit(solution)/shard_map/pallas_call | solution.py:359
  61.7 1.5 %collective-permute-start = (bf16[4608,128]{1,0:T(8,128)(2,1)}, bf16[4608,128]{1,0:T(8,128)(2,1)}, u32[]{:S(2)}, u32[]{:S(2)}) collective-permute-start(bf16[4608,128]{1,0:T(8,128)(2,1)} %get-tuple-element.32), channel_id=1, source_target_pairs={{0,16},{16,0},{32,48},{48,32},{64,80},{80,64},{96,112},{112,96},{1... | collective-permute-start | bytes 3538952 | tf_op jit(solution)/shard_map/ppermute | solution.py:381
  63.3 0.0 copy-start
  63.3 1.4 copy-done
  64.7 0.0 copy-start.2
  64.7 1.3 copy-done.2
  65.9 0.0 copy-start.1
  65.9 1.9 %shard_map.150._ = bf16[128,88,128]{2,1,0:T(8,128)(2,1)S(1)} custom-call(bf16[1024,768]{1,0:T(8,128)(2,1)S(1)} %copy-done, bf16[768,768]{1,0:T(8,128)(2,1)S(1)} %copy-done.2), custom_call_target="tpu_custom_call" | custom-call | bytes 5636096 | tf_op jit(solution)/shard_map/pallas_call | solution.py:359
  67.8 0.0 collective-permute-done.other_ref
  67.8 0.0 copy-done.1
  67.8 1.6 %shard_map.151 = bf16[128,88,128]{2,1,0:T(8,128)(2,1)S(1)} custom-call(f32[4608,128]{1,0:T(8,128)S(1)} %copy-done.1, bf16[4608,128]{1,0:T(8,128)(2,1)} %collective-permute-done.other_ref, bf16[128,88,128]{2,1,0:T(8,128)(2,1)S(1)} %shard_map.150._), custom_call_target="tpu_custom_call", output_to_operand_aliasing={{}: (2, {})} | custom-call | bytes 9306112 | tf_op jit(solution)/shard_map/pallas_call | solution.py:359
  69.4 0.9 all-to-all-done.1
  70.3 45.7 %all_to_all.20.mail_ref = bf16[128,88,128]{2,1,0:T(8,128)(2,1)S(1)} all-to-all(bf16[128,88,128]{2,1,0:T(8,128)(2,1)S(1)} %shard_map.151), channel_id=1, replica_groups=mesh['px'=8,'py'=16] {'px','py'}, dimensions={0} | all-to-all | bytes 5767168 | tf_op jit(solution)/shard_map/all_to_all | solution.py:374
  116.0 1.2 shard_map.152
  117.2 0.0 copy-start.3
  117.2 23.7 %all_to_all.21.mine_ref = bf16[64,72,128]{2,1,0:T(8,128)(2,1)S(1)} all-to-all(bf16[64,72,128]{2,1,0:T(8,128)(2,1)S(1)} %get-tuple-element.39), channel_id=1, replica_groups={{0,1,2,3,4,5,6,7,8,9,10,11,12,13,14,15,32,33,34,35,36,37,38,39,40,41,42..., dimensions={0} | all-to-all | bytes 2359296 | tf_op jit(solution)/shard_map/all_to_all | solution.py:374
  140.9 2.5 %collective-permute-start.1 = (bf16[64,72,128]{2,1,0:T(8,128)(2,1)S(1)}, bf16[64,72,128]{2,1,0:T(8,128)(2,1)S(1)}, u32[]{:S(2)}, u32[]{:S(2)}) collective-permute-start(bf16[64,72,128]{2,1,0:T(8,128)(2,1)S(1)} %all_to_all.21.mine_ref), channel_id=1, source_target_pairs={{0,16},{16,0},{32,48},{48,32},{64,80},{80,64},{96,112},{112,96},{1... | collective-permute-start | bytes 3538952 | tf_op jit(solution)/shard_map/ppermute | solution.py:381
  143.4 0.0 copy-done.3
  143.4 2.8 %compare_select_fusion = bf16[1024,768]{1,0:T(8,128)(2,1)} fusion(bf16[1024,768]{1,0:T(8,128)(2,1)S(1)} %copy-done.3, bf16[128,8,768]{2,1,0:T(8,128)(2,1)} %all-to-all-done.1), kind=kLoop, calls=%fused_computation | loop fusion | flops 1572864 | bytes 4718592 | tf_op jit(solution)/shard_map/jit(_where)/select_n | solution.py:496
  146.2 0.0 collective-permute-done.1.other_ref
  146.2 2.3 %shard_map.153 = (f32[768,768]{1,0:T(8,128)}, f32[768,768]{1,0:T(8,128)}) custom-call(s32[1]{0:T(128)} %bitcast.core_ref, bf16[64,72,128]{2,1,0:T(8,128)(2,1)S(1)} %all_to_all.21.mine_ref, bf16[64,72,128]{2,1,0:T(8,128)(2,1)S(1)} %collective-permute-done.1.other_ref), custom_call_target="tpu_custom_call" | custom-call | bytes 7077892 | tf_op jit(solution)/shard_map/pallas_call | solution.py:359
Async XLA Ops:
  4.8 35.7 %all-to-all-start = ((bf16[128,8,768]{2,1,0:T(8,128)(2,1)}), bf16[128,8,768]{2,1,0:T(8,128)(2,1)}, u32[]{:S(2)}, u32[]{:S(2)}) async-start(bf16[128,8,768]{2,1,0:T(8,128)(2,1)} %bitcast.16), calls=%async_computation | async-start | bytes 3145728 | tf_op jit(solution)/shard_map/all_to_all | solution.py:374
  40.6 29.8 %all-to-all-start.1 = ((bf16[128,8,768]{2,1,0:T(8,128)(2,1)}), bf16[128,8,768]{2,1,0:T(8,128)(2,1)}, u32[]{:S(2)}, u32[]{:S(2)}) async-start(bf16[128,8,768]{2,1,0:T(8,128)(2,1)} %get-tuple-element.34), calls=%async_computation.1 | async-start | bytes 3145728 | tf_op jit(solution)/shard_map/all_to_all | solution.py:374
  61.7 6.1 %collective-permute-start = (bf16[4608,128]{1,0:T(8,128)(2,1)}, bf16[4608,128]{1,0:T(8,128)(2,1)}, u32[]{:S(2)}, u32[]{:S(2)}) collective-permute-start(bf16[4608,128]{1,0:T(8,128)(2,1)} %get-tuple-element.32), channel_id=1, source_target_pairs={{0,16},{16,0},{32,48},{48,32},{64,80},{80,64},{96,112},{112,96},{1... | collective-permute-start | bytes 3538952 | tf_op jit(solution)/shard_map/ppermute | solution.py:381
  63.3 1.4 copy-start
  64.7 1.3 copy-start.2
  65.9 1.9 %copy-start.1 = (f32[4608,128]{1,0:T(8,128)S(1)}, f32[4608,128]{1,0:T(8,128)}, u32[]{:S(2)}) copy-start(f32[4608,128]{1,0:T(8,128)} %get-tuple-element.31.keep_ref) | copy-start | bytes 7077892
  117.2 26.3 %copy-start.3 = (bf16[1024,768]{1,0:T(8,128)(2,1)S(1)}, bf16[1024,768]{1,0:T(8,128)(2,1)}, u32[]{:S(2)}) copy-start(bf16[1024,768]{1,0:T(8,128)(2,1)} %get-tuple-element.23) | copy-start | bytes 4718596
  140.9 5.3 %collective-permute-start.1 = (bf16[64,72,128]{2,1,0:T(8,128)(2,1)S(1)}, bf16[64,72,128]{2,1,0:T(8,128)(2,1)S(1)}, u32[]{:S(2)}, u32[]{:S(2)}) collective-permute-start(bf16[64,72,128]{2,1,0:T(8,128)(2,1)S(1)} %all_to_all.21.mine_ref), channel_id=1, source_target_pairs={{0,16},{16,0},{32,48},{48,32},{64,80},{80,64},{96,112},{112,96},{1... | collective-permute-start | bytes 3538952 | tf_op jit(solution)/shard_map/ppermute | solution.py:381

commit v8 on v7

--- a/solution.py
+++ b/solution.py
@@ -273,7 +273,7 @@
     save.wait()
 
 
-def sum_kernel(n_z, n_py, odd_ref, mail_ref, out_ref, hidden_hbm, sems):
+def sum_kernel(n_z, n_py, core_ref, mail_ref, out_ref, hidden_hbm, sems):
     chips, share = out_ref.shape[:2]
     start = hidden_hbm.shape[1]
     size = mail_ref.shape[1] - start
@@ -292,11 +292,11 @@
         both = jnp.concatenate([one, two], axis=0).astype(out_ref.dtype)
         out_ref[...] = jnp.broadcast_to(both[None], (chips, share, LANES))
 
-    @pl.when(odd_ref[0] == 0)
+    @pl.when(core_ref[1] == 0)
     def _():
         give(sums[0], sums[1][:rest])
 
-    @pl.when(odd_ref[0] != 0)
+    @pl.when(core_ref[1] != 0)
     def _():
         give(sums[0][size - rest :], sums[1])
 
@@ -401,7 +401,7 @@
     slots = send_rows.shape[2]
     boundary = parts * slots
     shape = jax.ShapeDtypeStruct
-    core = (lax.axis_index("px") % 2).astype(jnp.int32).reshape(1)
+    core = jnp.stack([lax.axis_index("px") % 2, lax.axis_index("py") % 2]).astype(jnp.int32)
     n_z, n_py = lax.axis_size("px") // 2, lax.axis_size("py")
 
     square, square32 = shape((own, width), bf16), shape((own, width), f32)
@@ -474,8 +474,7 @@
         PIECE,
         {2: 0},
     )(keep, other, mail)
-    odd = lax.axis_index("py").astype(jnp.int32).reshape(1) % 2
-    mail, grads, odd = lax.optimization_barrier((mail, grads, odd))
+    mail, grads = lax.optimization_barrier((mail, grads))
     mail = trade(mail)
     chips = parts // 2
     mine, next_hidden = call(
@@ -487,7 +486,7 @@
         SUM,
         None,
         (VMEM, HBM),
-    )(odd, mail)
+    )(core, mail)
     next_hidden = next_hidden.reshape(parts, width // LANES, slots, LANES)
     next_hidden = jnp.swapaxes(next_hidden, 1, 2).reshape(boundary, width)
     same_core = [[(2 * z + c) * n_py + i for z in range(n_z) for i in range(n_py)] for c in range(2)]

time: 149 us -> 149 us (level)
  no operation moved by 1% of the time
where the time goes in v8:
time: 149 us; the launch traced here: 148 us
  blocking collectives  68.1 us (46%)
  Pallas kernels  38.7 us (26%)
  starting transfers between devices  21.8 us (15%)
  waiting for transfers between devices  13.7 us (9%)
  other arithmetic  3.35 us (2%)
  between operations  1.56 us (1%)
    all_to_all x2, blocking collectives, trade(): lax.all_to_all(value, BOTH, split_axis=0, concat_axis=0, tiled=True, axis...  68.1 us
    pallas_call x7, Pallas kernels, run(): pl.pallas_call(kernel, out_shape=out_shape, in_specs=[SMEM] * scalars + [...  38.7 us
    all_to_all x2, starting transfers between devices, trade(): lax.all_to_all(value, BOTH, split_axis=0, concat_axis=0, tiled=True, axis...  17.8 us
    all_to_all x2, waiting for transfers between devices, trade(): lax.all_to_all(value, BOTH, split_axis=0, concat_axis=0, tiled=True, axis...  13.7 us
    ppermute x2, starting transfers between devices, sibling(): return lax.ppermute(value, 'px', [(i, i ^ 1) for i in range(n)])  4.05 us
  transfers between devices with their start and end apart: 4, of which 2 were waited for; matrix products, arithmetic and copies ran while one was open for 2% of the time, Pallas kernels for 20%

profile of v8, /device:TPU:1, one launch (start us, length us, event | category | flops | bytes accessed | tf_op | source)
XLA Modules:
  0.0 148.5 jit_solution(17034164923975789006)
XLA Ops:
  0.6 4.2 %shard_map.147 = (bf16[1024,768]{1,0:T(8,128)(2,1)}, bf16[1024,768]{1,0:T(8,128)(2,1)}) custom-call(s32[8,128]{1,0:T(8,128)} %bitcast.17, s32[1,128]{1,0:T(1,128)} %counts_ref.1, bf16[768,768]{1,0:T(8,128)(2,1)} %features_hbm.3), custom_call_target="tpu_custom_call" | custom-call | bytes 4329984 | tf_op jit(solution)/shard_map/pallas_call | solution.py:359
  4.8 11.9 %all-to-all-start = ((bf16[128,8,768]{2,1,0:T(8,128)(2,1)}), bf16[128,8,768]{2,1,0:T(8,128)(2,1)}, u32[]{:S(2)}, u32[]{:S(2)}) async-start(bf16[128,8,768]{2,1,0:T(8,128)(2,1)} %bitcast.16), calls=%async_computation | async-start | bytes 3145728 | tf_op jit(solution)/shard_map/all_to_all | solution.py:374
  17.4 11.6 %shard_map.148 = (bf16[768,768]{1,0:T(8,128)(2,1)}, bf16[768,1024]{1,0:T(8,128)(2,1)}, f32[768,768]{1,0:T(8,128)}, f32[768,768]{1,0:T(8,128)}, bf16[128,8,768]{2,1,0:T(8,128)(2,1)}) custom-call(s32[32]{0:T(128)} %bitcast.18, s32[32]{0:T(128)} %bitcast.19, s32[1]{0:T(128)S(6)} %copy.18.count_ref, bf16[32,128,128]{2,1,0:T(8,128)(2,1)} %tiles_hbm.1, ...), custom_call_target="tpu_custom_call" | custom-call | bytes 16777476 | tf_op jit(solution)/shard_map/pallas_call | solution.py:359
  29.1 11.5 %all-to-all-done = bf16[128,8,768]{2,1,0:T(8,128)(2,1)} async-done(((bf16[128,8,768]{2,1,0:T(8,128)(2,1)}), bf16[128,8,768]{2,1,0:T(8,128)(2,1)}, u32[]{:S(2)}, u32[]{:S(2)}) %all-to-all-start) | async-done | bytes 1572896 | tf_op jit(solution)/shard_map/all_to_all | solution.py:374
  40.6 5.8 %all-to-all-start.1 = ((bf16[128,8,768]{2,1,0:T(8,128)(2,1)}), bf16[128,8,768]{2,1,0:T(8,128)(2,1)}, u32[]{:S(2)}, u32[]{:S(2)}) async-start(bf16[128,8,768]{2,1,0:T(8,128)(2,1)} %get-tuple-element.33), calls=%async_computation.1 | async-start | bytes 3145728 | tf_op jit(solution)/shard_map/all_to_all | solution.py:374
  46.4 0.6 pad_add_fusion.core_ref
  47.0 0.0 copy-start
  47.0 16.1 %shard_map.149 = (bf16[768,768]{1,0:T(8,128)(2,1)}, f32[4608,128]{1,0:T(8,128)}, bf16[4608,128]{1,0:T(8,128)(2,1)}) custom-call(s32[2]{0:T(128)} %pad_add_fusion.core_ref, bf16[1024,768]{1,0:T(8,128)(2,1)} %bitcast.5.arrived_hbm, bf16[768,768]{1,0:T(8,128)(2,1)} %get-tuple-element.26.near_hbm, bf16[768,1024]{1,0:T(8,128)(2,1)} %get-tuple-element.27.far_hbm, ...), custom_call_target="tpu_custom_call" | custom-call | bytes 17694728 | tf_op jit(solution)/shard_map/pallas_call | solution.py:359
  63.1 1.5 %collective-permute-start = (bf16[4608,128]{1,0:T(8,128)(2,1)}, bf16[4608,128]{1,0:T(8,128)(2,1)S(1)}, u32[]{:S(2)}, u32[]{:S(2)}) collective-permute-start(bf16[4608,128]{1,0:T(8,128)(2,1)} %get-tuple-element.31), channel_id=1, source_target_pairs={{0,16},{16,0},{32,48},{48,32},{64,80},{80,64},{96,112},{112,96},{1... | collective-permute-start | bytes 3538952 | tf_op jit(solution)/shard_map/ppermute | solution.py:381
  64.6 0.0 copy-done
  64.6 0.0 copy-start.2
  64.6 1.3 copy-done.2
  65.9 0.0 copy-start.1
  65.9 1.9 %shard_map.150._ = bf16[128,88,128]{2,1,0:T(8,128)(2,1)S(1)} custom-call(bf16[1024,768]{1,0:T(8,128)(2,1)S(1)} %copy-done, bf16[768,768]{1,0:T(8,128)(2,1)S(1)} %copy-done.2), custom_call_target="tpu_custom_call" | custom-call | bytes 5636096 | tf_op jit(solution)/shard_map/pallas_call | solution.py:359
  67.8 0.0 collective-permute-done.other_ref
  67.8 0.0 copy-done.1
  67.8 0.3 shard_map.151
  68.2 0.0 copy-start.3
  68.2 2.2 %all-to-all-done.1 = bf16[128,8,768]{2,1,0:T(8,128)(2,1)} async-done(((bf16[128,8,768]{2,1,0:T(8,128)(2,1)}), bf16[128,8,768]{2,1,0:T(8,128)(2,1)}, u32[]{:S(2)}, u32[]{:S(2)}) %all-to-all-start.1) | async-done | bytes 1572896 | tf_op jit(solution)/shard_map/all_to_all | solution.py:374
  70.3 44.4 %all_to_all.20.mail_ref = bf16[128,88,128]{2,1,0:T(8,128)(2,1)S(1)} all-to-all(bf16[128,88,128]{2,1,0:T(8,128)(2,1)S(1)} %shard_map.151), channel_id=1, replica_groups=mesh['px'=8,'py'=16] {'px','py'}, dimensions={0} | all-to-all | bytes 5767168 | tf_op jit(solution)/shard_map/all_to_all | solution.py:374
  114.7 0.0 copy-done.3
  114.7 1.7 %shard_map.152 = (bf16[64,72,128]{2,1,0:T(8,128)(2,1)S(1)}, bf16[128,48,128]{2,1,0:T(8,128)(2,1)}) custom-call(s32[2]{0:T(128)S(1)} %copy-done.3, bf16[128,88,128]{2,1,0:T(8,128)(2,1)S(1)} %all_to_all.20.mail_ref), custom_call_target="tpu_custom_call" | custom-call | bytes 5636104 | tf_op jit(solution)/shard_map/pallas_call | solution.py:359
  116.4 0.0 copy-start.4
  116.5 23.7 %all_to_all.21.mine_ref = bf16[64,72,128]{2,1,0:T(8,128)(2,1)S(1)} all-to-all(bf16[64,72,128]{2,1,0:T(8,128)(2,1)S(1)} %get-tuple-element.37), channel_id=1, replica_groups={{0,1,2,3,4,5,6,7,8,9,10,11,12,13,14,15,32,33,34,35,36,37,38,39,40,41,42..., dimensions={0} | all-to-all | bytes 2359296 | tf_op jit(solution)/shard_map/all_to_all | solution.py:374
  140.2 2.5 %collective-permute-start.1 = (bf16[64,72,128]{2,1,0:T(8,128)(2,1)S(1)}, bf16[64,72,128]{2,1,0:T(8,128)(2,1)S(1)}, u32[]{:S(2)}, u32[]{:S(2)}) collective-permute-start(bf16[64,72,128]{2,1,0:T(8,128)(2,1)S(1)} %all_to_all.21.mine_ref), channel_id=1, source_target_pairs={{0,16},{16,0},{32,48},{48,32},{64,80},{80,64},{96,112},{112,96},{1... | collective-permute-start | bytes 3538952 | tf_op jit(solution)/shard_map/ppermute | solution.py:381
  142.7 0.0 copy-done.4
  142.7 2.8 %compare_select_fusion = bf16[1024,768]{1,0:T(8,128)(2,1)} fusion(bf16[1024,768]{1,0:T(8,128)(2,1)S(1)} %copy-done.4, bf16[128,8,768]{2,1,0:T(8,128)(2,1)} %all-to-all-done.1), kind=kLoop, calls=%fused_computation | loop fusion | flops 1572864 | bytes 4718592 | tf_op jit(solution)/shard_map/jit(_where)/select_n | solution.py:495
  145.5 0.0 collective-permute-done.1.other_ref
  145.5 2.9 %shard_map.153 = (f32[768,768]{1,0:T(8,128)}, f32[768,768]{1,0:T(8,128)}) custom-call(s32[2]{0:T(128)S(1)} %copy-done.3, bf16[64,72,128]{2,1,0:T(8,128)(2,1)S(1)} %all_to_all.21.mine_ref, bf16[64,72,128]{2,1,0:T(8,128)(2,1)S(1)} %collective-permute-done.1.other_ref), custom_call_target="tpu_custom_call" | custom-call | bytes 7077896 | tf_op jit(solution)/shard_map/pallas_call | solution.py:359
Async XLA Ops:
  4.8 35.7 %all-to-all-start = ((bf16[128,8,768]{2,1,0:T(8,128)(2,1)}), bf16[128,8,768]{2,1,0:T(8,128)(2,1)}, u32[]{:S(2)}, u32[]{:S(2)}) async-start(bf16[128,8,768]{2,1,0:T(8,128)(2,1)} %bitcast.16), calls=%async_computation | async-start | bytes 3145728 | tf_op jit(solution)/shard_map/all_to_all | solution.py:374
  40.6 29.8 %all-to-all-start.1 = ((bf16[128,8,768]{2,1,0:T(8,128)(2,1)}), bf16[128,8,768]{2,1,0:T(8,128)(2,1)}, u32[]{:S(2)}, u32[]{:S(2)}) async-start(bf16[128,8,768]{2,1,0:T(8,128)(2,1)} %get-tuple-element.33), calls=%async_computation.1 | async-start | bytes 3145728 | tf_op jit(solution)/shard_map/all_to_all | solution.py:374
  47.0 17.6 %copy-start = (bf16[1024,768]{1,0:T(8,128)(2,1)S(1)}, bf16[1024,768]{1,0:T(8,128)(2,1)}, u32[]{:S(2)}) copy-start(bf16[1024,768]{1,0:T(8,128)(2,1)} %get-tuple-element.23.picks_hbm) | copy-start | bytes 4718596
  63.1 4.7 %collective-permute-start = (bf16[4608,128]{1,0:T(8,128)(2,1)}, bf16[4608,128]{1,0:T(8,128)(2,1)S(1)}, u32[]{:S(2)}, u32[]{:S(2)}) collective-permute-start(bf16[4608,128]{1,0:T(8,128)(2,1)} %get-tuple-element.31), channel_id=1, source_target_pairs={{0,16},{16,0},{32,48},{48,32},{64,80},{80,64},{96,112},{112,96},{1... | collective-permute-start | bytes 3538952 | tf_op jit(solution)/shard_map/ppermute | solution.py:381
  64.6 1.3 copy-start.2
  65.9 1.9 %copy-start.1 = (f32[4608,128]{1,0:T(8,128)S(1)}, f32[4608,128]{1,0:T(8,128)}, u32[]{:S(2)}) copy-start(f32[4608,128]{1,0:T(8,128)} %get-tuple-element.30.keep_ref) | copy-start | bytes 7077892
  68.2 46.6 %copy-start.3 = (s32[2]{0:T(128)S(1)}, s32[2]{0:T(128)}, u32[]{:S(2)}) copy-start(s32[2]{0:T(128)} %pad_add_fusion.core_ref) | copy-start | bytes 28
  116.4 26.3 %copy-start.4 = (bf16[1024,768]{1,0:T(8,128)(2,1)S(1)}, bf16[1024,768]{1,0:T(8,128)(2,1)}, u32[]{:S(2)}) copy-start(bf16[1024,768]{1,0:T(8,128)(2,1)} %get-tuple-element.22) | copy-start | bytes 4718596
  140.2 5.3 %collective-permute-start.1 = (bf16[64,72,128]{2,1,0:T(8,128)(2,1)S(1)}, bf16[64,72,128]{2,1,0:T(8,128)(2,1)S(1)}, u32[]{:S(2)}, u32[]{:S(2)}) collective-permute-start(bf16[64,72,128]{2,1,0:T(8,128)(2,1)S(1)} %all_to_all.21.mine_ref), channel_id=1, source_target_pairs={{0,16},{16,0},{32,48},{48,32},{64,80},{80,64},{96,112},{112,96},{1... | collective-permute-start | bytes 3538952 | tf_op jit(solution)/shard_map/ppermute | solution.py:381

commit v9 on v8

--- a/solution.py
+++ b/solution.py
@@ -232,7 +232,7 @@
     fetches[n - 1].wait()
     part_two = mm(agg_two, out_grad[...], ((0,), (0,)))
     part_one = mm(first_agg[...], pre_grad[...], ((0,), (0,)))
-    first = core_ref[0] == 0
+    first = (core_ref[0] & 1) == 0
     for k in range(width // LANES):
         at = slice(k * LANES, (k + 1) * LANES)
         one, two = part_one[:, at], part_two[:, at]
@@ -292,11 +292,11 @@
         both = jnp.concatenate([one, two], axis=0).astype(out_ref.dtype)
         out_ref[...] = jnp.broadcast_to(both[None], (chips, share, LANES))
 
-    @pl.when(core_ref[1] == 0)
+    @pl.when(core_ref[0] < 2)
     def _():
         give(sums[0], sums[1][:rest])
 
-    @pl.when(core_ref[1] != 0)
+    @pl.when(core_ref[0] >= 2)
     def _():
         give(sums[0][size - rest :], sums[1])
 
@@ -338,11 +338,11 @@
         for save in saves:
             save.wait()
 
-    @pl.when(core_ref[0] == 0)
+    @pl.when((core_ref[0] & 1) == 0)
     def _():
         fill((mine_ref, other_ref))
 
-    @pl.when(core_ref[0] != 0)
+    @pl.when((core_ref[0] & 1) != 0)
     def _():
         fill((other_ref, mine_ref))
 
@@ -401,7 +401,7 @@
     slots = send_rows.shape[2]
     boundary = parts * slots
     shape = jax.ShapeDtypeStruct
-    core = jnp.stack([lax.axis_index("px") % 2, lax.axis_index("py") % 2]).astype(jnp.int32)
+    core = ((lax.axis_index("px") & 1) + 2 * (lax.axis_index("py") & 1)).astype(jnp.int32).reshape(1)
     n_z, n_py = lax.axis_size("px") // 2, lax.axis_size("py")
 
     square, square32 = shape((own, width), bf16), shape((own, width), f32)

time: 149 us -> 147 us (0.987)
  Pallas kernels: 38.7 us -> 36.9 us
    pallas_call x7, Pallas kernels: 38.7 us -> 36.9 us  [run(): pl.pallas_call(kernel, out_shape=out_shape, in_specs=[SMEM] * scalars + [...]
where the time goes in v9:
time: 147 us; the launch traced here: 146 us
  blocking collectives  66.8 us (45%)
  Pallas kernels  36.9 us (25%)
  starting transfers between devices  21.8 us (15%)
  waiting for transfers between devices  15 us (10%)
  other arithmetic  2.75 us (2%)
  between operations  1.55 us (1%)
    all_to_all x2, blocking collectives, trade(): lax.all_to_all(value, BOTH, split_axis=0, concat_axis=0, tiled=True, axis...  66.8 us
    pallas_call x7, Pallas kernels, run(): pl.pallas_call(kernel, out_shape=out_shape, in_specs=[SMEM] * scalars + [...  36.9 us
    all_to_all x2, starting transfers between devices, trade(): lax.all_to_all(value, BOTH, split_axis=0, concat_axis=0, tiled=True, axis...  17.8 us
    all_to_all x2, waiting for transfers between devices, trade(): lax.all_to_all(value, BOTH, split_axis=0, concat_axis=0, tiled=True, axis...  15 us
    ppermute x2, starting transfers between devices, sibling(): return lax.ppermute(value, 'px', [(i, i ^ 1) for i in range(n)])  4.05 us
  transfers between devices with their start and end apart: 4, of which 2 were waited for; matrix products, arithmetic and copies ran while one was open for 2% of the time, Pallas kernels for 20%

profile of v9, /device:TPU:1, one launch (start us, length us, event | category | flops | bytes accessed | tf_op | source)
XLA Modules:
  0.0 146.1 jit_solution(14445682549275968011)
XLA Ops:
  0.6 4.2 %shard_map.147 = (bf16[1024,768]{1,0:T(8,128)(2,1)}, bf16[1024,768]{1,0:T(8,128)(2,1)}) custom-call(s32[8,128]{1,0:T(8,128)} %bitcast.16, s32[1,128]{1,0:T(1,128)} %counts_ref.1, bf16[768,768]{1,0:T(8,128)(2,1)} %features_hbm.3), custom_call_target="tpu_custom_call" | custom-call | bytes 4329984 | tf_op jit(solution)/shard_map/pallas_call | solution.py:359
  4.8 11.9 %all-to-all-start = ((bf16[128,8,768]{2,1,0:T(8,128)(2,1)}), bf16[128,8,768]{2,1,0:T(8,128)(2,1)}, u32[]{:S(2)}, u32[]{:S(2)}) async-start(bf16[128,8,768]{2,1,0:T(8,128)(2,1)} %bitcast.15), calls=%async_computation | async-start | bytes 3145728 | tf_op jit(solution)/shard_map/all_to_all | solution.py:374
  17.4 11.6 %shard_map.148 = (bf16[768,768]{1,0:T(8,128)(2,1)}, bf16[768,1024]{1,0:T(8,128)(2,1)}, f32[768,768]{1,0:T(8,128)}, f32[768,768]{1,0:T(8,128)}, bf16[128,8,768]{2,1,0:T(8,128)(2,1)}) custom-call(s32[32]{0:T(128)} %bitcast.17, s32[32]{0:T(128)} %bitcast.18, s32[1]{0:T(128)S(6)} %copy.18.count_ref, bf16[32,128,128]{2,1,0:T(8,128)(2,1)} %tiles_hbm.1, ...), custom_call_target="tpu_custom_call" | custom-call | bytes 16777476 | tf_op jit(solution)/shard_map/pallas_call | solution.py:359
  29.1 11.5 %all-to-all-done = bf16[128,8,768]{2,1,0:T(8,128)(2,1)} async-done(((bf16[128,8,768]{2,1,0:T(8,128)(2,1)}), bf16[128,8,768]{2,1,0:T(8,128)(2,1)}, u32[]{:S(2)}, u32[]{:S(2)}) %all-to-all-start) | async-done | bytes 1572896 | tf_op jit(solution)/shard_map/all_to_all | solution.py:374
  40.6 5.9 %all-to-all-start.1 = ((bf16[128,8,768]{2,1,0:T(8,128)(2,1)}), bf16[128,8,768]{2,1,0:T(8,128)(2,1)}, u32[]{:S(2)}, u32[]{:S(2)}) async-start(bf16[128,8,768]{2,1,0:T(8,128)(2,1)} %get-tuple-element.33), calls=%async_computation.1 | async-start | bytes 3145728 | tf_op jit(solution)/shard_map/all_to_all | solution.py:374
  46.4 0.0 copy-start
  46.4 15.4 %shard_map.149 = (bf16[768,768]{1,0:T(8,128)(2,1)}, f32[4608,128]{1,0:T(8,128)}, bf16[4608,128]{1,0:T(8,128)(2,1)}) custom-call(s32[1]{0:T(128)} %bitcast.core_ref, bf16[1024,768]{1,0:T(8,128)(2,1)} %bitcast.4.arrived_hbm, bf16[768,768]{1,0:T(8,128)(2,1)} %get-tuple-element.26.near_hbm, bf16[768,1024]{1,0:T(8,128)(2,1)} %get-tuple-element.27.far_hbm, ...), custom_call_target="tpu_custom_call" | custom-call | bytes 17694724 | tf_op jit(solution)/shard_map/pallas_call | solution.py:359
  61.9 1.5 %collective-permute-start = (bf16[4608,128]{1,0:T(8,128)(2,1)}, bf16[4608,128]{1,0:T(8,128)(2,1)S(1)}, u32[]{:S(2)}, u32[]{:S(2)}) collective-permute-start(bf16[4608,128]{1,0:T(8,128)(2,1)} %get-tuple-element.31), channel_id=1, source_target_pairs={{0,16},{16,0},{32,48},{48,32},{64,80},{80,64},{96,112},{112,96},{1... | collective-permute-start | bytes 3538952 | tf_op jit(solution)/shard_map/ppermute | solution.py:381
  63.4 0.0 copy-done
  63.4 0.0 copy-start.2
  63.4 1.3 copy-done.2
  64.6 0.0 copy-start.1
  64.7 1.9 %shard_map.150._ = bf16[128,88,128]{2,1,0:T(8,128)(2,1)S(1)} custom-call(bf16[1024,768]{1,0:T(8,128)(2,1)S(1)} %copy-done, bf16[768,768]{1,0:T(8,128)(2,1)S(1)} %copy-done.2), custom_call_target="tpu_custom_call" | custom-call | bytes 5636096 | tf_op jit(solution)/shard_map/pallas_call | solution.py:359
  66.5 0.0 collective-permute-done.other_ref
  66.5 0.0 copy-done.1
  66.5 0.3 shard_map.151
  66.9 3.5 %all-to-all-done.1 = bf16[128,8,768]{2,1,0:T(8,128)(2,1)} async-done(((bf16[128,8,768]{2,1,0:T(8,128)(2,1)}), bf16[128,8,768]{2,1,0:T(8,128)(2,1)}, u32[]{:S(2)}, u32[]{:S(2)}) %all-to-all-start.1) | async-done | bytes 1572896 | tf_op jit(solution)/shard_map/all_to_all | solution.py:374
  70.3 43.1 %all_to_all.20.mail_ref = bf16[128,88,128]{2,1,0:T(8,128)(2,1)S(1)} all-to-all(bf16[128,88,128]{2,1,0:T(8,128)(2,1)S(1)} %shard_map.151), channel_id=1, replica_groups=mesh['px'=8,'py'=16] {'px','py'}, dimensions={0} | all-to-all | bytes 5767168 | tf_op jit(solution)/shard_map/all_to_all | solution.py:374
  113.5 1.2 shard_map.152
  114.6 0.0 copy-start.3
  114.6 23.7 %all_to_all.21.mine_ref = bf16[64,72,128]{2,1,0:T(8,128)(2,1)S(1)} all-to-all(bf16[64,72,128]{2,1,0:T(8,128)(2,1)S(1)} %get-tuple-element.37), channel_id=1, replica_groups={{0,1,2,3,4,5,6,7,8,9,10,11,12,13,14,15,32,33,34,35,36,37,38,39,40,41,42..., dimensions={0} | all-to-all | bytes 2359296 | tf_op jit(solution)/shard_map/all_to_all | solution.py:374
  138.4 2.5 %collective-permute-start.1 = (bf16[64,72,128]{2,1,0:T(8,128)(2,1)S(1)}, bf16[64,72,128]{2,1,0:T(8,128)(2,1)S(1)}, u32[]{:S(2)}, u32[]{:S(2)}) collective-permute-start(bf16[64,72,128]{2,1,0:T(8,128)(2,1)S(1)} %all_to_all.21.mine_ref), channel_id=1, source_target_pairs={{0,16},{16,0},{32,48},{48,32},{64,80},{80,64},{96,112},{112,96},{1... | collective-permute-start | bytes 3538952 | tf_op jit(solution)/shard_map/ppermute | solution.py:381
  140.9 0.0 copy-done.3
  140.9 2.8 %compare_select_fusion = bf16[1024,768]{1,0:T(8,128)(2,1)} fusion(bf16[1024,768]{1,0:T(8,128)(2,1)S(1)} %copy-done.3, bf16[128,8,768]{2,1,0:T(8,128)(2,1)} %all-to-all-done.1), kind=kLoop, calls=%fused_computation | loop fusion | flops 1572864 | bytes 4718592 | tf_op jit(solution)/shard_map/jit(_where)/select_n | solution.py:495
  143.6 0.0 collective-permute-done.1.other_ref
  143.7 2.3 %shard_map.153 = (f32[768,768]{1,0:T(8,128)}, f32[768,768]{1,0:T(8,128)}) custom-call(s32[1]{0:T(128)} %bitcast.core_ref, bf16[64,72,128]{2,1,0:T(8,128)(2,1)S(1)} %all_to_all.21.mine_ref, bf16[64,72,128]{2,1,0:T(8,128)(2,1)S(1)} %collective-permute-done.1.other_ref), custom_call_target="tpu_custom_call" | custom-call | bytes 7077892 | tf_op jit(solution)/shard_map/pallas_call | solution.py:359
Async XLA Ops:
  4.8 35.7 %all-to-all-start = ((bf16[128,8,768]{2,1,0:T(8,128)(2,1)}), bf16[128,8,768]{2,1,0:T(8,128)(2,1)}, u32[]{:S(2)}, u32[]{:S(2)}) async-start(bf16[128,8,768]{2,1,0:T(8,128)(2,1)} %bitcast.15), calls=%async_computation | async-start | bytes 3145728 | tf_op jit(solution)/shard_map/all_to_all | solution.py:374
  40.6 29.8 %all-to-all-start.1 = ((bf16[128,8,768]{2,1,0:T(8,128)(2,1)}), bf16[128,8,768]{2,1,0:T(8,128)(2,1)}, u32[]{:S(2)}, u32[]{:S(2)}) async-start(bf16[128,8,768]{2,1,0:T(8,128)(2,1)} %get-tuple-element.33), calls=%async_computation.1 | async-start | bytes 3145728 | tf_op jit(solution)/shard_map/all_to_all | solution.py:374
  46.4 17.0 %copy-start = (bf16[1024,768]{1,0:T(8,128)(2,1)S(1)}, bf16[1024,768]{1,0:T(8,128)(2,1)}, u32[]{:S(2)}) copy-start(bf16[1024,768]{1,0:T(8,128)(2,1)} %get-tuple-element.23.picks_hbm) | copy-start | bytes 4718596
  61.9 4.7 %collective-permute-start = (bf16[4608,128]{1,0:T(8,128)(2,1)}, bf16[4608,128]{1,0:T(8,128)(2,1)S(1)}, u32[]{:S(2)}, u32[]{:S(2)}) collective-permute-start(bf16[4608,128]{1,0:T(8,128)(2,1)} %get-tuple-element.31), channel_id=1, source_target_pairs={{0,16},{16,0},{32,48},{48,32},{64,80},{80,64},{96,112},{112,96},{1... | collective-permute-start | bytes 3538952 | tf_op jit(solution)/shard_map/ppermute | solution.py:381
  63.4 1.3 copy-start.2
  64.6 1.9 %copy-start.1 = (f32[4608,128]{1,0:T(8,128)S(1)}, f32[4608,128]{1,0:T(8,128)}, u32[]{:S(2)}) copy-start(f32[4608,128]{1,0:T(8,128)} %get-tuple-element.30.keep_ref) | copy-start | bytes 7077892
  114.6 26.3 %copy-start.3 = (bf16[1024,768]{1,0:T(8,128)(2,1)S(1)}, bf16[1024,768]{1,0:T(8,128)(2,1)}, u32[]{:S(2)}) copy-start(bf16[1024,768]{1,0:T(8,128)(2,1)} %get-tuple-element.22) | copy-start | bytes 4718596
  138.4 5.3 %collective-permute-start.1 = (bf16[64,72,128]{2,1,0:T(8,128)(2,1)S(1)}, bf16[64,72,128]{2,1,0:T(8,128)(2,1)S(1)}, u32[]{:S(2)}, u32[]{:S(2)}) collective-permute-start(bf16[64,72,128]{2,1,0:T(8,128)(2,1)S(1)} %all_to_all.21.mine_ref), channel_id=1, source_target_pairs={{0,16},{16,0},{32,48},{48,32},{64,80},{80,64},{96,112},{112,96},{1... | collective-permute-start | bytes 3538952 | tf_op jit(solution)/shard_map/ppermute | solution.py:381

commit v10 on v9

--- a/solution.py
+++ b/solution.py
@@ -12,7 +12,7 @@
 LANES = 128
 UNUSED = 2.0**126
 PACK, LOCAL, MAIN = 58, 63, 56
-BOX, PIECE, SUM, FINISH = 20, 12, 8, 16
+BOX, PIECE, SUM, OWN, FINISH = 20, 12, 8, 20, 16
 VMEM = pl.BlockSpec(memory_space=pltpu.VMEM)
 HBM = pl.BlockSpec(memory_space=pltpu.HBM)
 SMEM = pl.BlockSpec(memory_space=pltpu.SMEM)
@@ -304,16 +304,14 @@
         save.wait()
 
 
-def finish_kernel(scale, size, n_py, core_ref, mine_ref, other_ref, one_hbm, two_hbm, one, two, sems):
-    chips, share = mine_ref.shape[:2]
+def fill_half(scale, size, n_py, c, source_ref, one, two, one_hbm, two_hbm, sems):
+    chips, share = source_ref.shape[:2]
     rest = share - size
     width = one.shape[0]
-
-    def fill(sources):
-        saves = []
-        for q in range(2 * chips):
-            row, py = divmod(q, n_py)
-            z, c = divmod(row, 2)
+    saves = []
+    for z in range(chips // n_py):
+        first = (z * 2 + c) * n_py
+        for q in range(first, first + n_py):
             pair, odd = divmod(q, 2)
             spans = ((size, rest, one), (rest, size, two)) if odd else ((0, size, one), (0, rest, two))
             at = 0
@@ -323,28 +321,57 @@
                 while line < end:
                     k, r = divmod(line, width)
                     run = min(end - line, width - r)
-                    value = sources[c][z * n_py + py, at : at + run, :]
+                    value = source_ref[z * n_py + q - first, at : at + run, :]
                     block = slice(k * LANES, (k + 1) * LANES)
                     out[r : r + run, block] = value.astype(jnp.float32) * scale
                     line += run
                     at += run
-            done, before = (pair + 1) * share // width, pair * share // width
-            for k in range(before, done if odd else before):
-                block = slice(k * LANES, (k + 1) * LANES)
-                saves += copies(
-                    sems.at[pl.ds(2 * k, 2)],
-                    [(one.at[:, block], one_hbm.at[:, block]), (two.at[:, block], two_hbm.at[:, block])],
-                )
-        for save in saves:
-            save.wait()
-
-    @pl.when((core_ref[0] & 1) == 0)
-    def _():
-        fill((mine_ref, other_ref))
-
-    @pl.when((core_ref[0] & 1) != 0)
-    def _():
-        fill((other_ref, mine_ref))
+        line, end = first * share // 2, (first + n_py) * share // 2
+        while line < end:
+            k, r = divmod(line, width)
+            run = min(end - line, width - r)
+            rows, block = slice(r, r + run), slice(k * LANES, (k + 1) * LANES)
+            saves += copies(
+                sems.at[pl.ds(len(saves), 2)],
+                [
+                    (one.at[rows, block], one_hbm.at[rows, block]),
+                    (two.at[rows, block], two_hbm.at[rows, block]),
+                ],
+            )
+            line += run
+    for save in saves:
+        save.wait()
+
+
+def own_half_kernel(
+    scale, size, n_py, core_ref, mine_ref, sent_hbm, grads_hbm, one_hbm, two_hbm, next_hbm, one, two, sent, grads, sems
+):
+    fetches = copies(sems, [(sent_hbm, sent), (grads_hbm, grads)])
+    for c in range(2):
+
+        @pl.when((core_ref[0] & 1) == c)
+        def _():
+            fill_half(scale, size, n_py, c, mine_ref, one, two, one_hbm, two_hbm, sems.at[pl.ds(6, 16)])
+
+    for fetch in fetches:
+        fetch.wait()
+    saves = []
+    step = grads.shape[0] // 4
+    for k in range(4):
+        at = pl.ds(k * step, step)
+        used = sent[at, :].astype(jnp.float32) != UNUSED
+        grads[at, :] = jnp.where(used, grads[at, :].astype(jnp.float32), 0.0).astype(grads.dtype)
+        saves += copies(sems.at[pl.ds(2 + k, 1)], [(grads.at[at, :], next_hbm.at[at, :])])
+    for save in saves:
+        save.wait()
+
+
+def other_half_kernel(scale, size, n_py, core_ref, other_ref, _, __, one_hbm, two_hbm, one, two, sems):
+    for c in range(2):
+
+        @pl.when((core_ref[0] & 1) != c)
+        def _():
+            fill_half(scale, size, n_py, c, other_ref, one, two, one_hbm, two_hbm, sems)
 
 
 def in_vmem(*refs):
@@ -491,19 +518,29 @@
     next_hidden = jnp.swapaxes(next_hidden, 1, 2).reshape(boundary, width)
     same_core = [[(2 * z + c) * n_py + i for z in range(n_z) for i in range(n_py)] for c in range(2)]
     mine = trade(mine, same_core)
-    grads = grads.reshape(boundary, width)
-    next_grad = jnp.where(outgoing == UNUSED, jnp.zeros_like(grads), grads)
     scale = 1.0 / math.sqrt(own * parts)
-    one, two = call(
-        functools.partial(finish_kernel, scale, size, n_py),
-        (shape((width, width), f32),) * 2,
-        1,
-        in_vmem(*(shape((width, width), f32),) * 2) + semaphores(2 * (width // LANES)),
-        None,
-        FINISH,
+    whole = shape((width, width), f32)
+    other = sibling(mine)
+    one, two, next_grad = call(
+        functools.partial(own_half_kernel, scale, size, n_py),
+        (whole, whole, slab),
+        1,
+        in_vmem(whole, whole, slab, slab) + semaphores(22),
+        1,
+        OWN,
         None,
         HBM,
-    )(core, mine, sibling(mine))
+    )(core, mine, outgoing, grads.reshape(boundary, width))
+    one, two = call(
+        functools.partial(other_half_kernel, scale, size, n_py),
+        (whole, whole),
+        1,
+        in_vmem(whole, whole) + semaphores(16),
+        1,
+        FINISH,
+        {2: 0, 3: 1},
+        HBM,
+    )(core, other, one, two)
 
     return next_hidden, next_grad, one, two
 

time: 147 us -> 147 us (level)
  Pallas kernels: 36.9 us -> 40 us
  other arithmetic: 2.75 us -> 0 us
    pallas_call x7 -> x8, Pallas kernels: 36.9 us -> 40 us  [run(): pl.pallas_call(kernel, out_shape=out_shape, in_specs=[SMEM] * scalars + [...]
    select_n x1 -> x0, other arithmetic: 2.75 us -> none  [local(): next_grad = jnp.where(outgoing == UNUSED, jnp.zeros_like(grads), grads)]
  transfers between devices with their start and end apart: 4 -> 4, of which waited for: 2 -> 2; matrix products, arithmetic and copies ran while one was open for 2% -> 0% of each run, Pallas kernels for 20% -> 23%
where the time goes in v10:
time: 147 us; the launch traced here: 146 us
  blocking collectives  66.8 us (45%)
  Pallas kernels  40 us (27%)
  starting transfers between devices  21.8 us (15%)
  waiting for transfers between devices  15 us (10%)
  between operations  1.56 us (1%)
    all_to_all x2, blocking collectives, trade(): lax.all_to_all(value, BOTH, split_axis=0, concat_axis=0, tiled=True, axis...  66.8 us
    pallas_call x8, Pallas kernels, run(): pl.pallas_call(kernel, out_shape=out_shape, in_specs=[SMEM] * scalars + [...  40 us
    all_to_all x2, starting transfers between devices, trade(): lax.all_to_all(value, BOTH, split_axis=0, concat_axis=0, tiled=True, axis...  17.8 us
    all_to_all x2, waiting for transfers between devices, trade(): lax.all_to_all(value, BOTH, split_axis=0, concat_axis=0, tiled=True, axis...  15 us
    ppermute x2, starting transfers between devices, sibling(): return lax.ppermute(value, 'px', [(i, i ^ 1) for i in range(n)])  4.05 us
  transfers between devices with their start and end apart: 4, of which 2 were waited for; matrix products, arithmetic and copies ran while one was open for 0% of the time, Pallas kernels for 23%

profile of v10, /device:TPU:1, one launch (start us, length us, event | category | flops | bytes accessed | tf_op | source)
XLA Modules:
  0.0 146.4 jit_solution(9327061824614644494)
XLA Ops:
  0.6 4.2 %shard_map.147 = (bf16[1024,768]{1,0:T(8,128)(2,1)}, bf16[1024,768]{1,0:T(8,128)(2,1)}) custom-call(s32[8,128]{1,0:T(8,128)} %bitcast.15, s32[1,128]{1,0:T(1,128)} %counts_ref.1, bf16[768,768]{1,0:T(8,128)(2,1)} %features_hbm.3), custom_call_target="tpu_custom_call" | custom-call | bytes 4329984 | tf_op jit(solution)/shard_map/pallas_call | solution.py:386
  4.8 11.9 %all-to-all-start = ((bf16[128,8,768]{2,1,0:T(8,128)(2,1)}), bf16[128,8,768]{2,1,0:T(8,128)(2,1)}, u32[]{:S(2)}, u32[]{:S(2)}) async-start(bf16[128,8,768]{2,1,0:T(8,128)(2,1)} %bitcast.14), calls=%async_computation | async-start | bytes 3145728 | tf_op jit(solution)/shard_map/all_to_all | solution.py:401
  17.4 11.6 %shard_map.148 = (bf16[768,768]{1,0:T(8,128)(2,1)}, bf16[768,1024]{1,0:T(8,128)(2,1)}, f32[768,768]{1,0:T(8,128)}, f32[768,768]{1,0:T(8,128)}, bf16[128,8,768]{2,1,0:T(8,128)(2,1)}) custom-call(s32[32]{0:T(128)} %bitcast.16, s32[32]{0:T(128)} %bitcast.17, s32[1]{0:T(128)S(6)} %copy.22.count_ref, bf16[32,128,128]{2,1,0:T(8,128)(2,1)} %tiles_hbm.1, ...), custom_call_target="tpu_custom_call" | custom-call | bytes 16777476 | tf_op jit(solution)/shard_map/pallas_call | solution.py:386
  29.1 11.5 %all-to-all-done = bf16[128,8,768]{2,1,0:T(8,128)(2,1)} async-done(((bf16[128,8,768]{2,1,0:T(8,128)(2,1)}), bf16[128,8,768]{2,1,0:T(8,128)(2,1)}, u32[]{:S(2)}, u32[]{:S(2)}) %all-to-all-start) | async-done | bytes 1572896 | tf_op jit(solution)/shard_map/all_to_all | solution.py:401
  40.6 5.8 %all-to-all-start.1 = ((bf16[128,8,768]{2,1,0:T(8,128)(2,1)}), bf16[128,8,768]{2,1,0:T(8,128)(2,1)}, u32[]{:S(2)}, u32[]{:S(2)}) async-start(bf16[128,8,768]{2,1,0:T(8,128)(2,1)} %get-tuple-element.36), calls=%async_computation.1 | async-start | bytes 3145728 | tf_op jit(solution)/shard_map/all_to_all | solution.py:401
  46.4 0.0 copy-start.1
  46.4 15.4 %shard_map.149 = (bf16[768,768]{1,0:T(8,128)(2,1)}, f32[4608,128]{1,0:T(8,128)}, bf16[4608,128]{1,0:T(8,128)(2,1)}) custom-call(s32[1]{0:T(128)} %bitcast.core_ref, bf16[1024,768]{1,0:T(8,128)(2,1)} %bitcast.4.arrived_hbm, bf16[768,768]{1,0:T(8,128)(2,1)} %get-tuple-element.29.near_hbm, bf16[768,1024]{1,0:T(8,128)(2,1)} %get-tuple-element.30.far_hbm, ...), custom_call_target="tpu_custom_call" | custom-call | bytes 17694724 | tf_op jit(solution)/shard_map/pallas_call | solution.py:386
  61.8 1.5 %collective-permute-start = (bf16[4608,128]{1,0:T(8,128)(2,1)}, bf16[4608,128]{1,0:T(8,128)(2,1)S(1)}, u32[]{:S(2)}, u32[]{:S(2)}) collective-permute-start(bf16[4608,128]{1,0:T(8,128)(2,1)} %get-tuple-element.34), channel_id=1, source_target_pairs={{0,16},{16,0},{32,48},{48,32},{64,80},{80,64},{96,112},{112,96},{1... | collective-permute-start | bytes 3538952 | tf_op jit(solution)/shard_map/ppermute | solution.py:408
  63.4 0.0 copy-done.1
  63.4 0.0 copy-start.3
  63.4 1.3 copy-done.3
  64.6 0.0 copy-start.2
  64.6 1.9 %shard_map.150._ = bf16[128,88,128]{2,1,0:T(8,128)(2,1)S(1)} custom-call(bf16[1024,768]{1,0:T(8,128)(2,1)S(1)} %copy-done.1, bf16[768,768]{1,0:T(8,128)(2,1)S(1)} %copy-done.3), custom_call_target="tpu_custom_call" | custom-call | bytes 5636096 | tf_op jit(solution)/shard_map/pallas_call | solution.py:386
  66.5 0.0 collective-permute-done.other_ref
  66.5 0.0 copy-done.2
  66.5 0.3 shard_map.151
  66.9 3.5 %all-to-all-done.1 = bf16[128,8,768]{2,1,0:T(8,128)(2,1)} async-done(((bf16[128,8,768]{2,1,0:T(8,128)(2,1)}), bf16[128,8,768]{2,1,0:T(8,128)(2,1)}, u32[]{:S(2)}, u32[]{:S(2)}) %all-to-all-start.1) | async-done | bytes 1572896 | tf_op jit(solution)/shard_map/all_to_all | solution.py:401
  70.3 43.1 %all_to_all.20.mail_ref = bf16[128,88,128]{2,1,0:T(8,128)(2,1)S(1)} all-to-all(bf16[128,88,128]{2,1,0:T(8,128)(2,1)S(1)} %shard_map.151), channel_id=1, replica_groups=mesh['px'=8,'py'=16] {'px','py'}, dimensions={0} | all-to-all | bytes 5767168 | tf_op jit(solution)/shard_map/all_to_all | solution.py:401
  113.5 1.2 shard_map.152
  114.6 0.0 copy-start
  114.6 23.7 %all_to_all.21.mine_ref = bf16[64,72,128]{2,1,0:T(8,128)(2,1)S(1)} all-to-all(bf16[64,72,128]{2,1,0:T(8,128)(2,1)S(1)} %get-tuple-element.39), channel_id=1, replica_groups={{0,1,2,3,4,5,6,7,8,9,10,11,12,13,14,15,32,33,34,35,36,37,38,39,40,41,42..., dimensions={0} | all-to-all | bytes 2359296 | tf_op jit(solution)/shard_map/all_to_all | solution.py:401
  138.4 2.5 %collective-permute-start.1 = (bf16[64,72,128]{2,1,0:T(8,128)(2,1)S(1)}, bf16[64,72,128]{2,1,0:T(8,128)(2,1)S(1)}, u32[]{:S(2)}, u32[]{:S(2)}) collective-permute-start(bf16[64,72,128]{2,1,0:T(8,128)(2,1)S(1)} %all_to_all.21.mine_ref), channel_id=1, source_target_pairs={{0,16},{16,0},{32,48},{48,32},{64,80},{80,64},{96,112},{112,96},{1... | collective-permute-start | bytes 3538952 | tf_op jit(solution)/shard_map/ppermute | solution.py:408
  140.9 0.0 copy-done
  140.9 3.8 %shard_map.153 = (f32[768,768]{1,0:T(8,128)}, f32[768,768]{1,0:T(8,128)}, bf16[1024,768]{1,0:T(8,128)(2,1)}) custom-call(s32[1]{0:T(128)} %bitcast.core_ref, bf16[64,72,128]{2,1,0:T(8,128)(2,1)S(1)} %all_to_all.21.mine_ref, bf16[1024,768]{1,0:T(8,128)(2,1)S(1)} %copy-done, bf16[1024,768]{1,0:T(8,128)(2,1)} %bitcast.10.grads_hbm), custom_call_target="tpu_custom_call" | custom-call | bytes 10616836 | tf_op jit(solution)/shard_map/pallas_call | solution.py:386
  144.7 0.0 collective-permute-done.1.other_ref
  144.7 1.6 %shard_map.154 = (f32[768,768]{1,0:T(8,128)}, f32[768,768]{1,0:T(8,128)}) custom-call(s32[1]{0:T(128)} %bitcast.core_ref, bf16[64,72,128]{2,1,0:T(8,128)(2,1)S(1)} %collective-permute-done.1.other_ref, f32[768,768]{1,0:T(8,128)} %get-tuple-element.42._, f32[768,768]{1,0:T(8,128)} %get-tuple-element.43.__), custom_call_target="tpu_custom_call", output_to_operand_aliasing={{0}: (2, {}), {1}: (3, {})} | custom-call | bytes 10616836 | tf_op jit(solution)/shard_map/pallas_call | solution.py:386
Async XLA Ops:
  4.8 35.7 %all-to-all-start = ((bf16[128,8,768]{2,1,0:T(8,128)(2,1)}), bf16[128,8,768]{2,1,0:T(8,128)(2,1)}, u32[]{:S(2)}, u32[]{:S(2)}) async-start(bf16[128,8,768]{2,1,0:T(8,128)(2,1)} %bitcast.14), calls=%async_computation | async-start | bytes 3145728 | tf_op jit(solution)/shard_map/all_to_all | solution.py:401
  40.6 29.8 %all-to-all-start.1 = ((bf16[128,8,768]{2,1,0:T(8,128)(2,1)}), bf16[128,8,768]{2,1,0:T(8,128)(2,1)}, u32[]{:S(2)}, u32[]{:S(2)}) async-start(bf16[128,8,768]{2,1,0:T(8,128)(2,1)} %get-tuple-element.36), calls=%async_computation.1 | async-start | bytes 3145728 | tf_op jit(solution)/shard_map/all_to_all | solution.py:401
  46.4 16.9 %copy-start.1 = (bf16[1024,768]{1,0:T(8,128)(2,1)S(1)}, bf16[1024,768]{1,0:T(8,128)(2,1)}, u32[]{:S(2)}) copy-start(bf16[1024,768]{1,0:T(8,128)(2,1)} %get-tuple-element.26.picks_hbm) | copy-start | bytes 4718596
  61.8 4.7 %collective-permute-start = (bf16[4608,128]{1,0:T(8,128)(2,1)}, bf16[4608,128]{1,0:T(8,128)(2,1)S(1)}, u32[]{:S(2)}, u32[]{:S(2)}) collective-permute-start(bf16[4608,128]{1,0:T(8,128)(2,1)} %get-tuple-element.34), channel_id=1, source_target_pairs={{0,16},{16,0},{32,48},{48,32},{64,80},{80,64},{96,112},{112,96},{1... | collective-permute-start | bytes 3538952 | tf_op jit(solution)/shard_map/ppermute | solution.py:408
  63.4 1.3 copy-start.3
  64.6 1.9 %copy-start.2 = (f32[4608,128]{1,0:T(8,128)S(1)}, f32[4608,128]{1,0:T(8,128)}, u32[]{:S(2)}) copy-start(f32[4608,128]{1,0:T(8,128)} %get-tuple-element.33.keep_ref) | copy-start | bytes 7077892
  114.6 26.3 %copy-start = (bf16[1024,768]{1,0:T(8,128)(2,1)S(1)}, bf16[1024,768]{1,0:T(8,128)(2,1)}, u32[]{:S(2)}) copy-start(bf16[1024,768]{1,0:T(8,128)(2,1)} %get-tuple-element.25.sent_hbm) | copy-start | bytes 4718596
  138.4 6.3 %collective-permute-start.1 = (bf16[64,72,128]{2,1,0:T(8,128)(2,1)S(1)}, bf16[64,72,128]{2,1,0:T(8,128)(2,1)S(1)}, u32[]{:S(2)}, u32[]{:S(2)}) collective-permute-start(bf16[64,72,128]{2,1,0:T(8,128)(2,1)S(1)} %all_to_all.21.mine_ref), channel_id=1, source_target_pairs={{0,16},{16,0},{32,48},{48,32},{64,80},{80,64},{96,112},{112,96},{1... | collective-permute-start | bytes 3538952 | tf_op jit(solution)/shard_map/ppermute | solution.py:408

commit v11 on v10

--- a/solution.py
+++ b/solution.py
@@ -304,7 +304,7 @@
         save.wait()
 
 
-def fill_half(scale, size, n_py, c, source_ref, one, two, one_hbm, two_hbm, sems):
+def fill_half(scale, size, n_py, c, source_ref, one, two, one_hbm, two_hbm, sems, meanwhile=None):
     chips, share = source_ref.shape[:2]
     rest = share - size
     width = one.shape[0]
@@ -339,6 +339,8 @@
                 ],
             )
             line += run
+    if meanwhile is not None:
+        saves += meanwhile()
     for save in saves:
         save.wait()
 
@@ -347,23 +349,25 @@
     scale, size, n_py, core_ref, mine_ref, sent_hbm, grads_hbm, one_hbm, two_hbm, next_hbm, one, two, sent, grads, sems
 ):
     fetches = copies(sems, [(sent_hbm, sent), (grads_hbm, grads)])
+
+    def clear():
+        for fetch in fetches:
+            fetch.wait()
+        saves = []
+        step = grads.shape[0] // 4
+        for k in range(4):
+            at = pl.ds(k * step, step)
+            used = sent[at, :].astype(jnp.float32) != UNUSED
+            grads[at, :] = jnp.where(used, grads[at, :].astype(jnp.float32), 0.0).astype(grads.dtype)
+            saves += copies(sems.at[pl.ds(2 + k, 1)], [(grads.at[at, :], next_hbm.at[at, :])])
+        return saves
+
     for c in range(2):
 
         @pl.when((core_ref[0] & 1) == c)
         def _():
-            fill_half(scale, size, n_py, c, mine_ref, one, two, one_hbm, two_hbm, sems.at[pl.ds(6, 16)])
-
-    for fetch in fetches:
-        fetch.wait()
-    saves = []
-    step = grads.shape[0] // 4
-    for k in range(4):
-        at = pl.ds(k * step, step)
-        used = sent[at, :].astype(jnp.float32) != UNUSED
-        grads[at, :] = jnp.where(used, grads[at, :].astype(jnp.float32), 0.0).astype(grads.dtype)
-        saves += copies(sems.at[pl.ds(2 + k, 1)], [(grads.at[at, :], next_hbm.at[at, :])])
-    for save in saves:
-        save.wait()
+            own = sems.at[pl.ds(6, 16)]
+            fill_half(scale, size, n_py, c, mine_ref, one, two, one_hbm, two_hbm, own, clear)
 
 
 def other_half_kernel(scale, size, n_py, core_ref, other_ref, _, __, one_hbm, two_hbm, one, two, sems):

time: 147 us -> 147 us (level)
  no operation moved by 1% of the time
where the time goes in v11:
time: 147 us; the launch traced here: 146 us
  blocking collectives  66.8 us (45%)
  Pallas kernels  40 us (27%)
  starting transfers between devices  21.8 us (15%)
  waiting for transfers between devices  15 us (10%)
  between operations  1.56 us (1%)
    all_to_all x2, blocking collectives, trade(): lax.all_to_all(value, BOTH, split_axis=0, concat_axis=0, tiled=True, axis...  66.8 us
    pallas_call x8, Pallas kernels, run(): pl.pallas_call(kernel, out_shape=out_shape, in_specs=[SMEM] * scalars + [...  40 us
    all_to_all x2, starting transfers between devices, trade(): lax.all_to_all(value, BOTH, split_axis=0, concat_axis=0, tiled=True, axis...  17.8 us
    all_to_all x2, waiting for transfers between devices, trade(): lax.all_to_all(value, BOTH, split_axis=0, concat_axis=0, tiled=True, axis...  15 us
    ppermute x2, starting transfers between devices, sibling(): return lax.ppermute(value, 'px', [(i, i ^ 1) for i in range(n)])  4.05 us
  transfers between devices with their start and end apart: 4, of which 2 were waited for; matrix products, arithmetic and copies ran while one was open for 0% of the time, Pallas kernels for 23%

profile of v11, /device:TPU:1, one launch (start us, length us, event | category | flops | bytes accessed | tf_op | source)
XLA Modules:
  0.0 146.4 jit_solution(16167455866608026975)
XLA Ops:
  0.6 4.2 %shard_map.147 = (bf16[1024,768]{1,0:T(8,128)(2,1)}, bf16[1024,768]{1,0:T(8,128)(2,1)}) custom-call(s32[8,128]{1,0:T(8,128)} %bitcast.15, s32[1,128]{1,0:T(1,128)} %counts_ref.1, bf16[768,768]{1,0:T(8,128)(2,1)} %features_hbm.3), custom_call_target="tpu_custom_call" | custom-call | bytes 4329984 | tf_op jit(solution)/shard_map/pallas_call | solution.py:390
  4.8 11.9 %all-to-all-start = ((bf16[128,8,768]{2,1,0:T(8,128)(2,1)}), bf16[128,8,768]{2,1,0:T(8,128)(2,1)}, u32[]{:S(2)}, u32[]{:S(2)}) async-start(bf16[128,8,768]{2,1,0:T(8,128)(2,1)} %bitcast.14), calls=%async_computation | async-start | bytes 3145728 | tf_op jit(solution)/shard_map/all_to_all | solution.py:405
  17.4 11.6 %shard_map.148 = (bf16[768,768]{1,0:T(8,128)(2,1)}, bf16[768,1024]{1,0:T(8,128)(2,1)}, f32[768,768]{1,0:T(8,128)}, f32[768,768]{1,0:T(8,128)}, bf16[128,8,768]{2,1,0:T(8,128)(2,1)}) custom-call(s32[32]{0:T(128)} %bitcast.16, s32[32]{0:T(128)} %bitcast.17, s32[1]{0:T(128)S(6)} %copy.22.count_ref, bf16[32,128,128]{2,1,0:T(8,128)(2,1)} %tiles_hbm.1, ...), custom_call_target="tpu_custom_call" | custom-call | bytes 16777476 | tf_op jit(solution)/shard_map/pallas_call | solution.py:390
  29.1 11.5 %all-to-all-done = bf16[128,8,768]{2,1,0:T(8,128)(2,1)} async-done(((bf16[128,8,768]{2,1,0:T(8,128)(2,1)}), bf16[128,8,768]{2,1,0:T(8,128)(2,1)}, u32[]{:S(2)}, u32[]{:S(2)}) %all-to-all-start) | async-done | bytes 1572896 | tf_op jit(solution)/shard_map/all_to_all | solution.py:405
  40.6 5.8 %all-to-all-start.1 = ((bf16[128,8,768]{2,1,0:T(8,128)(2,1)}), bf16[128,8,768]{2,1,0:T(8,128)(2,1)}, u32[]{:S(2)}, u32[]{:S(2)}) async-start(bf16[128,8,768]{2,1,0:T(8,128)(2,1)} %get-tuple-element.36), calls=%async_computation.1 | async-start | bytes 3145728 | tf_op jit(solution)/shard_map/all_to_all | solution.py:405
  46.4 0.0 copy-start.1
  46.4 15.4 %shard_map.149 = (bf16[768,768]{1,0:T(8,128)(2,1)}, f32[4608,128]{1,0:T(8,128)}, bf16[4608,128]{1,0:T(8,128)(2,1)}) custom-call(s32[1]{0:T(128)} %bitcast.core_ref, bf16[1024,768]{1,0:T(8,128)(2,1)} %bitcast.4.arrived_hbm, bf16[768,768]{1,0:T(8,128)(2,1)} %get-tuple-element.29.near_hbm, bf16[768,1024]{1,0:T(8,128)(2,1)} %get-tuple-element.30.far_hbm, ...), custom_call_target="tpu_custom_call" | custom-call | bytes 17694724 | tf_op jit(solution)/shard_map/pallas_call | solution.py:390
  61.8 1.5 %collective-permute-start = (bf16[4608,128]{1,0:T(8,128)(2,1)}, bf16[4608,128]{1,0:T(8,128)(2,1)S(1)}, u32[]{:S(2)}, u32[]{:S(2)}) collective-permute-start(bf16[4608,128]{1,0:T(8,128)(2,1)} %get-tuple-element.34), channel_id=1, source_target_pairs={{0,16},{16,0},{32,48},{48,32},{64,80},{80,64},{96,112},{112,96},{1... | collective-permute-start | bytes 3538952 | tf_op jit(solution)/shard_map/ppermute | solution.py:412
  63.4 0.0 copy-done.1
  63.4 0.0 copy-start.3
  63.4 1.3 copy-done.3
  64.6 0.0 copy-start.2
  64.6 1.9 %shard_map.150._ = bf16[128,88,128]{2,1,0:T(8,128)(2,1)S(1)} custom-call(bf16[1024,768]{1,0:T(8,128)(2,1)S(1)} %copy-done.1, bf16[768,768]{1,0:T(8,128)(2,1)S(1)} %copy-done.3), custom_call_target="tpu_custom_call" | custom-call | bytes 5636096 | tf_op jit(solution)/shard_map/pallas_call | solution.py:390
  66.5 0.0 collective-permute-done.other_ref
  66.5 0.0 copy-done.2
  66.5 0.3 shard_map.151
  66.9 3.5 %all-to-all-done.1 = bf16[128,8,768]{2,1,0:T(8,128)(2,1)} async-done(((bf16[128,8,768]{2,1,0:T(8,128)(2,1)}), bf16[128,8,768]{2,1,0:T(8,128)(2,1)}, u32[]{:S(2)}, u32[]{:S(2)}) %all-to-all-start.1) | async-done | bytes 1572896 | tf_op jit(solution)/shard_map/all_to_all | solution.py:405
  70.3 43.1 %all_to_all.20.mail_ref = bf16[128,88,128]{2,1,0:T(8,128)(2,1)S(1)} all-to-all(bf16[128,88,128]{2,1,0:T(8,128)(2,1)S(1)} %shard_map.151), channel_id=1, replica_groups=mesh['px'=8,'py'=16] {'px','py'}, dimensions={0} | all-to-all | bytes 5767168 | tf_op jit(solution)/shard_map/all_to_all | solution.py:405
  113.5 1.2 shard_map.152
  114.6 0.0 copy-start
  114.6 23.7 %all_to_all.21.mine_ref = bf16[64,72,128]{2,1,0:T(8,128)(2,1)S(1)} all-to-all(bf16[64,72,128]{2,1,0:T(8,128)(2,1)S(1)} %get-tuple-element.39), channel_id=1, replica_groups={{0,1,2,3,4,5,6,7,8,9,10,11,12,13,14,15,32,33,34,35,36,37,38,39,40,41,42..., dimensions={0} | all-to-all | bytes 2359296 | tf_op jit(solution)/shard_map/all_to_all | solution.py:405
  138.4 2.5 %collective-permute-start.1 = (bf16[64,72,128]{2,1,0:T(8,128)(2,1)S(1)}, bf16[64,72,128]{2,1,0:T(8,128)(2,1)S(1)}, u32[]{:S(2)}, u32[]{:S(2)}) collective-permute-start(bf16[64,72,128]{2,1,0:T(8,128)(2,1)S(1)} %all_to_all.21.mine_ref), channel_id=1, source_target_pairs={{0,16},{16,0},{32,48},{48,32},{64,80},{80,64},{96,112},{112,96},{1... | collective-permute-start | bytes 3538952 | tf_op jit(solution)/shard_map/ppermute | solution.py:412
  140.9 0.0 copy-done
  140.9 3.8 %shard_map.153 = (f32[768,768]{1,0:T(8,128)}, f32[768,768]{1,0:T(8,128)}, bf16[1024,768]{1,0:T(8,128)(2,1)}) custom-call(s32[1]{0:T(128)} %bitcast.core_ref, bf16[64,72,128]{2,1,0:T(8,128)(2,1)S(1)} %all_to_all.21.mine_ref, bf16[1024,768]{1,0:T(8,128)(2,1)S(1)} %copy-done, bf16[1024,768]{1,0:T(8,128)(2,1)} %bitcast.10.grads_hbm), custom_call_target="tpu_custom_call" | custom-call | bytes 10616836 | tf_op jit(solution)/shard_map/pallas_call | solution.py:390
  144.7 0.0 collective-permute-done.1.other_ref
  144.7 1.6 %shard_map.154 = (f32[768,768]{1,0:T(8,128)}, f32[768,768]{1,0:T(8,128)}) custom-call(s32[1]{0:T(128)} %bitcast.core_ref, bf16[64,72,128]{2,1,0:T(8,128)(2,1)S(1)} %collective-permute-done.1.other_ref, f32[768,768]{1,0:T(8,128)} %get-tuple-element.42._, f32[768,768]{1,0:T(8,128)} %get-tuple-element.43.__), custom_call_target="tpu_custom_call", output_to_operand_aliasing={{0}: (2, {}), {1}: (3, {})} | custom-call | bytes 10616836 | tf_op jit(solution)/shard_map/pallas_call | solution.py:390
Async XLA Ops:
  4.8 35.7 %all-to-all-start = ((bf16[128,8,768]{2,1,0:T(8,128)(2,1)}), bf16[128,8,768]{2,1,0:T(8,128)(2,1)}, u32[]{:S(2)}, u32[]{:S(2)}) async-start(bf16[128,8,768]{2,1,0:T(8,128)(2,1)} %bitcast.14), calls=%async_computation | async-start | bytes 3145728 | tf_op jit(solution)/shard_map/all_to_all | solution.py:405
  40.6 29.8 %all-to-all-start.1 = ((bf16[128,8,768]{2,1,0:T(8,128)(2,1)}), bf16[128,8,768]{2,1,0:T(8,128)(2,1)}, u32[]{:S(2)}, u32[]{:S(2)}) async-start(bf16[128,8,768]{2,1,0:T(8,128)(2,1)} %get-tuple-element.36), calls=%async_computation.1 | async-start | bytes 3145728 | tf_op jit(solution)/shard_map/all_to_all | solution.py:405
  46.4 16.9 %copy-start.1 = (bf16[1024,768]{1,0:T(8,128)(2,1)S(1)}, bf16[1024,768]{1,0:T(8,128)(2,1)}, u32[]{:S(2)}) copy-start(bf16[1024,768]{1,0:T(8,128)(2,1)} %get-tuple-element.26.picks_hbm) | copy-start | bytes 4718596
  61.8 4.7 %collective-permute-start = (bf16[4608,128]{1,0:T(8,128)(2,1)}, bf16[4608,128]{1,0:T(8,128)(2,1)S(1)}, u32[]{:S(2)}, u32[]{:S(2)}) collective-permute-start(bf16[4608,128]{1,0:T(8,128)(2,1)} %get-tuple-element.34), channel_id=1, source_target_pairs={{0,16},{16,0},{32,48},{48,32},{64,80},{80,64},{96,112},{112,96},{1... | collective-permute-start | bytes 3538952 | tf_op jit(solution)/shard_map/ppermute | solution.py:412
  63.4 1.3 copy-start.3
  64.6 1.9 %copy-start.2 = (f32[4608,128]{1,0:T(8,128)S(1)}, f32[4608,128]{1,0:T(8,128)}, u32[]{:S(2)}) copy-start(f32[4608,128]{1,0:T(8,128)} %get-tuple-element.33.keep_ref) | copy-start | bytes 7077892
  114.6 26.3 %copy-start = (bf16[1024,768]{1,0:T(8,128)(2,1)S(1)}, bf16[1024,768]{1,0:T(8,128)(2,1)}, u32[]{:S(2)}) copy-start(bf16[1024,768]{1,0:T(8,128)(2,1)} %get-tuple-element.25.sent_hbm) | copy-start | bytes 4718596
  138.4 6.3 %collective-permute-start.1 = (bf16[64,72,128]{2,1,0:T(8,128)(2,1)S(1)}, bf16[64,72,128]{2,1,0:T(8,128)(2,1)S(1)}, u32[]{:S(2)}, u32[]{:S(2)}) collective-permute-start(bf16[64,72,128]{2,1,0:T(8,128)(2,1)S(1)} %all_to_all.21.mine_ref), channel_id=1, source_target_pairs={{0,16},{16,0},{32,48},{48,32},{64,80},{80,64},{96,112},{112,96},{1... | collective-permute-start | bytes 3538952 | tf_op jit(solution)/shard_map/ppermute | solution.py:412
